TPU v7x, 32 devices: a whole 2x2x4 slice. The times are simulated.
32 devices in a mesh: row: 8 (over z, y), col: 4 (over x, core).
Axes of the slice: x: 2, y: 2, z: 4, core: 2. Of those that a mesh axis runs over, the one named last changes fastest.
Arguments:
- inputs: float32 [16384, 768], P(('row', 'col')), may hold values from -25 to 25, as said below
- cotangent: float32 [16384, 768], P(('row', 'col')), may hold values from -6 to 6
- token_order: int32 [16384], P('row'), may hold values from 0 to 16383, as said below
- token_place: int32 [16384], P('row'), may hold values from 0 to 16383, as said below
- seq_lengths: int32 [8, 8], P('row'), may hold values from 1 to 512, 2048 in all within a row
- query_weight: bfloat16 [768, 768], P('row', 'col'), may hold values from -0.21875 to 0.21875
- key_weight: bfloat16 [768, 768], P('row', 'col'), may hold values from -0.21875 to 0.21875
- value_weight: bfloat16 [768, 768], P('row', 'col'), may hold values from -0.21875 to 0.21875
- output_weight: bfloat16 [768, 768], P('col', 'row'), may hold values from -0.875 to 0.875
- inner_weight: bfloat16 [768, 3072], P('row', 'col'), may hold values from -0.21875 to 0.21875
- outer_weight: bfloat16 [3072, 768], P('col', 'row'), may hold values from -0.109375 to 0.109375
- query_bias: bfloat16 [768], P(('col', 'row')), may hold values from -3 to 3
- value_bias: bfloat16 [768], P(('col', 'row')), may hold values from -3 to 3
- output_bias: bfloat16 [768], P(('col', 'row')), may hold values from -2 to 2
- inner_bias: bfloat16 [3072], P(('col', 'row')), may hold values from -3 to 3
- outer_bias: bfloat16 [768], P(('col', 'row')), may hold values from -2 to 2
- first_gain: bfloat16 [768], P(('col', 'row')), may hold values from 0.5 to 1.5
- first_shift: bfloat16 [768], P(('col', 'row')), may hold values from -2 to 2
- second_gain: bfloat16 [768], P(('col', 'row')), may hold values from 0.5 to 1.5
- second_shift: bfloat16 [768], P(('col', 'row')), may hold values from -2 to 2
Outputs:
- output: float32 [16384, 768], P(('row', 'col'))
- input_grad: float32 [16384, 768], P(('row', 'col'))
- query_weight_grad: float32 [768, 768], P('row', 'col')
- key_weight_grad: float32 [768, 768], P('row', 'col')
- value_weight_grad: float32 [768, 768], P('row', 'col')
- output_weight_grad: float32 [768, 768], P('col', 'row')
- inner_weight_grad: float32 [768, 3072], P('row', 'col')
- outer_weight_grad: float32 [3072, 768], P('col', 'row')
- query_bias_grad: float32 [768], P(('col', 'row'))
- value_bias_grad: float32 [768], P(('col', 'row'))
- output_bias_grad: float32 [768], P(('col', 'row'))
- inner_bias_grad: float32 [3072], P(('col', 'row'))
- outer_bias_grad: float32 [768], P(('col', 'row'))
- first_gain_grad: float32 [768], P(('col', 'row'))
- first_shift_grad: float32 [768], P(('col', 'row'))
- second_gain_grad: float32 [768], P(('col', 'row'))
- second_shift_grad: float32 [768], P(('col', 'row'))
Inputs may be any that keep to these rules, and one draw needn't show every extreme that they name: `inputs`: drawn from a normal or uniform law times independent row and feature scales. `token_order`: A permutation of all tokens. Every work block of 2048 rows takes exactly 256 tokens from each block of 2048 given rows. The inverse permutation of token_order: token_order[token_place[i]] = i. `seq_lengths`: each row sums to 2048; its sequences lie one after another in that work block.
All inputs are finite; a program needn't handle non-finite values.
Results may differ from a plain program's by a relative error of at most 0.013.
The roundings to bfloat16 on the way count: a program that leaves them out, or rounds other values in their place, can miss the bound.
Values may be sent and summed in bfloat16 or wider, within the bound.
A program may use at most 128 MiB of HBM per device.

v0:
```python
import jax
import jax.numpy as jnp
from jax import lax
from jax.sharding import PartitionSpec as P

D = 768
HD = 64
QBLOCK = 512


norm_eps = 1e-12
root_half = 0.7071067811865476
inv_root_two_pi = 0.3989422804014327
contract_last = (((1,), (1,)), ((), ()))
contract_first = (((0,), (0,)), ((), ()))


def split_up(value, dim, size):
    before, after = (value.shape[:dim], value.shape[dim + 1 :])
    return jnp.moveaxis(value.reshape(*before, size, -1, *after), dim, 0)


def sent_and_summed(value, axis, dim):
    size = lax.axis_size(axis)
    parts = lax.all_to_all(split_up(value, dim, size), axis, 0, 0, tiled=True)
    return jnp.sum(parts.astype(jnp.float32), axis=0)


def side_by_side(arrays, axis, dim, along):
    ends, at = ([], 0)
    for a in arrays[:-1]:
        at += a.shape[along]
        ends.append(at)
    both = jnp.concatenate(arrays, axis=along)
    return tuple(jnp.split(sent_and_summed(both, axis, dim), ends, axis=along))


def as_sent(value):

    def short(part):
        return part.astype(jnp.bfloat16) if part.dtype == jnp.float32 else part

    return jax.tree.map(short, value)


def gelu_parts(inner_pre):
    cumulative = 0.5 * (1.0 + jax.scipy.special.erf(inner_pre * root_half))
    density = jnp.exp(-0.5 * inner_pre * inner_pre) * inv_root_two_pi
    return (inner_pre * cumulative, cumulative + inner_pre * density)


def widen(piece_in):
    return lax.all_gather(piece_in, "col", axis=1, tiled=True)


def narrow(partial_value):
    return lax.psum_scatter(partial_value, "col", scatter_dimension=1, tiled=True)


def row_pair(first_sum, second_sum):
    return lax.psum((first_sum, second_sum), "col")


def layer_stats(resid_in):
    sum_one, sum_two = row_pair(jnp.sum(resid_in, axis=1), jnp.sum(resid_in * resid_in, axis=1))
    mean_val = sum_one[:, None] / D
    inv_std = lax.rsqrt(sum_two[:, None] / D - mean_val * mean_val + norm_eps)
    return ((resid_in - mean_val) * inv_std, inv_std)


def back_norm(grad_out, gain_vec, x_hat, inv_std):
    scaled = grad_out * gain_vec
    sum_grad, sum_cross = row_pair(jnp.sum(scaled, axis=1), jnp.sum(scaled * x_hat, axis=1))
    return inv_std * (scaled - sum_grad[:, None] / D - x_hat * (sum_cross[:, None] / D))


def attend_forward(queries, keys_all, values_all, seg_ids):
    tok_rows, head_cols = queries.shape
    local_heads = head_cols // HD
    block_count = tok_rows // QBLOCK
    key_heads = keys_all.reshape(tok_rows, local_heads, HD)
    value_heads = values_all.reshape(tok_rows, local_heads, HD)
    score_scale = HD ** (-0.5)

    def one_block(block_args):
        query_block, seg_block = block_args
        scores = (
            jnp.einsum("qhd,khd->hqk", query_block, key_heads, preferred_element_type=jnp.float32)
            * score_scale
        )
        allowed = seg_block[:, None] == seg_ids[None, :]
        scores = jnp.where(allowed[None], scores, -1e30)
        row_top = jnp.max(scores, axis=2, keepdims=True)
        weights = jnp.exp(scores - row_top)
        totals = jnp.sum(weights, axis=2, keepdims=True)
        prob_low = (weights / totals).astype(jnp.bfloat16)
        mixed_out = jnp.einsum(
            "hqk,khd->qhd", prob_low, value_heads, preferred_element_type=jnp.float32
        )
        return (mixed_out.reshape(QBLOCK, head_cols), (row_top + jnp.log(totals))[:, :, 0])

    mixed_all, log_totals = lax.map(
        one_block,
        (
            queries.reshape(block_count, QBLOCK, local_heads, HD),
            seg_ids.reshape(block_count, QBLOCK),
        ),
    )
    return (mixed_all.reshape(tok_rows, head_cols), log_totals)


def attend_backward(queries, keys_all, values_all, seg_ids, log_totals, grad_mixed):
    tok_rows, head_cols = queries.shape
    local_heads = head_cols // HD
    block_count = tok_rows // QBLOCK
    key_heads = keys_all.reshape(tok_rows, local_heads, HD)
    value_heads = values_all.reshape(tok_rows, local_heads, HD)
    score_scale = HD ** (-0.5)

    def one_block(running, block_args):
        grad_keys, grad_values = running
        query_block, seg_block, log_block, grad_block = block_args
        scores = (
            jnp.einsum("qhd,khd->hqk", query_block, key_heads, preferred_element_type=jnp.float32)
            * score_scale
        )
        allowed = seg_block[:, None] == seg_ids[None, :]
        prob_full = jnp.where(allowed[None], jnp.exp(scores - log_block[:, :, None]), 0.0)
        prob_low = prob_full.astype(jnp.bfloat16)
        grad_values = grad_values + jnp.einsum(
            "hqk,qhd->khd", prob_low, grad_block, preferred_element_type=jnp.float32
        )
        grad_probs = jnp.einsum(
            "qhd,khd->hqk", grad_block, value_heads, preferred_element_type=jnp.float32
        )
        inner_sum = jnp.sum(prob_full * grad_probs, axis=2, keepdims=True)
        grad_scores = (prob_full * (grad_probs - inner_sum)).astype(jnp.bfloat16)
        grad_query = (
            jnp.einsum("hqk,khd->qhd", grad_scores, key_heads, preferred_element_type=jnp.float32)
            * score_scale
        )
        grad_keys = (
            grad_keys
            + jnp.einsum(
                "hqk,qhd->khd", grad_scores, query_block, preferred_element_type=jnp.float32
            )
            * score_scale
        )
        return ((grad_keys, grad_values), grad_query.reshape(QBLOCK, head_cols))

    zeros_init = jnp.zeros((tok_rows, local_heads, HD), jnp.float32)
    block_inputs = (
        queries.reshape(block_count, QBLOCK, local_heads, HD),
        seg_ids.reshape(block_count, QBLOCK),
        log_totals,
        grad_mixed.reshape(block_count, QBLOCK, local_heads, HD),
    )
    (grad_keys, grad_values), grad_query = lax.scan(
        one_block, (zeros_init, zeros_init), block_inputs
    )
    return (
        grad_query.reshape(tok_rows, head_cols),
        grad_keys.reshape(tok_rows, head_cols),
        grad_values.reshape(tok_rows, head_cols),
    )


def per_device(
    inputs,
    cotangent,
    token_order,
    token_place,
    seq_lengths,
    query_weight,
    key_weight,
    value_weight,
    output_weight,
    inner_weight,
    outer_weight,
    query_bias,
    value_bias,
    output_bias,
    inner_bias,
    outer_bias,
    first_gain,
    first_shift,
    second_gain,
    second_shift,
):
    given_tokens, given_grads = (
        lax.all_to_all(inputs, "col", split_axis=1, concat_axis=0, tiled=True),
        lax.all_to_all(cotangent, "col", split_axis=1, concat_axis=0, tiled=True),
    )
    tok_rows = given_tokens.shape[0]
    dest_rows = token_place // tok_rows
    send_order = jnp.argsort(dest_rows, stable=True)
    arrive_order = jnp.argsort(token_order, stable=True)
    got_tokens, got_grads = (
        lax.all_to_all(given_tokens[send_order], "row", split_axis=0, concat_axis=0, tiled=True),
        lax.all_to_all(given_grads[send_order], "row", split_axis=0, concat_axis=0, tiled=True),
    )
    dealt_tokens = jnp.zeros_like(got_tokens).at[arrive_order].set(got_tokens)
    dealt_grads = jnp.zeros_like(got_grads).at[arrive_order].set(got_grads)
    seq_ends = jnp.cumsum(seq_lengths[0])
    positions = jnp.arange(tok_rows, dtype=jnp.int32)
    seg_ids = jnp.sum((positions[:, None] >= seq_ends[None, :]).astype(jnp.int32), axis=1)
    gathered = (
        lax.all_gather(query_weight, "row", axis=0, tiled=True),
        lax.all_gather(key_weight, "row", axis=0, tiled=True),
        lax.all_gather(value_weight, "row", axis=0, tiled=True),
        lax.all_gather(output_weight, "row", axis=1, tiled=True),
        lax.all_gather(inner_weight, "row", axis=0, tiled=True),
        lax.all_gather(outer_weight, "row", axis=1, tiled=True),
        lax.all_gather(query_bias, "row", axis=0, tiled=True),
        lax.all_gather(value_bias, "row", axis=0, tiled=True),
        lax.all_gather(output_bias, "row", axis=0, tiled=True),
        lax.all_gather(inner_bias, "row", axis=0, tiled=True),
        lax.all_gather(outer_bias, "row", axis=0, tiled=True),
        lax.all_gather(first_gain, "row", axis=0, tiled=True),
        lax.all_gather(first_shift, "row", axis=0, tiled=True),
        lax.all_gather(second_gain, "row", axis=0, tiled=True),
        lax.all_gather(second_shift, "row", axis=0, tiled=True),
    )
    w_query, w_key, w_value, w_output, w_inner, w_outer = gathered[:6]
    bias_query, bias_value, bias_inner = (
        gathered[6].astype(jnp.float32),
        gathered[7].astype(jnp.float32),
        gathered[9].astype(jnp.float32),
    )
    work_tokens, work_grads = (dealt_tokens, dealt_grads)
    bias_output, bias_outer, gain_first, shift_first, gain_second, shift_second = tuple(
        (gathered[pick].astype(jnp.float32) for pick in (8, 10, 11, 12, 13, 14))
    )
    tokens_low = work_tokens.astype(jnp.bfloat16)
    tokens_full = widen(tokens_low)
    queries = (
        jnp.dot(tokens_full, w_query, preferred_element_type=jnp.float32) + bias_query
    ).astype(jnp.bfloat16)
    keys_all = jnp.dot(tokens_full, w_key, preferred_element_type=jnp.float32).astype(jnp.bfloat16)
    values_all = (
        jnp.dot(tokens_full, w_value, preferred_element_type=jnp.float32) + bias_value
    ).astype(jnp.bfloat16)
    mixed_out, log_totals = attend_forward(queries, keys_all, values_all, seg_ids)
    mixed_low = mixed_out.astype(jnp.bfloat16)
    attn_part = jnp.dot(mixed_low, w_output, preferred_element_type=jnp.float32)
    hat_first, inv_first = layer_stats(narrow(attn_part) + work_tokens + bias_output)
    normed = hat_first * gain_first + shift_first
    normed_low_full = lax.all_gather(normed.astype(jnp.bfloat16), "col", axis=1, tiled=True)
    inner_pre = jnp.dot(normed_low_full, w_inner, preferred_element_type=jnp.float32) + bias_inner
    activated, gelu_slope = gelu_parts(inner_pre)
    hidden_low = activated.astype(jnp.bfloat16)
    outer_part = jnp.dot(hidden_low, w_outer, preferred_element_type=jnp.float32)
    hat_second, inv_second = layer_stats(narrow(outer_part) + normed + bias_outer)
    output_work = hat_second * gain_second + shift_second
    grad_two = back_norm(work_grads, gain_second, hat_second, inv_second)
    grad_gain_second = jnp.sum(work_grads * hat_second, axis=0)
    grad_shift_second = jnp.sum(work_grads, axis=0)
    grad_bias_outer = jnp.sum(grad_two, axis=0)
    grad_two_full = widen(grad_two.astype(jnp.bfloat16))
    grad_hidden = lax.dot_general(
        grad_two_full, w_outer, contract_last, preferred_element_type=jnp.float32
    )
    grad_w_outer = lax.dot_general(
        hidden_low, grad_two_full, contract_first, preferred_element_type=jnp.float32
    )
    grad_pre = grad_hidden * gelu_slope
    grad_bias_inner = jnp.sum(grad_pre, axis=0)
    grad_pre_low = grad_pre.astype(jnp.bfloat16)
    grad_w_inner = lax.dot_general(
        normed_low_full, grad_pre_low, contract_first, preferred_element_type=jnp.float32
    )
    grad_normed = (
        narrow(
            lax.dot_general(
                grad_pre_low, w_inner, contract_last, preferred_element_type=jnp.float32
            )
        )
        + grad_two
    )
    grad_one = back_norm(grad_normed, gain_first, hat_first, inv_first)
    grad_gain_first = jnp.sum(grad_normed * hat_first, axis=0)
    grad_shift_first = jnp.sum(grad_normed, axis=0)
    grad_bias_output = jnp.sum(grad_one, axis=0)
    grad_one_full = widen(grad_one.astype(jnp.bfloat16))
    grad_mixed = lax.dot_general(
        grad_one_full, w_output, contract_last, preferred_element_type=jnp.float32
    ).astype(jnp.bfloat16)
    grad_w_output = lax.dot_general(
        mixed_low, grad_one_full, contract_first, preferred_element_type=jnp.float32
    )
    grad_query, grad_key, grad_value = attend_backward(
        queries, keys_all, values_all, seg_ids, log_totals, grad_mixed
    )
    query_grad_low = grad_query.astype(jnp.bfloat16)
    key_grad_low = grad_key.astype(jnp.bfloat16)
    value_grad_low = grad_value.astype(jnp.bfloat16)
    grad_bias_query = jnp.sum(query_grad_low.astype(jnp.float32), axis=0)
    grad_bias_value = jnp.sum(value_grad_low.astype(jnp.float32), axis=0)
    grad_w_query = lax.dot_general(
        tokens_full, query_grad_low, contract_first, preferred_element_type=jnp.float32
    )
    grad_w_key = lax.dot_general(
        tokens_full, key_grad_low, contract_first, preferred_element_type=jnp.float32
    )
    grad_w_value = lax.dot_general(
        tokens_full, value_grad_low, contract_first, preferred_element_type=jnp.float32
    )
    back_part = lax.dot_general(
        query_grad_low, w_query, contract_last, preferred_element_type=jnp.float32
    )
    back_part = back_part + lax.dot_general(
        key_grad_low, w_key, contract_last, preferred_element_type=jnp.float32
    )
    back_part = back_part + lax.dot_general(
        value_grad_low, w_value, contract_last, preferred_element_type=jnp.float32
    )
    grad_tokens = narrow(back_part) + grad_one
    summed = (
        *side_by_side(
            (
                grad_w_query.astype(jnp.bfloat16),
                grad_w_key.astype(jnp.bfloat16),
                grad_w_value.astype(jnp.bfloat16),
            ),
            "row",
            0,
            1,
        ),
        sent_and_summed(grad_w_output.astype(jnp.bfloat16), "row", 1),
        sent_and_summed(grad_w_inner.astype(jnp.bfloat16), "row", 0),
        sent_and_summed(grad_w_outer.astype(jnp.bfloat16), "row", 1),
        sent_and_summed(grad_bias_query.astype(jnp.bfloat16), "row", 0),
        sent_and_summed(grad_bias_value.astype(jnp.bfloat16), "row", 0),
        sent_and_summed(grad_bias_output.astype(jnp.bfloat16), "row", 0),
        sent_and_summed(grad_bias_inner.astype(jnp.bfloat16), "row", 0),
        sent_and_summed(grad_bias_outer.astype(jnp.bfloat16), "row", 0),
        sent_and_summed(grad_gain_first.astype(jnp.bfloat16), "row", 0),
        sent_and_summed(grad_shift_first.astype(jnp.bfloat16), "row", 0),
        sent_and_summed(grad_gain_second.astype(jnp.bfloat16), "row", 0),
        sent_and_summed(grad_shift_second.astype(jnp.bfloat16), "row", 0),
    )
    share_out, share_back = (output_work, grad_tokens)
    back_tokens, back_grads = (
        lax.all_to_all(
            share_out[arrive_order].astype(jnp.bfloat16),
            "row",
            split_axis=0,
            concat_axis=0,
            tiled=True,
        ).astype(jnp.float32),
        lax.all_to_all(
            share_back[arrive_order].astype(jnp.bfloat16),
            "row",
            split_axis=0,
            concat_axis=0,
            tiled=True,
        ).astype(jnp.float32),
    )
    given_out = jnp.zeros_like(back_tokens).at[send_order].set(back_tokens)
    given_back = jnp.zeros_like(back_grads).at[send_order].set(back_grads)
    output, input_grad = (
        lax.all_to_all(as_sent(given_out), "col", split_axis=0, concat_axis=1, tiled=True).astype(
            given_out.dtype
        ),
        lax.all_to_all(as_sent(given_back), "col", split_axis=0, concat_axis=1, tiled=True).astype(
            given_back.dtype
        ),
    )
    return (
        output,
        input_grad,
        summed[0],
        summed[1],
        summed[2],
        summed[3],
        summed[4],
        summed[5],
        summed[6],
        summed[7],
        summed[8],
        summed[9],
        summed[10],
        summed[11],
        summed[12],
        summed[13],
        summed[14],
    )


def solution(mesh):
    in_specs = (
        P(("row", "col"), None),
        P(("row", "col"), None),
        P("row"),
        P("row"),
        P("row", None),
        P("row", "col"),
        P("row", "col"),
        P("row", "col"),
        P("col", "row"),
        P("row", "col"),
        P("col", "row"),
        P(("col", "row")),
        P(("col", "row")),
        P(("col", "row")),
        P(("col", "row")),
        P(("col", "row")),
        P(("col", "row")),
        P(("col", "row")),
        P(("col", "row")),
        P(("col", "row")),
    )
    out_specs = (
        P(("row", "col"), None),
        P(("row", "col"), None),
        P("row", "col"),
        P("row", "col"),
        P("row", "col"),
        P("col", "row"),
        P("row", "col"),
        P("col", "row"),
        P(("col", "row")),
        P(("col", "row")),
        P(("col", "row")),
        P(("col", "row")),
        P(("col", "row")),
        P(("col", "row")),
        P(("col", "row")),
        P(("col", "row")),
        P(("col", "row")),
    )
    return jax.shard_map(
        per_device, mesh=mesh, in_specs=in_specs, out_specs=out_specs, check_vma=False
    )
```

profile of v0, /device:TPU:0, one launch (start us, length us, event | category | flops | bytes accessed | tf_op | source)
XLA Modules:
  0.0 1226.1 jit_solution(2952440549609494633)
XLA Ops:
  21.1 14.4 %all-to-all-done = f32[512,4,192]{0,2,1:T(8,128)S(1)} async-done(((f32[512,4,192]{0,2,1:T(8,128)}), f32[512,4,192]{0,2,1:T(8,128)S(1)}, u32[]{:S(2)}, u32[]{:S(2)}) %all-to-all-start) | async-done | bytes 1572896 | tf_op jit(solution)/shard_map/all_to_all | solution.py:191
  38.4 8.6 gather_fusion
  62.2 31.1 %all-to-all-done.1 = f32[8,256,192]{1,2,0:T(8,128)S(1)} async-done(((f32[8,256,192]{1,2,0:T(8,128)}), f32[8,256,192]{1,2,0:T(8,128)S(1)}, u32[]{:S(2)}, u32[]{:S(2)}) %all-to-all-start.1) | async-done | bytes 1572896 | tf_op jit(solution)/shard_map/all_to_all | solution.py:199
  95.1 10.8 scatter_custom_fusion
  113.4 20.3 %all-reduce.13 = (bf16[192]{0:T(256)(128)(2,1)S(1)}, bf16[192]{0:T(256)(128)(2,1)S(1)}, bf16[192]{0:T(256)(128)(2,1)S(1)}, bf16[192]{0:T(256)(128)(2,1)S(1)}, bf...) all-reduce(bf16[192]{0:T(256)(128)(2,1)S(1)} %dynamic-update-slice,, ...), channel_id=1, replica_groups=mesh['row'=8,'col'=4] {'row'}, use_global_device_ids=true, to_apply=%add | all-reduce | flops 2304 | bytes 9216
  133.9 31.4 %all_gather.63 = bf16[192,768]{0,1:T(8,128)(2,1)S(1)} all-gather(bf16[192,96]{0,1:T(8,128)(2,1)S(1)} %copy.197), channel_id=1, replica_groups=mesh['row'=8,'col'=4] {'row'}, dimensions={1}, use_global_device_ids=true | all-gather | bytes 331776 | tf_op jit(solution)/shard_map/all_gather | solution.py:211
  165.4 31.0 %all_gather.58 = bf16[768,192]{1,0:T(8,128)(2,1)S(1)} all-gather(bf16[96,192]{1,0:T(8,128)(2,1)S(1)} %copy-done.44), channel_id=1, replica_groups=mesh['row'=8,'col'=4] {'row'}, dimensions={0}, use_global_device_ids=true | all-gather | bytes 331776 | tf_op jit(solution)/shard_map/all_gather | solution.py:208
  196.3 31.3 %all_gather.60 = bf16[768,192]{1,0:T(8,128)(2,1)S(1)} all-gather(bf16[96,192]{1,0:T(8,128)(2,1)S(1)} %copy-done.45), channel_id=1, replica_groups=mesh['row'=8,'col'=4] {'row'}, dimensions={0}, use_global_device_ids=true | all-gather | bytes 331776 | tf_op jit(solution)/shard_map/all_gather | solution.py:209
  227.6 33.3 %all_gather.61 = bf16[768,192]{1,0:T(8,128)(2,1)} all-gather(bf16[96,192]{1,0:T(8,128)(2,1)S(1)} %copy-done.46), channel_id=1, replica_groups=mesh['row'=8,'col'=4] {'row'}, dimensions={0}, use_global_device_ids=true | all-gather | bytes 331776 | tf_op jit(solution)/shard_map/all_gather | solution.py:210
  269.2 83.1 %while.27 = (s32[]{:T(128)}, bf16[4,512,192]{1,2,0:T(8,128)(2,1)}, f32[4,3,512]{2,1,0:T(4,128)S(1)}, s32[4,512]{1,0:T(4,128)S(1)}, s32[2048]{0:T(1024)S(1)}, /*i...) while((s32[]{:T(128)}, bf16[4,512,192]{1,2,0:T(8,128)(2,1)}, ...), condition=%wide.region_8.9_spmd, body=%wide.region_5.8_spmd.sunk | while | flops 844102144 | bytes 44372084 | solution.py:102
  359.3 54.3 %reduce-scatter.5.cloned.1.call-done = f32[2048,192]{0,1:T(8,128)} async-done(((f32[2048,768]{0,1:T(8,128)}), f32[2048,192]{0,1:T(8,128)}) %reduce-scatter.5.cloned.1.call-update) | async-done | bytes 1572880 | tf_op jit(solution)/shard_map/reduce_scatter | solution.py:57
  415.9 10.3 all-reduce.12
  428.0 12.4 %reduce-scatter.7.cloned.1.call-start = ((), (), s32[]{:S(2)}) async-start(), calls=%async_computation.30 | async-start | bytes 7864320 | tf_op jit(solution)/shard_map/reduce_scatter | solution.py:57
  440.5 16.5 %all-gather.9.cloned.1.call-done = bf16[2048,768]{0,1:T(8,128)(2,1)} async-done(((bf16[2048,192]{0,1:T(8,128)(2,1)}), bf16[2048,768]{0,1:T(8,128)(2,1)}) %all-gather.9.cloned.1.call-update) | async-done | bytes 3145744 | tf_op jit(solution)/shard_map/all_gather | solution.py:248
  464.3 36.5 %all-gather.13.cloned.1.call-done = bf16[768,768]{0,1:T(8,128)(2,1)} async-done(((bf16[768,96]{0,1:T(8,128)(2,1)}), bf16[768,768]{0,1:T(8,128)(2,1)}) %all-gather.13.cloned.1.call-update) | async-done | bytes 1179664 | tf_op jit(solution)/shard_map/all_gather | solution.py:213
  510.1 26.9 %all_to_all.182 = f32[512,4,192]{0,2,1:T(8,128)} all-to-all(f32[512,4,192]{0,2,1:T(8,128)S(1)} %bitcast.192), channel_id=1, replica_groups=mesh['row'=8,'col'=4] {'col'}, dimensions={1} | all-to-all | bytes 3145728 | tf_op jit(solution)/shard_map/all_to_all | solution.py:192
  538.9 8.6 gather_fusion.2
  554.1 36.3 %all-to-all-done.5 = f32[8,256,192]{1,2,0:T(8,128)S(1)} async-done(((f32[8,256,192]{1,2,0:T(8,128)}), f32[8,256,192]{1,2,0:T(8,128)S(1)}, u32[]{:S(2)}, u32[]{:S(2)}) %all-to-all-start.5) | async-done | bytes 1572896 | tf_op jit(solution)/shard_map/all_to_all | solution.py:200
  592.2 10.9 scatter_custom_fusion.2
  609.2 10.2 all-reduce.11
  622.5 10.1 all-reduce.10
  637.8 27.8 %all-gather.15.cloned.1.call-done = bf16[2048,768]{0,1:T(8,128)(2,1)} async-done(((bf16[2048,192]{0,1:T(8,128)(2,1)}), bf16[2048,768]{0,1:T(8,128)(2,1)}) %all-gather.15.cloned.1.call-update) | async-done | bytes 3145744 | tf_op jit(solution)/shard_map/all_gather | solution.py:53
  680.1 58.3 %reduce-scatter.9.cloned.1.call-done = f32[2048,192]{0,1:T(8,128)} async-done(((f32[2048,768]{0,1:T(8,128)}), f32[2048,192]{0,1:T(8,128)}) %reduce-scatter.9.cloned.1.call-update) | async-done | bytes 1572880 | tf_op jit(solution)/shard_map/reduce_scatter | solution.py:57
  742.7 10.1 all-reduce.9
  757.5 29.3 %all-gather.17.cloned.1.call-done = bf16[2048,768]{0,1:T(8,128)(2,1)} async-done(((bf16[2048,192]{0,1:T(8,128)(2,1)}), bf16[2048,768]{0,1:T(8,128)(2,1)}) %all-gather.17.cloned.1.call-update) | async-done | bytes 3145744 | tf_op jit(solution)/shard_map/all_gather | solution.py:53
  791.2 122.8 %while.28 = (s32[]{:T(128)}, f32[2048,3,64]{0,2,1:T(8,128)}, f32[2048,3,64]{0,2,1:T(8,128)}, bf16[4,512,192]{1,2,0:T(8,128)(2,1)}, bf16[4,512,3,64]{1,3,2,0:T(8,...) while((s32[]{:T(128)}, f32[2048,3,64]{0,2,1:T(8,128)}, ...), condition=%wide.region_32.33_spmd.clone, body=%wide.region_30.32_spmd.clone.sunk | while | flops 2063661568 | bytes 150595920 | solution.py:158
  959.9 18.2 %all-to-all-done.2 = bf16[8,256,192]{1,2,0:T(8,128)(2,1)S(1)} async-done(((bf16[8,256,192]{1,2,0:T(8,128)(2,1)}), bf16[8,256,192]{1,2,0:T(8,128)(2,1)S(1)}, u32[]{:S(2)}, u32[]{:S(2)}) %all-to-all-start.2) | async-done | bytes 786464 | tf_op jit(solution)/shard_map/all_to_all | solution.py:344
  983.4 10.0 scatter_custom_fusion.1
  1000.8 10.9 all-to-all-done.3
  1036.9 21.5 %all-to-all-done.11 = bf16[8,768,96]{1,2,0:T(8,128)(2,1)S(1)} async-done(((bf16[8,768,96]{1,2,0:T(8,128)(2,1)}), bf16[8,768,96]{1,2,0:T(8,128)(2,1)S(1)}, u32[]{:S(2)}, u32[]{:S(2)}) %all-to-all-start.11) | async-done | bytes 1179680 | tf_op jit(solution)/shard_map/all_to_all | solution.py:25
  1063.4 27.5 %all-to-all-done.10 = bf16[8,96,768]{2,1,0:T(8,128)(2,1)} async-done(((bf16[8,96,768]{2,1,0:T(8,128)(2,1)}), bf16[8,96,768]{2,1,0:T(8,128)(2,1)}, u32[]{:S(2)}, u32[]{:S(2)}) %all-to-all-start.10) | async-done | bytes 1179680 | tf_op jit(solution)/shard_map/all_to_all | solution.py:25
  1190.2 10.0 scatter_custom_fusion.3
  (478 shorter events, 537.9 us)
Async XLA Ops:
  11.0 24.4 %all-to-all-start = ((f32[512,4,192]{0,2,1:T(8,128)}), f32[512,4,192]{0,2,1:T(8,128)S(1)}, u32[]{:S(2)}, u32[]{:S(2)}) async-start(f32[512,4,192]{0,2,1:T(8,128)} %bitcast.7), calls=%async_computation | async-start | bytes 3145728 | tf_op jit(solution)/shard_map/all_to_all | solution.py:191
  49.8 43.5 %all-to-all-start.1 = ((f32[8,256,192]{1,2,0:T(8,128)}), f32[8,256,192]{1,2,0:T(8,128)S(1)}, u32[]{:S(2)}, u32[]{:S(2)}) async-start(f32[8,256,192]{1,2,0:T(8,128)} %copy.191), calls=%async_computation.1 | async-start | bytes 3145728 | tf_op jit(solution)/shard_map/all_to_all | solution.py:199
  56.5 204.4 %all-gather.7.cloned.1.call-start = ((), (), s32[]{:S(2)}) async-start(), calls=%async_computation.25 | async-start | bytes 3932160 | tf_op jit(solution)/shard_map/all_gather | solution.py:53
  108.0 119.6 %copy-start.46 = (bf16[96,192]{1,0:T(8,128)(2,1)S(1)}, bf16[96,192]{1,0:T(8,128)(2,1)}, u32[]{:S(2)}) copy-start(bf16[96,192]{1,0:T(8,128)(2,1)} %param.31) | copy-start | bytes 110596
  109.1 304.5 %reduce-scatter.5.cloned.1.call-start = ((), (), s32[]{:S(2)}) async-start(), calls=%async_computation.26 | async-start | bytes 7864320 | tf_op jit(solution)/shard_map/reduce_scatter | solution.py:57
  358.6 81.8 %all-gather.11.cloned.1.call-start = ((), (), s32[]{:S(2)}) async-start(), calls=%async_computation.28 | async-start | bytes 1327104 | tf_op jit(solution)/shard_map/all_gather | solution.py:212
  359.2 97.7 %all-gather.9.cloned.1.call-start = ((), (), s32[]{:S(2)}) async-start(), calls=%async_computation.27 | async-start | bytes 3932160 | tf_op jit(solution)/shard_map/all_gather | solution.py:248
  427.4 73.3 %all-gather.13.cloned.1.call-start = ((), (), s32[]{:S(2)}) async-start(), calls=%async_computation.29 | async-start | bytes 1327104 | tf_op jit(solution)/shard_map/all_gather | solution.py:213
  428.0 178.0 %reduce-scatter.7.cloned.1.call-start = ((), (), s32[]{:S(2)}) async-start(), calls=%async_computation.30 | async-start | bytes 7864320 | tf_op jit(solution)/shard_map/reduce_scatter | solution.py:57
  550.3 40.2 %all-to-all-start.5 = ((f32[8,256,192]{1,2,0:T(8,128)}), f32[8,256,192]{1,2,0:T(8,128)S(1)}, u32[]{:S(2)}, u32[]{:S(2)}) async-start(f32[8,256,192]{1,2,0:T(8,128)} %copy.206), calls=%async_computation.7 | async-start | bytes 3145728 | tf_op jit(solution)/shard_map/all_to_all | solution.py:200
  554.0 111.6 %all-gather.15.cloned.1.call-start = ((), (), s32[]{:S(2)}) async-start(), calls=%async_computation.31 | async-start | bytes 3932160 | tf_op jit(solution)/shard_map/all_gather | solution.py:53
  637.8 100.7 %reduce-scatter.9.cloned.1.call-start = ((), (), s32[]{:S(2)}) async-start(), calls=%async_computation.32 | async-start | bytes 7864320 | tf_op jit(solution)/shard_map/reduce_scatter | solution.py:57
  680.1 106.7 %all-gather.17.cloned.1.call-start = ((), (), s32[]{:S(2)}) async-start(), calls=%async_computation.33 | async-start | bytes 3932160 | tf_op jit(solution)/shard_map/all_gather | solution.py:53
  757.4 385.9 %reduce-scatter.11.cloned.1.call-start = ((), (), s32[]{:S(2)}) async-start(), calls=%async_computation.34 | async-start | bytes 7864320 | tf_op jit(solution)/shard_map/reduce_scatter | solution.py:57
  926.6 11.9 all-to-all-start.20
  938.5 14.8 %all-to-all-start.19 = ((bf16[8,1,24]{2,1,0:T(2,128)(2,1)}), bf16[8,1,24]{2,1,0:T(2,128)(2,1)S(1)}, u32[]{:S(2)}, u32[]{:S(2)}) async-start(bf16[8,1,24]{2,1,0:T(2,128)(2,1)} %convert_element_type.403), calls=%async_computation.23 | async-start | bytes 8192 | tf_op jit(solution)/shard_map/all_to_all | solution.py:25
  953.3 24.8 %all-to-all-start.2 = ((bf16[8,256,192]{1,2,0:T(8,128)(2,1)}), bf16[8,256,192]{1,2,0:T(8,128)(2,1)S(1)}, u32[]{:S(2)}, u32[]{:S(2)}) async-start(bf16[8,256,192]{1,2,0:T(8,128)(2,1)} %copy.200), calls=%async_computation.4 | async-start | bytes 1572864 | tf_op jit(solution)/shard_map/all_to_all | solution.py:344
  978.2 18.5 %all-to-all-start.16 = ((bf16[8,1,24]{2,1,0:T(2,128)(2,1)}), bf16[8,1,24]{2,1,0:T(2,128)(2,1)S(1)}, u32[]{:S(2)}, u32[]{:S(2)}) async-start(bf16[8,1,24]{2,1,0:T(2,128)(2,1)} %convert_element_type.400), calls=%async_computation.20 | async-start | bytes 8192 | tf_op jit(solution)/shard_map/all_to_all | solution.py:25
  996.6 15.1 %all-to-all-start.3 = ((bf16[4,512,192]{1,2,0:T(8,128)(2,1)}), bf16[4,512,192]{1,2,0:T(8,128)(2,1)S(1)}, u32[]{:S(2)}, u32[]{:S(2)}) async-start(bf16[4,512,192]{1,2,0:T(8,128)(2,1)} %copy.203), calls=%async_computation.5 | async-start | bytes 1572864 | tf_op jit(solution)/shard_map/all_to_all | solution.py:362
  1011.8 12.5 %all-to-all-start.15 = ((bf16[8,1,96]{2,1,0:T(2,128)(2,1)}), bf16[8,1,96]{2,1,0:T(2,128)(2,1)S(1)}, u32[]{:S(2)}, u32[]{:S(2)}) async-start(bf16[8,1,96]{2,1,0:T(2,128)(2,1)} %convert_element_type.399), calls=%async_computation.19 | async-start | bytes 8192 | tf_op jit(solution)/shard_map/all_to_all | solution.py:25
  1024.2 34.2 %all-to-all-start.11 = ((bf16[8,768,96]{1,2,0:T(8,128)(2,1)}), bf16[8,768,96]{1,2,0:T(8,128)(2,1)S(1)}, u32[]{:S(2)}, u32[]{:S(2)}) async-start(bf16[8,768,96]{1,2,0:T(8,128)(2,1)} %bitcast.209), calls=%async_computation.15 | async-start | bytes 2359296 | tf_op jit(solution)/shard_map/all_to_all | solution.py:25
  1036.9 96.0 %copy-start.14 = (bf16[4,24,8,512]{3,2,0,1:T(8,128)(2,1)S(1)}, bf16[4,24,8,512]{3,2,0,1:T(8,128)(2,1)}, u32[]{:S(2)}) copy-start(bf16[4,24,8,512]{3,2,0,1:T(8,128)(2,1)} %copy-done.13) | copy-start | bytes 2359300
  1058.5 32.5 %all-to-all-start.10 = ((bf16[8,96,768]{2,1,0:T(8,128)(2,1)}), bf16[8,96,768]{2,1,0:T(8,128)(2,1)}, u32[]{:S(2)}, u32[]{:S(2)}) async-start(bf16[8,96,768]{2,1,0:T(8,128)(2,1)} %bitcast.210), calls=%async_computation.14 | async-start | bytes 2359296 | tf_op jit(solution)/shard_map/all_to_all | solution.py:25
  1090.9 9.8 all-to-all-start.18
  1100.7 9.6 all-to-all-start.17
  1110.3 9.6 all-to-all-start.14
  1120.0 9.6 all-to-all-start.12
  1129.6 9.7 all-to-all-start.13
  1139.3 14.9 %all-to-all-start.9 = ((bf16[8,192,96]{2,1,0:T(8,128)(2,1)}), bf16[8,192,96]{2,1,0:T(8,128)(2,1)S(1)}, u32[]{:S(2)}, u32[]{:S(2)}) async-start(bf16[8,192,96]{2,1,0:T(8,128)(2,1)} %bitcast.133), calls=%async_computation.13 | async-start | bytes 786432 | tf_op jit(solution)/shard_map/all_to_all | solution.py:25
  1154.2 20.7 %all-to-all-start.6 = ((bf16[8,256,192]{1,2,0:T(8,128)(2,1)}), bf16[8,256,192]{1,2,0:T(8,128)(2,1)S(1)}, u32[]{:S(2)}, u32[]{:S(2)}) async-start(bf16[8,256,192]{1,2,0:T(8,128)(2,1)} %copy.214), calls=%async_computation.10 | async-start | bytes 1572864 | tf_op jit(solution)/shard_map/all_to_all | solution.py:351
  1174.9 26.6 %all-to-all-start.8 = ((bf16[8,96,576]{2,1,0:T(8,128)(2,1)}), bf16[8,96,576]{2,1,0:T(8,128)(2,1)}, u32[]{:S(2)}, u32[]{:S(2)}) async-start(bf16[8,96,576]{2,1,0:T(8,128)(2,1)} %bitcast.33), calls=%async_computation.12 | async-start | bytes 1966080 | tf_op jit(solution)/shard_map/all_to_all | solution.py:25
  1201.5 15.1 %all-to-all-start.7 = ((bf16[4,512,192]{1,2,0:T(8,128)(2,1)}), bf16[4,512,192]{1,2,0:T(8,128)(2,1)S(1)}, u32[]{:S(2)}, u32[]{:S(2)}) async-start(bf16[4,512,192]{1,2,0:T(8,128)(2,1)} %copy.217), calls=%async_computation.11 | async-start | bytes 1572864 | tf_op jit(solution)/shard_map/all_to_all | solution.py:365
  (104 other events, 1318.4 us)
Sparse Core Ops, SparseCore 0:
  109.2 26.7 all-gather.6
  358.7 54.7 reduce-scatter.4
  637.9 27.6 all-gather.14
  757.6 29.1 all-gather.16
  924.0 58.3 reduce-scatter.10
Sparse Core Ops, SparseCore 1:
  361.3 37.9 all-gather.10
  427.5 29.4 all-gather.8
  459.2 41.5 all-gather.12
  508.3 60.2 reduce-scatter.6
  680.2 58.2 reduce-scatter.8
where the time goes:
time: 1240 us; the launch traced here: 1230 us
  waiting for transfers between devices  430 us (35%)
  blocking collectives  215 us (17%)
  matrix products  210 us (17%)
  local copies, waits for them, and re-layouts  141 us (11%)
  other arithmetic  111 us (9%)
  starting transfers between devices  100 us (8%)
  between operations  18.3 us (1%)
    reduce_scatter x4, waiting for transfers between devices, narrow(): lax.psum_scatter(partial_value, 'col', scatter_dimension=1, tiled=True)  113 us
    all_to_all x13, waiting for transfers between devices, sent_and_summed(): parts = lax.all_to_all(split_up(value, dim, size), axis, 0, 0, tiled=True)  79.1 us
    all_gather x3, waiting for transfers between devices, widen(): return lax.all_gather(piece_in, 'col', axis=1, tiled=True)  57 us
    all_to_all x13, starting transfers between devices, sent_and_summed(): parts = lax.all_to_all(split_up(value, dim, size), axis, 0, 0, tiled=True)  54 us
    psum x4, blocking collectives, row_pair(): return lax.psum((first_sum, second_sum), 'col')  40.7 us
    all_gather x1, waiting for transfers between devices, per_device(): lax.all_gather(outer_weight, 'row', axis=1, tiled=True)  36.5 us
    all_to_all x1, waiting for transfers between devices, per_device(): lax.all_to_all(given_grads[send_order], 'row', split_axis=0, concat_axis=...  36.3 us
    dot_general x8, matrix products, one_block(): jnp.einsum('qhd,khd->hqk', query_block, key_heads, preferred_element_type...  35.8 us
  transfers between devices with their start and end apart: 30, of which 21 were waited for; matrix products, arithmetic and copies ran while one was open for 12% of the time, Pallas kernels for 0%

commit v1 on v0

v1 whole, which is shorter than its diff:
```python
import functools

import jax
import jax.numpy as jnp
from jax import lax
from jax.experimental import pallas as pl
from jax.experimental.pallas import tpu as pltpu
from jax.sharding import PartitionSpec as P

D = 768
HD = 64
FEAT = 192
HEADS = 3
QB = 256
KB = 256

norm_eps = 1e-12
root_half = 0.7071067811865476
inv_root_two_pi = 0.3989422804014327
NN = (((1,), (0,)), ((), ()))
NT = (((1,), (1,)), ((), ()))
TN = (((0,), (0,)), ((), ()))
MESH = pl.DeviceIdType.MESH
f32 = jnp.float32
bf16 = jnp.bfloat16
VM = pl.BlockSpec(memory_space=pltpu.VMEM)
SM = pl.BlockSpec(memory_space=pltpu.SMEM)


def mm(a, b, dims):
    return lax.dot_general(a, b, dims, preferred_element_type=f32)


def lane_head(rows):
    return lax.broadcasted_iota(jnp.int32, (rows, FEAT), 1) // HD


def attend_fwd_body(lo_ref, hi_ref, start_ref, end_ref, q_ref, k_ref, v_ref, mix_ref, lse_ref, s_buf):
    scale = HD ** (-0.5)
    blocks = q_ref.shape[0] // QB
    heads = lane_head(QB)

    @pl.loop(0, blocks)
    def _(qb):
        rows = pl.ds(qb * QB, QB)
        qv = q_ref[rows, :]
        qs = [jnp.where(heads == h, qv, jnp.zeros_like(qv)) for h in range(HEADS)]
        q_start = start_ref[:, rows]
        q_end = end_ref[:, rows]
        lo, hi = lo_ref[qb], hi_ref[qb]

        def scores(kb, tops):
            keys = pl.ds(pl.multiple_of(kb * KB, KB), KB)
            kv = k_ref[keys, :]
            pos = lax.broadcasted_iota(jnp.int32, (KB, QB), 0) + kb * KB
            allowed = (pos >= q_start) & (pos < q_end)
            out = []
            for h in range(HEADS):
                s = jnp.where(allowed, mm(kv, qs[h], NT) * scale, -1e30)
                s_buf[h, keys, :] = s
                out.append(jnp.maximum(tops[h], jnp.max(s, axis=0, keepdims=True)))
            return tuple(out)

        tops = lax.fori_loop(lo, hi, scores, tuple(jnp.full((1, QB), -1e30, f32) for _ in range(HEADS)))

        def weigh(kb, sums):
            keys = pl.ds(pl.multiple_of(kb * KB, KB), KB)
            out = []
            for h in range(HEADS):
                e = jnp.exp(s_buf[h, keys, :] - tops[h])
                s_buf[h, keys, :] = e
                out.append(sums[h] + jnp.sum(e, axis=0, keepdims=True))
            return tuple(out)

        sums = lax.fori_loop(lo, hi, weigh, tuple(jnp.zeros((1, QB), f32) for _ in range(HEADS)))
        inv = [1.0 / s for s in sums]

        def mix(kb, acc):
            keys = pl.ds(pl.multiple_of(kb * KB, KB), KB)
            vv = v_ref[keys, :]
            for h in range(HEADS):
                p = (s_buf[h, keys, :] * inv[h]).astype(bf16)
                acc = acc + jnp.where(heads == h, mm(p, vv, TN), 0.0)
            return acc

        acc = lax.fori_loop(lo, hi, mix, jnp.zeros((QB, FEAT), f32))
        mix_ref[rows, :] = acc.astype(bf16)
        for h in range(HEADS):
            lse_ref[pl.ds(h, 1), rows] = tops[h] + jnp.log(sums[h])


def attend_fwd(lo, hi, start, end, q, k, v):
    rows = q.shape[0]
    return pl.pallas_call(
        attend_fwd_body,
        out_shape=(
            jax.ShapeDtypeStruct((rows, FEAT), bf16),
            jax.ShapeDtypeStruct((8, rows), f32),
        ),
        in_specs=[SM, SM, VM, VM, VM, VM, VM],
        out_specs=(VM, VM),
        scratch_shapes=[pltpu.VMEM((HEADS, rows, QB), f32)],
        name="attend_fwd",
        compiler_params=pltpu.CompilerParams(vmem_limit_bytes=40 << 20),
        cost_estimate=pl.CostEstimate(flops=8_000_000_000, bytes_accessed=4_000_000, transcendentals=4_000_000),
    )(lo, hi, start, end, q, k, v)


def attend_bwd_body(
    lo_ref, hi_ref, start_ref, end_ref, q_ref, k_ref, v_ref, do_ref, lse_ref,
    dq_ref, dk_ref, dv_ref, p_buf, dp_buf, dk_acc, dv_acc,
):
    scale = HD ** (-0.5)
    blocks = q_ref.shape[0] // QB
    heads = lane_head(QB)
    key_heads = lane_head(KB)
    dk_acc[...] = jnp.zeros_like(dk_acc)
    dv_acc[...] = jnp.zeros_like(dv_acc)

    @pl.loop(0, blocks)
    def _(qb):
        rows = pl.ds(qb * QB, QB)
        qv = q_ref[rows, :]
        dv_in = do_ref[rows, :]
        qs = [jnp.where(heads == h, qv, jnp.zeros_like(qv)) for h in range(HEADS)]
        dos = [jnp.where(heads == h, dv_in, jnp.zeros_like(dv_in)) for h in range(HEADS)]
        q_start = start_ref[:, rows]
        q_end = end_ref[:, rows]
        lse = [lse_ref[pl.ds(h, 1), rows] for h in range(HEADS)]
        lo, hi = lo_ref[qb], hi_ref[qb]

        def first(kb, sums):
            keys = pl.ds(pl.multiple_of(kb * KB, KB), KB)
            kv, vv = k_ref[keys, :], v_ref[keys, :]
            pos = lax.broadcasted_iota(jnp.int32, (KB, QB), 0) + kb * KB
            allowed = (pos >= q_start) & (pos < q_end)
            out = []
            grad_v = dv_acc[keys, :]
            for h in range(HEADS):
                p = jnp.where(allowed, jnp.exp(mm(kv, qs[h], NT) * scale - lse[h]), 0.0)
                dp = mm(vv, dos[h], NT)
                p_buf[h, keys, :] = p
                dp_buf[h, keys, :] = dp
                out.append(sums[h] + jnp.sum(p * dp, axis=0, keepdims=True))
                grad_v = grad_v + mm(p.astype(bf16), dos[h], NN)
            dv_acc[keys, :] = grad_v
            return tuple(out)

        sums = lax.fori_loop(lo, hi, first, tuple(jnp.zeros((1, QB), f32) for _ in range(HEADS)))

        def second(kb, acc):
            keys = pl.ds(pl.multiple_of(kb * KB, KB), KB)
            kv = k_ref[keys, :]
            grad_k = dk_acc[keys, :]
            for h in range(HEADS):
                ds = (p_buf[h, keys, :] * (dp_buf[h, keys, :] - sums[h])).astype(bf16)
                grad_k = grad_k + mm(ds, qs[h], NN)
                acc = acc + jnp.where(heads == h, mm(ds, kv, TN), 0.0)
            dk_acc[keys, :] = grad_k
            return acc

        acc = lax.fori_loop(lo, hi, second, jnp.zeros((QB, FEAT), f32))
        dq_ref[rows, :] = (acc * scale).astype(bf16)

    dk_ref[...] = (dk_acc[...] * scale).astype(bf16)
    dv_ref[...] = dv_acc[...].astype(bf16)


def attend_bwd(lo, hi, start, end, q, k, v, do, lse):
    rows = q.shape[0]
    shape = jax.ShapeDtypeStruct((rows, FEAT), bf16)
    return pl.pallas_call(
        attend_bwd_body,
        out_shape=(shape, shape, shape),
        in_specs=[SM, SM] + [VM] * 7,
        out_specs=(VM, VM, VM),
        scratch_shapes=[
            pltpu.VMEM((HEADS, rows, QB), f32),
            pltpu.VMEM((HEADS, rows, QB), f32),
            pltpu.VMEM((rows, FEAT), f32),
            pltpu.VMEM((rows, FEAT), f32),
        ],
        name="attend_bwd",
        compiler_params=pltpu.CompilerParams(vmem_limit_bytes=48 << 20),
        cost_estimate=pl.CostEstimate(flops=20_000_000_000, bytes_accessed=6_000_000, transcendentals=4_000_000),
    )(lo, hi, start, end, q, k, v, do, lse)


def remote(src, dst, send_sem, recv_sem, device):
    return pltpu.make_async_remote_copy(
        src_ref=src, dst_ref=dst, send_sem=send_sem, recv_sem=recv_sem,
        device_id=device, device_id_type=MESH,
    )


def col_peers():
    r, c = lax.axis_index("row"), lax.axis_index("col")
    sib, nbr, diag = c + 1 - 2 * (c % 2), (c + 2) % 4, 3 - c
    return r, c, sib, nbr, diag


def norm_rows(x):
    mean = jnp.mean(x, axis=1, keepdims=True)
    center = x - mean
    var = jnp.mean(center * center, axis=1, keepdims=True)
    inv = lax.rsqrt(var + norm_eps)
    return center * inv, inv


def norm_back(grad, gain, hat, inv):
    e = grad * gain
    mean_e = jnp.mean(e, axis=1, keepdims=True)
    mean_c = jnp.mean(e * hat, axis=1, keepdims=True)
    return inv * (e - mean_e - hat * mean_c)


CH = 128


def middle_body(
    mixed_ref, tok_ref, cot_ref, wo_ref, win_ref, wout_ref, vec_ref, bin_ref,
    out_ref, g1_ref, gmix_ref, dwo_ref, dwin_ref, dwout_ref, dvec_ref, dbin_ref,
    nfull, hidden, slope, g2full, own, d2ds, d2dr, xs, xr, normed, hat1, inv1, grad2,
    ds_s, ds_r, x_s, x_r, asib_s, asib_r, anbr_s, anbr_r, afwd_s, afwd_r,
):
    r, c, sib, nbr, diag = col_peers()
    chunks = tok_ref.shape[0] // CH

    barrier = pltpu.get_barrier_semaphore()
    for peer in (sib, nbr):
        pl.semaphore_signal(barrier, inc=1, device_id=(r, peer), device_id_type=MESH)
    pl.semaphore_wait(barrier, 2)

    bo, g1, s1, b2, g2, s2 = [vec_ref[pl.ds(i, 1), :] for i in range(6)]

    def d2d(st, k):
        return remote(d2ds.at[st, k], d2dr.at[st, k], ds_s.at[st, k], ds_r.at[st, k], (r, sib))

    def xcopy(st, k):
        return remote(xs.at[st, k], xr.at[st, k], x_s.at[st, k], x_r.at[st, k], (r, nbr))

    def rs_start(st, k, part):
        d2ds[st, k, 0] = part(sib).astype(bf16)
        d2ds[st, k, 1] = part(diag).astype(bf16)
        d2d(st, k).start()
        mine = part(c)
        other = part(nbr)
        d2d(st, k).wait_recv()
        xs[st, k] = (other + d2dr[st, k, 1].astype(f32)).astype(bf16)
        xcopy(st, k).start()
        own[st, k] = mine + d2dr[st, k, 0].astype(f32)

    def rs_end(st, k):
        xcopy(st, k).wait_recv()
        return own[st, k] + xr[st, k].astype(f32)

    gathered = (nfull, g2full, g1_ref)

    def piece(st, q, k):
        return gathered[st].at[q, pl.ds(pl.multiple_of(k * CH, CH), CH), :]

    def ag_copy(st, k, q, sems, target):
        return remote(piece(st, q, k), piece(st, q, k), sems[0].at[st, k], sems[1].at[st, k], (r, target))

    to_sib = functools.partial(ag_copy, sems=(asib_s, asib_r), target=sib)
    to_nbr = functools.partial(ag_copy, sems=(anbr_s, anbr_r), target=nbr)
    fwd = functools.partial(ag_copy, sems=(afwd_s, afwd_r), target=sib)

    def ag_start(st, k, value):
        gathered[st][c, pl.ds(pl.multiple_of(k * CH, CH), CH), :] = value
        to_nbr(st, k, c).start()
        to_sib(st, k, c).start()

    def ag_end(st, k):
        to_nbr(st, k, c).wait_recv()
        fwd(st, k, nbr).start()
        to_sib(st, k, c).wait_recv()
        fwd(st, k, nbr).wait_recv()

    def rows_of(k):
        return pl.ds(pl.multiple_of(k * CH, CH), CH)

    def all_rows(ref, k):
        return ref[:, rows_of(k), :].reshape(4 * CH, ref.shape[2])

    @pl.loop(0, chunks)
    def _(k):
        rs_start(0, k, lambda q: mm(mixed_ref[q, rows_of(k), :], wo_ref[...], NT))

    @pl.loop(0, chunks)
    def _(k):
        resid = rs_end(0, k) + tok_ref[rows_of(k), :].astype(f32) + bo
        hat, inv = norm_rows(resid)
        hat1[k] = hat
        inv1[k] = inv
        val = hat * g1 + s1
        normed[k] = val
        ag_start(0, k, val.astype(bf16))

    @pl.loop(0, chunks)
    def _(k):
        ag_end(0, k)
        pre = mm(all_rows(nfull, k), win_ref[...], NN) + bin_ref[...]
        cum = 0.5 * (1.0 + lax.erf(pre * root_half))
        dens = jnp.exp(-0.5 * pre * pre) * inv_root_two_pi
        hidden[:, rows_of(k), :] = (pre * cum).astype(bf16).reshape(4, CH, D)
        slope[:, rows_of(k), :] = (cum + pre * dens).reshape(4, CH, D)
        rs_start(1, k, lambda q: mm(hidden[q, rows_of(k), :], wout_ref[...], NT))

    dvec_ref[...] = jnp.zeros_like(dvec_ref)

    @pl.loop(0, chunks)
    def _(k):
        resid = rs_end(1, k) + normed[k] + b2
        hat, inv = norm_rows(resid)
        out_ref[rows_of(k), :] = (hat * g2 + s2).astype(out_ref.dtype)
        cot = cot_ref[rows_of(k), :].astype(f32)
        grad = norm_back(cot, g2, hat, inv)
        grad2[k] = grad
        ag_start(1, k, grad.astype(bf16))
        dvec_ref[pl.ds(2, 1), :] += jnp.sum(grad, axis=0, keepdims=True)
        dvec_ref[pl.ds(5, 1), :] += jnp.sum(cot * hat, axis=0, keepdims=True)
        dvec_ref[pl.ds(6, 1), :] += jnp.sum(cot, axis=0, keepdims=True)

    dwin_ref[...] = jnp.zeros_like(dwin_ref)
    dwout_ref[...] = jnp.zeros_like(dwout_ref)
    dwo_ref[...] = jnp.zeros_like(dwo_ref)
    dbin_ref[...] = jnp.zeros_like(dbin_ref)

    @pl.loop(0, chunks)
    def _(k):
        ag_end(1, k)
        g2c = all_rows(g2full, k)
        grad_pre = mm(g2c, wout_ref[...], NN) * all_rows(slope, k)
        dbin_ref[...] += jnp.sum(grad_pre, axis=0, keepdims=True)
        low = grad_pre.astype(bf16)
        hid = all_rows(hidden, k)
        hidden[:, rows_of(k), :] = low.reshape(4, CH, D)
        rs_start(2, k, lambda q: mm(hidden[q, rows_of(k), :], win_ref[...], NT))
        dwout_ref[...] += mm(g2c, hid, TN)
        dwin_ref[...] += mm(all_rows(nfull, k), low, TN)

    @pl.loop(0, chunks)
    def _(k):
        grad_normed = rs_end(2, k) + grad2[k]
        hat = hat1[k]
        grad = norm_back(grad_normed, g1, hat, inv1[k])
        ag_start(2, k, grad.astype(bf16))
        dvec_ref[pl.ds(1, 1), :] += jnp.sum(grad, axis=0, keepdims=True)
        dvec_ref[pl.ds(3, 1), :] += jnp.sum(grad_normed * hat, axis=0, keepdims=True)
        dvec_ref[pl.ds(4, 1), :] += jnp.sum(grad_normed, axis=0, keepdims=True)

    @pl.loop(0, chunks)
    def _(k):
        ag_end(2, k)
        g1c = all_rows(g1_ref, k)
        gmix_ref[:, rows_of(k), :] = mm(g1c, wo_ref[...], NN).astype(bf16).reshape(4, CH, FEAT)
        dwo_ref[...] += mm(g1c, all_rows(mixed_ref, k), TN)

    @pl.loop(0, chunks)
    def _(k):
        for st in range(3):
            d2d(st, k).wait_send()
            xcopy(st, k).wait_send()
            to_sib(st, k, c).wait_send()
            to_nbr(st, k, c).wait_send()
            fwd(st, k, nbr).wait_send()


def middle(mixed, tok, cot, wo, win, wout, vec, b_in):
    own_rows = tok.shape[0]
    chunks = own_rows // CH
    sem = pltpu.SemaphoreType.DMA((3, chunks))
    S = jax.ShapeDtypeStruct
    return pl.pallas_call(
        middle_body,
        out_shape=(
            S((own_rows, D), bf16),
            S((4, own_rows, D), bf16),
            S((4, own_rows, FEAT), bf16),
            S((D, FEAT), f32),
            S((D, D), f32),
            S((D, D), f32),
            S((8, D), f32),
            S((1, D), f32),
        ),
        in_specs=[VM] * 8,
        out_specs=(VM,) * 8,
        scratch_shapes=[
            pltpu.VMEM((4, own_rows, D), bf16),
            pltpu.VMEM((4, own_rows, D), bf16),
            pltpu.VMEM((4, own_rows, D), f32),
            pltpu.VMEM((4, own_rows, D), bf16),
            pltpu.VMEM((3, chunks, CH, D), f32),
            pltpu.VMEM((3, chunks, 2, CH, D), bf16),
            pltpu.VMEM((3, chunks, 2, CH, D), bf16),
            pltpu.VMEM((3, chunks, CH, D), bf16),
            pltpu.VMEM((3, chunks, CH, D), bf16),
            pltpu.VMEM((chunks, CH, D), f32),
            pltpu.VMEM((chunks, CH, D), f32),
            pltpu.VMEM((chunks, CH, 1), f32),
            pltpu.VMEM((chunks, CH, D), f32),
        ]
        + [sem] * 10,
        name="middle",
        compiler_params=pltpu.CompilerParams(collective_id=2, has_side_effects=True, vmem_limit_bytes=60 << 20),
        cost_estimate=pl.CostEstimate(flops=80_000_000_000, bytes_accessed=20_000_000, transcendentals=4_000_000),
    )(mixed, tok, cot, wo, win, wout, vec, b_in)


def sent_and_summed(value, dim):
    size = lax.axis_size("row")
    before, after = value.shape[:dim], value.shape[dim + 1 :]
    pieces = jnp.moveaxis(value.reshape(*before, size, -1, *after), dim, 0)
    return jnp.sum(lax.all_to_all(pieces, "row", 0, 0, tiled=True).astype(f32), axis=0)


def per_device(
    inputs, cotangent, token_order, token_place, seq_lengths,
    query_weight, key_weight, value_weight, output_weight, inner_weight, outer_weight,
    query_bias, value_bias, output_bias, inner_bias, outer_bias,
    first_gain, first_shift, second_gain, second_shift,
):
    rows = lax.axis_size("row")
    col = lax.axis_index("col")
    given = lax.all_to_all(inputs.astype(bf16), "col", split_axis=1, concat_axis=0, tiled=True)
    given_g = lax.all_to_all(cotangent.astype(bf16), "col", split_axis=1, concat_axis=0, tiled=True)
    tok_rows = given.shape[0]
    send_order = jnp.argsort(token_place // tok_rows, stable=True)
    arrive_order = jnp.argsort(token_order, stable=True)
    got = lax.all_to_all(given[send_order], "row", split_axis=0, concat_axis=0, tiled=True)
    got_g = lax.all_to_all(given_g[send_order], "row", split_axis=0, concat_axis=0, tiled=True)
    dealt = jnp.zeros_like(got).at[arrive_order].set(got)
    dealt_g = jnp.zeros_like(got_g).at[arrive_order].set(got_g)
    own_rows = tok_rows // 4

    pack = jnp.concatenate(
        [query_weight, key_weight, value_weight, output_weight.T, inner_weight, outer_weight.T], axis=1
    )
    pack = lax.all_gather(pack, "row", axis=0, tiled=True)
    w_qkv, wo, win, wout = pack[:, :576], pack[:, 576:768], pack[:, 768:1536], pack[:, 1536:]
    vecs = jnp.concatenate(
        [query_bias, value_bias, output_bias, first_gain, first_shift, outer_bias, second_gain, second_shift, inner_bias]
    )[None]
    vecs = lax.all_gather(vecs, "row", axis=0, tiled=True)
    small = query_bias.shape[0]
    mine = vecs[:, : 8 * small].reshape(rows, 8, small).transpose(1, 0, 2).reshape(8, FEAT)
    b_in = vecs[:, 8 * small :].reshape(1, D).astype(f32)
    full = lax.all_gather(mine[2:], "col", axis=1, tiled=True).astype(f32)
    vec = jnp.concatenate([full, jnp.zeros((2, D), f32)], axis=0)

    seq_ends = jnp.cumsum(seq_lengths[0])
    seq_starts = seq_ends - seq_lengths[0]
    positions = jnp.arange(tok_rows, dtype=jnp.int32)
    seg = jnp.sum((positions[:, None] >= seq_ends[None, :]).astype(jnp.int32), axis=1)
    hot = (seg[:, None] == jnp.arange(seq_ends.shape[0])[None, :]).astype(jnp.int32)
    start = jnp.sum(hot * seq_starts[None], axis=1)
    end = jnp.sum(hot * seq_ends[None], axis=1)
    lo = start[::QB] // KB
    hi = (end[QB - 1 :: QB] + KB - 1) // KB
    start, end = start[None], end[None]

    tokens = lax.all_gather(dealt, "col", axis=1, tiled=True)
    cot = lax.all_to_all(dealt_g, "col", split_axis=0, concat_axis=1, tiled=True)
    qkv = jnp.dot(tokens, w_qkv, preferred_element_type=f32)
    q = (qkv[:, :192] + mine[0].astype(f32)).astype(bf16)
    k = qkv[:, 192:384].astype(bf16)
    v = (qkv[:, 384:] + mine[1].astype(f32)).astype(bf16)
    mixed, lse = attend_fwd(lo, hi, start, end, q, k, v)
    own_tok = lax.dynamic_slice_in_dim(tokens, col * own_rows, own_rows, axis=0)
    out, g1, gmix, dwo, dwin, dwout, dvec, dbin = middle(
        mixed.reshape(4, own_rows, FEAT), own_tok, cot, wo, win, wout, vec, b_in
    )
    dq, dk, dv = attend_bwd(lo, hi, start, end, q, k, v, gmix.reshape(tok_rows, FEAT), lse)
    dqkv = jnp.concatenate([dq, dk, dv], axis=1)
    dw_qkv = lax.dot_general(tokens, dqkv, TN, preferred_element_type=f32)
    db_q = jnp.sum(dq.astype(f32), axis=0)
    db_v = jnp.sum(dv.astype(f32), axis=0)
    back = lax.dot_general(dqkv, w_qkv, NT, preferred_element_type=f32).astype(bf16)
    grad_tok = lax.psum_scatter(back, "col", scatter_dimension=1, tiled=True).astype(f32)
    g1_cols = lax.dynamic_slice_in_dim(g1.reshape(tok_rows, D), col * FEAT, FEAT, axis=1)
    grad_tok = (grad_tok + g1_cols.astype(f32)).astype(bf16)

    dpack = jnp.concatenate([dw_qkv.astype(bf16), dwo.astype(bf16), dwin.astype(bf16), dwout.astype(bf16)], axis=1)
    dpack = sent_and_summed(dpack, 0)
    dmine = lax.psum_scatter(dvec[1:7], "col", scatter_dimension=1, tiled=True)
    dmine = jnp.concatenate([db_q[None], db_v[None], dmine], axis=0)
    dmine = dmine.reshape(8, rows, small).transpose(1, 0, 2).reshape(rows, 8 * small)
    dall = jnp.concatenate([dmine, dbin.reshape(rows, -1)], axis=1)
    dsum = jnp.sum(lax.all_to_all(dall, "row", 0, 0, tiled=True), axis=0)
    dv8 = dsum[: 8 * small].reshape(8, small)

    share = lax.all_to_all(out, "col", split_axis=1, concat_axis=0, tiled=True)

    def send_back(value):
        got_back = lax.all_to_all(value[arrive_order], "row", split_axis=0, concat_axis=0, tiled=True)
        placed = jnp.zeros_like(got_back).at[send_order].set(got_back)
        return lax.all_to_all(placed, "col", split_axis=0, concat_axis=1, tiled=True).astype(f32)

    output, input_grad = send_back(share), send_back(grad_tok)
    return (
        output, input_grad,
        dpack[:, :192], dpack[:, 192:384], dpack[:, 384:576], dpack[:, 576:768].T,
        dpack[:, 768:1536], dpack[:, 1536:].T,
        dv8[0], dv8[1], dv8[2], dsum[8 * small :], dv8[3], dv8[4], dv8[5], dv8[6], dv8[7],
    )


def solution(mesh):
    tok = P(("row", "col"), None)
    rc, cr, vec = P("row", "col"), P("col", "row"), P(("col", "row"))
    in_specs = (tok, tok, P("row"), P("row"), P("row", None), rc, rc, rc, cr, rc, cr) + (vec,) * 9
    out_specs = (tok, tok, rc, rc, rc, cr, rc, cr) + (vec,) * 9
    return jax.shard_map(per_device, mesh=mesh, in_specs=in_specs, out_specs=out_specs, check_vma=False)
```

time: 1240 us -> 632 us (0.51)
  waiting for transfers between devices: 430 us -> 129 us
  matrix products: 210 us -> 15 us
  Pallas kernels: 0 us -> 168 us
  blocking collectives: 215 us -> 74.1 us
  other arithmetic: 111 us -> 25.2 us
  starting transfers between devices: 100 us -> 48 us
    dot_general x46 -> x3, matrix products: 210 us -> 15 us  [the longest x1 5.41 us: per_device(): lax.dot_general(dqkv, w_qkv, NT, preferred_element_type=f32).astype(bf16)]
    pallas_call x0 -> x3, Pallas kernels: none -> 168 us  [the longest x1 117 us: middle(): pl.pallas_call(middle_body, out_shape=(S((own_rows, D), bf16), S((4, own_...]
    all_gather x4 -> x1, blocking collectives: 127 us -> 11.1 us  [per_device(): full = lax.all_gather(mine[2:], 'col', axis=1, tiled=True).astype(f32)]
    reduce_scatter x4 -> x1, waiting for transfers between devices: 113 us -> 0.01 us  [per_device(): lax.psum_scatter(back, 'col', scatter_dimension=1, tiled=True).astype(f32)]
    all_gather x6 -> x2, waiting for transfers between devices: 110 us -> 0.01 us  [the longest x1 0.01 us: per_device(): pack = lax.all_gather(pack, 'row', axis=0, tiled=True)]
    all_to_all x20 -> x10, waiting for transfers between devices: 206 us -> 129 us  [the longest x1 57.5 us: sent_and_summed(): lax.all_to_all(pieces, 'row', 0, 0, tiled=True).astype(f32)]
    reduce_sum x26 -> x5, other arithmetic: 59.5 us -> 1.18 us  [the longest x1 0.47 us: sent_and_summed(): jnp.sum(lax.all_to_all(pieces, 'row', 0, 0, tiled=True).astype(f32), axis=0)]
    psum x4 -> x0, blocking collectives: 40.7 us -> none  [row_pair(): return lax.psum((first_sum, second_sum), 'col')]
  transfers between devices with their start and end apart: 30 -> 14, of which waited for: 21 -> 6; matrix products, arithmetic and copies ran while one was open for 12% -> 26% of each run, Pallas kernels for 0% -> 5%
where the time goes in v1:
time: 632 us; the launch traced here: 623 us
  Pallas kernels  168 us (27%)
  local copies, waits for them, and re-layouts  148 us (23%)
  waiting for transfers between devices  129 us (20%)
  blocking collectives  74.1 us (12%)
  starting transfers between devices  48 us (8%)
  other arithmetic  25.2 us (4%)
  between operations  15.6 us (2%)
  matrix products  15 us (2%)
    pallas_call x1, Pallas kernels, middle(): pl.pallas_call(middle_body, out_shape=(S((own_rows, D), bf16), S((4, own_...  117 us
    all_to_all x1, waiting for transfers between devices, sent_and_summed(): lax.all_to_all(pieces, 'row', 0, 0, tiled=True).astype(f32)  57.5 us
    all_to_all x1, waiting for transfers between devices, per_device(): lax.all_to_all(given[send_order], 'row', split_axis=0, concat_axis=0, til...  36.8 us
    pallas_call x1, Pallas kernels, attend_bwd(): pl.pallas_call(attend_bwd_body, out_shape=(shape, shape, shape), in_specs...  30.1 us
    unnamed x1, blocking collectives  25.9 us
    unnamed x62, local copies, waits for them, and re-layouts  22.8 us
    all_to_all x2, waiting for transfers between devices, send_back(): lax.all_to_all(value[arrive_order], 'row', split_axis=0, concat_axis=0, t...  22.1 us
    all_to_all x1, blocking collectives, per_device(): lax.all_to_all(cotangent.astype(bf16), 'col', split_axis=1, concat_axis=0...  21.9 us
  transfers between devices with their start and end apart: 14, of which 6 were waited for; matrix products, arithmetic and copies ran while one was open for 26% of the time, Pallas kernels for 5%

profile of v1, /device:TPU:0, one launch (start us, length us, event | category | flops | bytes accessed | tf_op | source)
XLA Modules:
  0.0 623.3 jit_solution(467171180927266609)
XLA Ops:
  12.7 4.2 all-to-all-start
  16.9 5.0 sort.31
  22.6 6.0 all-to-all-done
  29.1 7.5 %gather_fusion = bf16[2048,192]{1,0:T(8,128)(2,1)S(1)} fusion(bf16[2048,192]{1,0:T(8,128)(2,1)S(1)} %bitcast.80, s32[2048]{0:T(1024)S(1)} %get-tuple-element.199), kind=kCustom, calls=%fused_computation | custom fusion | bytes 1581056 | tf_op jit(solution)/shard_map/gather | solution.py:431
  37.8 6.5 %all-to-all-start.1 = ((bf16[8,256,192]{1,2,0:T(8,128)(2,1)}), bf16[8,256,192]{1,2,0:T(8,128)(2,1)S(1)}, u32[]{:S(2)}, u32[]{:S(2)}) async-start(bf16[8,256,192]{1,2,0:T(8,128)(2,1)} %copy.264), calls=%async_computation.1 | async-start | bytes 1572864 | tf_op jit(solution)/shard_map/all_to_all | solution.py:431
  44.5 5.0 sort.32
  49.5 36.8 %all-to-all-done.1 = bf16[8,256,192]{1,2,0:T(8,128)(2,1)S(1)} async-done(((bf16[8,256,192]{1,2,0:T(8,128)(2,1)}), bf16[8,256,192]{1,2,0:T(8,128)(2,1)S(1)}, u32[]{:S(2)}, u32[]{:S(2)}) %all-to-all-start.1) | async-done | bytes 786464 | tf_op jit(solution)/shard_map/all_to_all | solution.py:431
  87.6 9.9 %scatter_custom_fusion = bf16[2048,192]{1,0:T(8,128)(2,1)S(1)} fusion(s32[2048]{0:T(1024)S(1)} %get-tuple-element.198, bf16[2048,192]{1,0:T(8,128)(2,1)} %bitcast.100, bf16[]{:T(256)} %constant.51.clone.1), kind=kCustom, calls=%fused_computation.27 | custom fusion | bytes 786944 | tf_op jit(solution)/shard_map/scatter | solution.py:433
  99.1 21.9 %all_to_all.164 = bf16[512,4,192]{0,2,1:T(8,128)(2,1)S(1)} all-to-all(bf16[512,4,192]{0,2,1:T(8,128)(2,1)S(1)} %bitcast.95), channel_id=1, replica_groups=mesh['row'=8,'col'=4] {'col'}, dimensions={1} | all-to-all | bytes 1572864 | tf_op jit(solution)/shard_map/all_to_all | solution.py:427
  121.4 7.5 %gather_fusion.1 = bf16[2048,192]{1,0:T(8,128)(2,1)S(1)} fusion(bf16[2048,192]{1,0:T(8,128)(2,1)S(1)} %bitcast.78, s32[2048]{0:T(1024)S(1)} %get-tuple-element.199), kind=kCustom, calls=%fused_computation.1 | custom fusion | bytes 1581056 | tf_op jit(solution)/shard_map/gather | solution.py:432
  135.6 25.9 %all-reduce.1 = bf16[2304]{0:T(1024)(128)(2,1)S(1)} all-reduce(bf16[2304]{0:T(1024)(128)(2,1)S(1)} %dynamic-update-slice), channel_id=2, replica_groups=mesh['row'=8,'col'=4] {'row'}, use_global_device_ids=true, to_apply=%add.1 | all-reduce | flops 2304 | bytes 9216
  162.5 9.6 %scatter_custom_fusion.1 = bf16[2048,192]{1,0:T(8,128)(2,1)S(1)} fusion(s32[2048]{0:T(1024)S(1)} %get-tuple-element.198, bf16[2048,192]{1,0:T(8,128)(2,1)S(1)} %bitcast.98, bf16[]{:T(256)} %constant.51.clone.1), kind=kCustom, calls=%fused_computation.25 | custom fusion | bytes 786434 | tf_op jit(solution)/shard_map/scatter | solution.py:434
  178.3 11.1 %all-gather.1 = bf16[4,192,6]{1,2,0:T(8,128)(2,1)S(1)} all-gather(bf16[1,192,6]{1,2,0:T(8,128)(2,1)S(1)} %bitcast.108), channel_id=1, replica_groups=mesh['row'=8,'col'=4] {'col'}, dimensions={0}, use_global_device_ids=true | all-gather | bytes 11520 | tf_op jit(solution)/shard_map/all_gather | solution.py:449
  196.5 4.3 fusion.1
  212.4 21.7 %attend_fwd.1 = (bf16[2048,192]{1,0:T(8,128)(2,1)S(1)}, f32[8,2048]{1,0:T(8,128)S(1)}) custom-call(s32[8]{0:T(128)S(1)} %get-tuple-element.210.lo_ref, s32[8]{0:T(128)S(1)} %get-tuple-element.209.hi_ref, s32[1,2048]{1,0:T(1,128)S(1)} %bitcast.75, s32[1,2048]{1,0:T(1,128)S(1)} %bitcast.73, bf16[2048,192]{1,0:T(8,128)(2,1)S(1)} %get-tuple-element.212.q_ref, ...), custom_call_target="tpu_custom_call" | custom-call | flops 8000000000 | bytes 4000000 | tf_op jit(solution)/shard_map/attend_fwd/pallas_call | solution.py:94
  235.1 116.6 %middle.1 = (bf16[512,768]{1,0:T(8,128)(2,1)}, bf16[4,512,768]{2,1,0:T(8,128)(2,1)}, bf16[4,512,192]{2,1,0:T(8,128)(2,1)}, f32[768,192]{1,0:T(8,128)}, f32[768,7...) custom-call(bf16[4,512,192]{2,1,0:T(8,128)(2,1)} %bitcast.77, ...), custom_call_target="tpu_custom_call" | custom-call | flops 80000000000 | bytes 20000000 | tf_op jit(solution)/shard_map/middle/pallas_call | solution.py:375
  354.7 30.1 %attend_bwd.1 = (bf16[2048,192]{1,0:T(8,128)(2,1)S(1)}, bf16[2048,192]{1,0:T(8,128)(2,1)S(1)}, bf16[2048,192]{1,0:T(8,128)(2,1)S(1)}) custom-call(s32[8]{0:T(128)S(1)} %get-tuple-element.210.lo_ref, s32[8]{0:T(128)S(1)} %get-tuple-element.209.hi_ref, s32[1,2048]{1,0:T(1,128)S(1)} %bitcast.76, s32[1,2048]{1,0:T(1,128)S(1)} %bitcast.74, ...), custom_call_target="tpu_custom_call" | custom-call | flops 20000000000 | bytes 6000000 | tf_op jit(solution)/shard_map/attend_bwd/pallas_call | solution.py:172
  385.8 5.4 convolution_convert_fusion
  392.6 15.3 %all_to_all.165 = bf16[512,4,192]{0,2,1:T(8,128)(2,1)} all-to-all(bf16[512,4,192]{0,2,1:T(8,128)(2,1)S(1)} %bitcast.94), channel_id=1, replica_groups=mesh['row'=8,'col'=4] {'col'}, dimensions={1} | all-to-all | bytes 1572864 | tf_op jit(solution)/shard_map/all_to_all | solution.py:493
  409.3 9.1 %gather_fusion.2 = bf16[2048,192]{1,0:T(8,128)(2,1)} fusion(bf16[2048,192]{1,0:T(8,128)(2,1)S(1)} %bitcast.79, s32[2048]{0:T(1024)S(1)} %get-tuple-element.197), kind=kCustom, calls=%fused_computation.2 | custom fusion | bytes 1581056 | tf_op jit(solution)/shard_map/gather | solution.py:496
  420.6 8.0 %all-to-all-start.6 = ((bf16[8,256,192]{1,2,0:T(8,128)(2,1)}), bf16[8,256,192]{1,2,0:T(8,128)(2,1)S(1)}, u32[]{:S(2)}, u32[]{:S(2)}) async-start(bf16[8,256,192]{1,2,0:T(8,128)(2,1)} %copy.285), calls=%async_computation.6 | async-start | bytes 1572864 | tf_op jit(solution)/shard_map/all_to_all | solution.py:496
  431.2 17.5 %all-to-all-done.6 = bf16[8,256,192]{1,2,0:T(8,128)(2,1)S(1)} async-done(((bf16[8,256,192]{1,2,0:T(8,128)(2,1)}), bf16[8,256,192]{1,2,0:T(8,128)(2,1)S(1)}, u32[]{:S(2)}, u32[]{:S(2)}) %all-to-all-start.6) | async-done | bytes 786464 | tf_op jit(solution)/shard_map/all_to_all | solution.py:496
  453.6 9.9 %scatter_custom_fusion.2 = bf16[2048,192]{1,0:T(8,128)(2,1)S(1)} fusion(s32[2048]{0:T(1024)} %get-tuple-element.200, bf16[2048,192]{1,0:T(8,128)(2,1)} %bitcast.99, bf16[]{:T(256)} %constant.51.clone.1), kind=kCustom, calls=%fused_computation.23 | custom fusion | bytes 786944 | tf_op jit(solution)/shard_map/scatter | solution.py:497
  464.8 4.2 all-to-all-start.7
  476.0 9.1 %gather_fusion.3 = bf16[2048,192]{1,0:T(8,128)(2,1)} fusion(bf16[2048,192]{1,0:T(8,128)(2,1)S(1)} %copy.291, s32[2048]{0:T(1024)S(1)} %get-tuple-element.197), kind=kCustom, calls=%fused_computation.3 | custom fusion | bytes 1581056 | tf_op jit(solution)/shard_map/gather | solution.py:496
  487.4 6.3 %all-to-all-start.8 = ((bf16[8,256,192]{1,2,0:T(8,128)(2,1)}), bf16[8,256,192]{1,2,0:T(8,128)(2,1)}, u32[]{:S(2)}, u32[]{:S(2)}) async-start(bf16[8,256,192]{1,2,0:T(8,128)(2,1)} %copy.292), calls=%async_computation.9 | async-start | bytes 1572864 | tf_op jit(solution)/shard_map/all_to_all | solution.py:496
  493.7 5.3 convolution_convert_fusion.1
  504.6 5.4 concatenate.35
  509.9 4.6 all-to-all-done.8
  527.1 10.7 %scatter_custom_fusion.3 = bf16[2048,192]{1,0:T(8,128)(2,1)} fusion(s32[2048]{0:T(1024)} %get-tuple-element.200, bf16[2048,192]{1,0:T(8,128)(2,1)} %bitcast.97, bf16[]{:T(256)} %constant.51.clone.1), kind=kCustom, calls=%fused_computation.21 | custom fusion | bytes 786944 | tf_op jit(solution)/shard_map/scatter | solution.py:497
  540.0 57.5 %all-to-all-done.10 = bf16[8,96,2304]{2,1,0:T(8,128)(2,1)S(1)} async-done(((bf16[8,96,2304]{2,1,0:T(8,128)(2,1)}), bf16[8,96,2304]{2,1,0:T(8,128)(2,1)S(1)}, u32[]{:S(2)}, u32[]{:S(2)}) %all-to-all-start.10) | async-done | bytes 3538976 | tf_op jit(solution)/shard_map/all_to_all | solution.py:415
  606.5 6.9 %all-to-all-done.9 = bf16[4,512,192]{1,2,0:T(8,128)(2,1)} async-done(((bf16[4,512,192]{1,2,0:T(8,128)(2,1)}), bf16[4,512,192]{1,2,0:T(8,128)(2,1)}, u32[]{:S(2)}, u32[]{:S(2)}) %all-to-all-start.9) | async-done | bytes 786464 | tf_op jit(solution)/shard_map/all_to_all | solution.py:498
  (160 shorter events, 103.1 us)
Async XLA Ops:
  7.2 184.1 %all-gather.7.cloned.1.call-start = ((), (), s32[]{:S(2)}) async-start(), calls=%async_computation.15 | async-start | bytes 3981312 | tf_op jit(solution)/shard_map/all_gather | solution.py:440
  8.1 8.8 %copy-start.9 = (s32[2048]{0:T(1024)S(1)}, s32[2048]{0:T(1024)}, u32[]{:S(2)}) copy-start(s32[2048]{0:T(1024)} %param.23) | copy-start | bytes 24580
  12.7 15.9 %all-to-all-start = ((bf16[512,4,192]{0,2,1:T(8,128)(2,1)}), bf16[512,4,192]{0,2,1:T(8,128)(2,1)S(1)}, u32[]{:S(2)}, u32[]{:S(2)}) async-start(bf16[512,4,192]{0,2,1:T(8,128)(2,1)} %bitcast.6), calls=%async_computation | async-start | bytes 1572864 | tf_op jit(solution)/shard_map/all_to_all | solution.py:426
  36.6 7.9 %copy-start.10 = (s32[2048]{0:T(1024)S(1)}, s32[2048]{0:T(1024)}, u32[]{:S(2)}) copy-start(s32[2048]{0:T(1024)} %param.22) | copy-start | bytes 24580
  37.8 48.4 %all-to-all-start.1 = ((bf16[8,256,192]{1,2,0:T(8,128)(2,1)}), bf16[8,256,192]{1,2,0:T(8,128)(2,1)S(1)}, u32[]{:S(2)}, u32[]{:S(2)}) async-start(bf16[8,256,192]{1,2,0:T(8,128)(2,1)} %copy.264), calls=%async_computation.1 | async-start | bytes 1572864 | tf_op jit(solution)/shard_map/all_to_all | solution.py:431
  44.4 152.1 %all-gather.5.cloned.1.call-start = ((), (), s32[]{:S(2)}) async-start(), calls=%async_computation.14 | async-start | bytes 3932160 | tf_op jit(solution)/shard_map/all_gather | solution.py:463
  49.5 49.3 %copy-start.8 = (f32[512,768]{1,0:T(8,128)S(1)}, f32[512,768]{1,0:T(8,128)}, u32[]{:S(2)}) copy-start(f32[512,768]{1,0:T(8,128)} %param.21) | copy-start | bytes 4718596
  128.9 5.0 copy-start.22
  128.9 6.2 copy-start.12
  129.0 6.2 copy-start.13
  129.0 6.2 copy-start.14
  129.0 6.2 copy-start.15
  129.0 6.2 copy-start.16
  129.0 6.2 copy-start.17
  129.0 6.2 copy-start.18
  129.0 6.2 copy-start.19
  129.0 6.2 copy-start.20
  129.1 32.5 %copy-start.21 = (s32[1,8]{1,0:T(1,128)S(1)}, s32[1,8]{1,0:T(1,128)}, u32[]{:S(2)}) copy-start(s32[1,8]{1,0:T(1,128)} %param.24) | copy-start | bytes 100
  130.3 31.6 %all-to-all-start.3 = ((bf16[8,256,192]{1,2,0:T(8,128)(2,1)}), bf16[8,256,192]{1,2,0:T(8,128)(2,1)S(1)}, u32[]{:S(2)}, u32[]{:S(2)}) async-start(bf16[8,256,192]{1,2,0:T(8,128)(2,1)} %copy.276), calls=%async_computation.3 | async-start | bytes 1572864 | tf_op jit(solution)/shard_map/all_to_all | solution.py:432
  173.3 16.8 %all-to-all-start.4 = ((bf16[4,512,192]{1,2,0:T(8,128)(2,1)}), bf16[4,512,192]{1,2,0:T(8,128)(2,1)S(1)}, u32[]{:S(2)}, u32[]{:S(2)}) async-start(bf16[4,512,192]{1,2,0:T(8,128)(2,1)} %copy.280), calls=%async_computation.4 | async-start | bytes 1572864 | tf_op jit(solution)/shard_map/all_to_all | solution.py:464
  176.8 252.6 %reduce-scatter.7.cloned.1.call-start = ((), (), s32[]{:S(2)}) async-start(), calls=%async_computation.17 | async-start | bytes 491520
  212.3 21.8 %copy-start = (bf16[2048,192]{1,0:T(8,128)(2,1)}, bf16[2048,192]{1,0:T(8,128)(2,1)S(1)}, u32[]{:S(2)}) copy-start(bf16[2048,192]{1,0:T(8,128)(2,1)S(1)} %get-tuple-element.211.v_ref) | copy-start | bytes 2359300
  212.3 21.8 %copy-start.1 = (bf16[2048,192]{1,0:T(8,128)(2,1)}, bf16[2048,192]{1,0:T(8,128)(2,1)S(1)}, u32[]{:S(2)}) copy-start(bf16[2048,192]{1,0:T(8,128)(2,1)S(1)} %get-tuple-element.212.q_ref) | copy-start | bytes 2359300
  353.4 118.7 %reduce-scatter.5.cloned.1.call-start = ((), (), s32[]{:S(2)}) async-start(), calls=%async_computation.16 | async-start | bytes 3932160 | tf_op jit(solution)/shard_map/reduce_scatter | solution.py:480
  418.4 10.9 %copy-start.11 = (f32[1,768]{1,0:T(1,128)S(1)}, f32[1,768]{1,0:T(1,128)}, u32[]{:S(2)}) copy-start(f32[1,768]{1,0:T(1,128)} %get-tuple-element.46) | copy-start | bytes 9220
  420.6 28.1 %all-to-all-start.6 = ((bf16[8,256,192]{1,2,0:T(8,128)(2,1)}), bf16[8,256,192]{1,2,0:T(8,128)(2,1)S(1)}, u32[]{:S(2)}, u32[]{:S(2)}) async-start(bf16[8,256,192]{1,2,0:T(8,128)(2,1)} %copy.285), calls=%async_computation.6 | async-start | bytes 1572864 | tf_op jit(solution)/shard_map/all_to_all | solution.py:496
  448.7 16.0 %all-to-all-start.11 = ((f32[8,1,288]{2,1,0:T(1,128)}), f32[8,1,288]{2,1,0:T(1,128)S(1)}, u32[]{:S(2)}, u32[]{:S(2)}) async-start(f32[8,1,288]{2,1,0:T(1,128)} %copy.299), calls=%async_computation.12 | async-start | bytes 24576 | tf_op jit(solution)/shard_map/all_to_all | solution.py:490
  464.8 22.6 %all-to-all-start.7 = ((bf16[4,512,192]{1,2,0:T(8,128)(2,1)}), bf16[4,512,192]{1,2,0:T(8,128)(2,1)}, u32[]{:S(2)}, u32[]{:S(2)}) async-start(bf16[4,512,192]{1,2,0:T(8,128)(2,1)} %copy.289), calls=%async_computation.7 | async-start | bytes 1572864 | tf_op jit(solution)/shard_map/all_to_all | solution.py:498
  485.1 8.6 %copy-start.5 = (bf16[2048,192]{1,0:T(8,128)(2,1)S(1)}, bf16[2048,192]{1,0:T(8,128)(2,1)}, u32[]{:S(2)}) copy-start(bf16[2048,192]{1,0:T(8,128)(2,1)} %copy-done.4) | copy-start | bytes 2359300
  487.4 27.1 %all-to-all-start.8 = ((bf16[8,256,192]{1,2,0:T(8,128)(2,1)}), bf16[8,256,192]{1,2,0:T(8,128)(2,1)}, u32[]{:S(2)}, u32[]{:S(2)}) async-start(bf16[8,256,192]{1,2,0:T(8,128)(2,1)} %copy.292), calls=%async_computation.9 | async-start | bytes 1572864 | tf_op jit(solution)/shard_map/all_to_all | solution.py:496
  514.5 83.0 %all-to-all-start.10 = ((bf16[8,96,2304]{2,1,0:T(8,128)(2,1)}), bf16[8,96,2304]{2,1,0:T(8,128)(2,1)S(1)}, u32[]{:S(2)}, u32[]{:S(2)}) async-start(bf16[8,96,2304]{2,1,0:T(8,128)(2,1)} %bitcast.42), calls=%async_computation.11 | async-start | bytes 7077888 | tf_op jit(solution)/shard_map/all_to_all | solution.py:415
  597.5 15.9 %all-to-all-start.9 = ((bf16[4,512,192]{1,2,0:T(8,128)(2,1)}), bf16[4,512,192]{1,2,0:T(8,128)(2,1)}, u32[]{:S(2)}, u32[]{:S(2)}) async-start(bf16[4,512,192]{1,2,0:T(8,128)(2,1)} %copy.296), calls=%async_computation.10 | async-start | bytes 1572864 | tf_op jit(solution)/shard_map/all_to_all | solution.py:498
  (5 other events, 8.0 us)
Sparse Core Ops, SparseCore 0:
  10.3 83.1 all-gather.6
  98.9 32.6 all-gather.4
  353.5 22.9 reduce-scatter.6
  391.3 42.1 reduce-scatter.4

commit v2 on v1

--- a/solution.py
+++ b/solution.py
@@ -35,10 +35,21 @@
     return lax.broadcasted_iota(jnp.int32, (rows, FEAT), 1) // HD
 
 
-def attend_fwd_body(lo_ref, hi_ref, start_ref, end_ref, q_ref, k_ref, v_ref, mix_ref, lse_ref, s_buf):
+def attend_fwd_body(
+    lo_ref, hi_ref, start_ref, end_ref, tok_ref, w_ref, b_ref, q_ref, k_ref, v_ref, mix_ref, lse_ref, s_buf,
+):
     scale = HD ** (-0.5)
     blocks = q_ref.shape[0] // QB
     heads = lane_head(QB)
+    b_q, b_v = b_ref[0:1, :], b_ref[1:2, :]
+
+    @pl.loop(0, blocks)
+    def _(qb):
+        rows = pl.ds(qb * QB, QB)
+        out = mm(tok_ref[rows, :], w_ref[...], NN)
+        q_ref[rows, :] = (out[:, :FEAT] + b_q).astype(bf16)
+        k_ref[rows, :] = out[:, FEAT : 2 * FEAT].astype(bf16)
+        v_ref[rows, :] = (out[:, 2 * FEAT :] + b_v).astype(bf16)
 
     @pl.loop(0, blocks)
     def _(qb):
@@ -89,26 +100,24 @@
             lse_ref[pl.ds(h, 1), rows] = tops[h] + jnp.log(sums[h])
 
 
-def attend_fwd(lo, hi, start, end, q, k, v):
-    rows = q.shape[0]
+def attend_fwd(lo, hi, start, end, tokens, w_qkv, bias):
+    rows = tokens.shape[0]
+    part = jax.ShapeDtypeStruct((rows, FEAT), bf16)
     return pl.pallas_call(
         attend_fwd_body,
-        out_shape=(
-            jax.ShapeDtypeStruct((rows, FEAT), bf16),
-            jax.ShapeDtypeStruct((8, rows), f32),
-        ),
-        in_specs=[SM, SM, VM, VM, VM, VM, VM],
-        out_specs=(VM, VM),
+        out_shape=(part, part, part, part, jax.ShapeDtypeStruct((8, rows), f32)),
+        in_specs=[SM, SM] + [VM] * 5,
+        out_specs=(VM,) * 5,
         scratch_shapes=[pltpu.VMEM((HEADS, rows, QB), f32)],
         name="attend_fwd",
         compiler_params=pltpu.CompilerParams(vmem_limit_bytes=40 << 20),
-        cost_estimate=pl.CostEstimate(flops=8_000_000_000, bytes_accessed=4_000_000, transcendentals=4_000_000),
-    )(lo, hi, start, end, q, k, v)
+        cost_estimate=pl.CostEstimate(flops=8_000_000_000, bytes_accessed=8_000_000, transcendentals=4_000_000),
+    )(lo, hi, start, end, tokens, w_qkv, bias)
 
 
 def attend_bwd_body(
     lo_ref, hi_ref, start_ref, end_ref, q_ref, k_ref, v_ref, do_ref, lse_ref,
-    dq_ref, dk_ref, dv_ref, p_buf, dp_buf, dk_acc, dv_acc,
+    dqkv_ref, p_buf, dp_buf, dq_acc, dk_acc, dv_acc,
 ):
     scale = HD ** (-0.5)
     blocks = q_ref.shape[0] // QB
@@ -160,23 +169,26 @@
             return acc
 
         acc = lax.fori_loop(lo, hi, second, jnp.zeros((QB, FEAT), f32))
-        dq_ref[rows, :] = (acc * scale).astype(bf16)
-
-    dk_ref[...] = (dk_acc[...] * scale).astype(bf16)
-    dv_ref[...] = dv_acc[...].astype(bf16)
+        dq_acc[rows, :] = acc
+
+    @pl.loop(0, blocks)
+    def _(qb):
+        rows = pl.ds(qb * QB, QB)
+        parts = [dq_acc[rows, :] * scale, dk_acc[rows, :] * scale, dv_acc[rows, :]]
+        dqkv_ref[rows, :] = jnp.concatenate([p.astype(bf16) for p in parts], axis=1)
 
 
 def attend_bwd(lo, hi, start, end, q, k, v, do, lse):
     rows = q.shape[0]
-    shape = jax.ShapeDtypeStruct((rows, FEAT), bf16)
     return pl.pallas_call(
         attend_bwd_body,
-        out_shape=(shape, shape, shape),
+        out_shape=jax.ShapeDtypeStruct((rows, 3 * FEAT), bf16),
         in_specs=[SM, SM] + [VM] * 7,
-        out_specs=(VM, VM, VM),
+        out_specs=VM,
         scratch_shapes=[
             pltpu.VMEM((HEADS, rows, QB), f32),
             pltpu.VMEM((HEADS, rows, QB), f32),
+            pltpu.VMEM((rows, FEAT), f32),
             pltpu.VMEM((rows, FEAT), f32),
             pltpu.VMEM((rows, FEAT), f32),
         ],
@@ -408,11 +420,605 @@
     )(mixed, tok, cot, wo, win, wout, vec, b_in)
 
 
-def sent_and_summed(value, dim):
-    size = lax.axis_size("row")
-    before, after = value.shape[:dim], value.shape[dim + 1 :]
-    pieces = jnp.moveaxis(value.reshape(*before, size, -1, *after), dim, 0)
-    return jnp.sum(lax.all_to_all(pieces, "row", 0, 0, tiled=True).astype(f32), axis=0)
+HALF = 384
+
+
+def half_lanes(h):
+    return pl.ds(pl.multiple_of(h * HALF, HALF), HALF)
+
+
+def greet(peers, rows, row, c):
+    barrier = pltpu.get_barrier_semaphore()
+    for peer in peers:
+        pl.semaphore_signal(barrier, inc=1, device_id=(row, peer), device_id_type=MESH)
+
+    @pl.loop(1, rows)
+    def _(i):
+        pl.semaphore_signal(barrier, inc=1, device_id=((row + i) % rows, c), device_id_type=MESH)
+
+    pl.semaphore_wait(barrier, len(peers) + rows - 1)
+
+
+def to_col(src, dst):
+    eye = lax.broadcasted_iota(jnp.int32, (128, 128), 0) == lax.broadcasted_iota(jnp.int32, (128, 128), 1)
+
+    @pl.loop(0, dst.shape[0] // 128)
+    def _(t):
+        at = pl.ds(pl.multiple_of(t * 128, 128), 128)
+        dst[at, :] = jnp.sum(jnp.where(eye, src[:, at], 0.0), axis=1, keepdims=True)
+
+
+def rank_row(row_ref, col_ref):
+    keys = row_ref[...]
+    size = keys.shape[1]
+
+    def step(t, acc):
+        col = col_ref[pl.ds(pl.multiple_of(t * 128, 128), 128), :]
+        less = jnp.where(col < keys, 1.0, 0.0)
+        return acc + jnp.sum(less.reshape(16, 8, size), axis=0)
+
+    acc = lax.fori_loop(0, size // 128, step, jnp.zeros((8, size), f32))
+    return jnp.sum(acc, axis=0, keepdims=True)
+
+
+def picker_rows(rank, first, count):
+    want = (lax.broadcasted_iota(jnp.int32, (count, rank.shape[1]), 0) + first).astype(f32)
+    return jnp.where(rank == want, 1.0, 0.0).astype(bf16)
+
+
+def picker_cols(rank, count):
+    have = lax.broadcasted_iota(jnp.int32, (rank.shape[0], count), 1).astype(f32)
+    return jnp.where(rank == have, 1.0, 0.0).astype(bf16)
+
+
+class Deal:
+    def __init__(self, a, rows, bufs, sems):
+        self.a, self.rows = a, rows
+        self.xin, self.xout, self.sbuf, self.rbuf = bufs
+        self.sib_s, self.sib_r, self.nbr_s, self.nbr_r, self.fwd_s, self.fwd_r, self.row_s, self.row_r, self.sh_s, self.sh_r = sems
+        self.r, self.c, self.sib, self.nbr, self.diag = col_peers()
+        self.h, self.core = self.c // 2, self.c % 2
+        self.tokens = self.xin.shape[2] * 4
+        self.slots = self.tokens // rows
+        self.own_slots = self.slots // 2
+
+    def to_sib(self):
+        v = self.xin.at[self.a, self.c]
+        return remote(v, v, self.sib_s.at[self.a], self.sib_r.at[self.a], (self.r, self.sib))
+
+    def to_nbr(self):
+        return remote(self.xout.at[self.a], self.xin.at[self.a, self.c], self.nbr_s.at[self.a], self.nbr_r.at[self.a], (self.r, self.nbr))
+
+    def fwd(self):
+        v = self.xin.at[self.a, self.nbr]
+        return remote(v, v, self.fwd_s.at[self.a], self.fwd_r.at[self.a], (self.r, self.sib))
+
+    def split(self, ref):
+        self.xout[self.a] = ref[:, half_lanes(1 - self.h)].astype(bf16)
+        self.to_nbr().start()
+        self.xin[self.a, self.c] = ref[:, half_lanes(self.h)].astype(bf16)
+        self.to_sib().start()
+
+    def joined(self):
+        self.to_nbr().wait_recv()
+        self.fwd().start()
+        self.to_sib().wait_recv()
+        self.fwd().wait_recv()
+
+    def row_copy(self, i):
+        to = (self.r + i) % self.rows
+        return remote(
+            self.sbuf.at[self.a, i], self.rbuf.at[self.a, self.r, self.core],
+            self.row_s.at[self.a, i], self.row_r.at[self.a, i], (to, self.c),
+        )
+
+    def share(self, i):
+        v = self.rbuf.at[self.a, (self.r + self.rows - i) % self.rows, self.core]
+        return remote(v, v, self.sh_s.at[self.a, i], self.sh_r.at[self.a, i], (self.r, self.sib))
+
+    def pick_and_send(self, rank):
+        source = self.xin[self.a].reshape(self.tokens, HALF)
+
+        def picked(to):
+            return mm(picker_rows(rank, to * self.slots + self.core * self.own_slots, self.own_slots), source, NN).astype(bf16)
+
+        @pl.loop(1, self.rows)
+        def _(i):
+            self.sbuf[self.a, i] = picked((self.r + i) % self.rows)
+            self.row_copy(i).start()
+
+        self.rbuf[self.a, self.r, self.core] = picked(self.r)
+        self.share(0).start()
+
+    def shared(self):
+        @pl.loop(1, self.rows)
+        def _(i):
+            self.row_copy(i).wait_recv()
+            self.share(i).start()
+
+        @pl.loop(0, self.rows)
+        def _(i):
+            self.share(i).wait_recv()
+
+    def placed(self, rank_col):
+        return mm(picker_cols(rank_col, self.tokens), self.rbuf[self.a].reshape(self.tokens, HALF), NN)
+
+    def finish(self, joins=True):
+        if joins:
+            self.to_sib().wait_send()
+            self.to_nbr().wait_send()
+        self.fwd().wait_send()
+
+        @pl.loop(1, self.rows)
+        def _(i):
+            self.row_copy(i).wait_send()
+
+        @pl.loop(0, self.rows)
+        def _(i):
+            self.share(i).wait_send()
+
+
+def deal_scratch(rows, own_rows):
+    slots = 4 * own_rows // rows
+    return [
+        pltpu.VMEM((2, 4, own_rows, HALF), bf16),
+        pltpu.VMEM((2, own_rows, HALF), bf16),
+        pltpu.VMEM((2, rows, slots // 2, HALF), bf16),
+        pltpu.VMEM((2, rows, 2, slots // 2, HALF), bf16),
+    ]
+
+
+def deal_sems(rows):
+    return [pltpu.SemaphoreType.DMA((2,))] * 6 + [pltpu.SemaphoreType.DMA((2, rows))] * 4
+
+
+def arrive_body(
+    rows, x_ref, g_ref, place_ref, order_ref, vin_ref,
+    tok_ref, cot_ref, rank_ref, vec_ref, bqv_ref, bin_ref,
+    *scratch,
+):
+    bufs, sems = scratch[:4], scratch[4:14]
+    key_g, key_w, col_g, col_w, cot_send, vbuf = scratch[14:20]
+    an_s, an_r, as_s, as_r, af_s, af_r, ct_s, ct_r, vr_s, vr_r, vc_s, vc_r = scratch[20:]
+    r, c, sib, nbr, diag = col_peers()
+    h = c // 2
+    own_rows = x_ref.shape[0]
+    tokens = 4 * own_rows
+    chunks = own_rows // CH
+    greet((sib, nbr, diag), rows, r, c)
+
+    first, second = Deal(0, rows, bufs, sems), Deal(1, rows, bufs, sems)
+    first.split(x_ref)
+    second.split(g_ref)
+
+    def vec_row(i):
+        v = vbuf.at[c, r]
+        return remote(v, v, vr_s.at[i], vr_r.at[i], ((r + i) % rows, c))
+
+    def vec_col(i, peer):
+        v = vbuf.at[c]
+        return remote(v, v, vc_s.at[i], vc_r.at[i], (r, peer))
+
+    vbuf[c, r] = vin_ref[...]
+
+    @pl.loop(1, rows)
+    def _(i):
+        vec_row(i).start()
+
+    key_g[...] = place_ref[...].astype(f32)
+    source = order_ref[...] // tokens
+    key_w[...] = (source * tokens + lax.broadcasted_iota(jnp.int32, (1, tokens), 1)).astype(f32)
+    to_col(key_g, col_g)
+    to_col(key_w, col_w)
+    rank_ref[0:1, :] = rank_row(key_g, col_g)
+    rank_ref[1:2, :] = rank_row(key_w, col_w)
+    rank_g = rank_ref[0:1, :]
+    key_w[...] = rank_ref[1:2, :]
+    to_col(key_w, col_w)
+
+    first.joined()
+    first.pick_and_send(rank_g)
+
+    @pl.loop(1, rows)
+    def _(i):
+        vec_row(i).wait_recv()
+
+    for i, peer in enumerate((sib, nbr, diag)):
+        vec_col(i, peer).start()
+
+    second.joined()
+    second.pick_and_send(rank_g)
+
+    for i, peer in enumerate((sib, nbr, diag)):
+        vec_col(i, peer).wait_recv()
+    width, wide = D // (4 * rows), 4 * D // (4 * rows)
+    lane = lax.broadcasted_iota(jnp.int32, (HALF, D), 0)
+    feat = lax.broadcasted_iota(jnp.int32, (HALF, D), 1)
+    everyone = vbuf[:, :, 0, :].reshape(4 * rows, HALF).astype(bf16)
+    mine = vbuf[c][:, 0, :].astype(bf16)
+    owner = lax.broadcasted_iota(jnp.int32, (4 * rows, D), 0) == lax.broadcasted_iota(jnp.int32, (4 * rows, D), 1) // width
+    vec_ref[...] = jnp.zeros_like(vec_ref)
+    for i in range(6):
+        hot = jnp.where(lane - (i + 2) * width == feat % width, 1.0, 0.0).astype(bf16)
+        vec_ref[i : i + 1, :] = jnp.sum(jnp.where(owner, mm(everyone, hot, NN), 0.0), axis=0, keepdims=True)
+    row_owner = lax.broadcasted_iota(jnp.int32, (rows, D), 0)
+    row_feat = lax.broadcasted_iota(jnp.int32, (rows, D), 1)
+    hot = jnp.where(lane - 8 * width == feat % wide, 1.0, 0.0).astype(bf16)
+    bin_ref[...] = jnp.sum(jnp.where(row_owner == row_feat // wide, mm(mine, hot, NN), 0.0), axis=0, keepdims=True)
+    bqv_ref[...] = jnp.zeros_like(bqv_ref)
+    for i in range(2):
+        hot = jnp.where(lane - i * width == feat % width, 1.0, 0.0).astype(bf16)
+        whole = jnp.sum(jnp.where(row_owner == row_feat // width, mm(mine, hot, NN), 0.0), axis=0, keepdims=True)
+        bqv_ref[i : i + 1, :] = whole[:, :FEAT]
+
+    def piece(q, k, half):
+        return tok_ref.at[q, pl.ds(pl.multiple_of(k * CH, CH), CH), half_lanes(half)]
+
+    def tok_copy(qi, q, k, half, s, rr, peer):
+        v = piece(q, k, half)
+        return remote(v, v, s.at[qi, k], rr.at[qi, k], (r, peer))
+
+    ours = ((0, c), (1, nbr))
+    first.shared()
+
+    @pl.loop(0, chunks)
+    def _(k):
+        at = pl.ds(pl.multiple_of(k * CH, CH), CH)
+        for qi, q in ours:
+            rank = col_w[pl.ds(pl.multiple_of(q * own_rows + k * CH, CH), CH), :]
+            tok_ref[q, at, half_lanes(h)] = first.placed(rank).astype(bf16)
+            tok_copy(qi, q, k, h, an_s, an_r, nbr).start()
+            tok_copy(qi, q, k, h, as_s, as_r, sib).start()
+
+    second.shared()
+    rank = col_w[pl.ds(pl.multiple_of(nbr * own_rows, CH), own_rows), :]
+    cot_send[...] = second.placed(rank).astype(bf16)
+    cot_copy = remote(cot_send, cot_ref.at[:, half_lanes(h)], ct_s.at[0], ct_r.at[0], (r, nbr))
+    cot_copy.start()
+    rank = col_w[pl.ds(pl.multiple_of(c * own_rows, CH), own_rows), :]
+    cot_ref[:, half_lanes(h)] = second.placed(rank).astype(bf16)
+
+    @pl.loop(0, chunks)
+    def _(k):
+        for qi, q in ours:
+            tok_copy(1 - qi, q, k, 1 - h, an_s, an_r, nbr).wait_recv()
+            tok_copy(qi, q, k, 1 - h, af_s, af_r, sib).start()
+
+    @pl.loop(0, chunks)
+    def _(k):
+        for qi, q in ours:
+            tok_copy(qi, q, k, h, as_s, as_r, sib).wait_recv()
+            tok_copy(qi, q, k, 1 - h, af_s, af_r, sib).wait_recv()
+            tok_copy(qi, q, k, h, an_s, an_r, nbr).wait_send()
+            tok_copy(qi, q, k, h, as_s, as_r, sib).wait_send()
+            tok_copy(qi, q, k, 1 - h, af_s, af_r, sib).wait_send()
+
+    cot_copy.wait()
+    first.finish()
+    second.finish()
+
+    @pl.loop(1, rows)
+    def _(i):
+        vec_row(i).wait_send()
+
+    for i, peer in enumerate((sib, nbr, diag)):
+        vec_col(i, peer).wait_send()
+
+
+def arrive(rows, x, g, place, order, vin):
+    own_rows = x.shape[0]
+    tokens = 4 * own_rows
+    chunks = own_rows // CH
+    S, V, DS = jax.ShapeDtypeStruct, pltpu.VMEM, pltpu.SemaphoreType.DMA
+    return pl.pallas_call(
+        functools.partial(arrive_body, rows),
+        out_shape=(
+            S((4, own_rows, D), bf16), S((own_rows, D), bf16), S((8, tokens), f32),
+            S((8, D), f32), S((8, FEAT), f32), S((1, D), f32),
+        ),
+        in_specs=[VM] * 5,
+        out_specs=(VM,) * 6,
+        scratch_shapes=deal_scratch(rows, own_rows)
+        + deal_sems(rows)
+        + [
+            V((1, tokens), f32), V((1, tokens), f32), V((tokens, 1), f32), V((tokens, 1), f32),
+            V((own_rows, HALF), bf16), V((4, rows, 8, HALF), f32),
+        ]
+        + [DS((2, chunks))] * 6
+        + [DS((1,))] * 2
+        + [DS((rows,))] * 2
+        + [DS((3,))] * 2,
+        name="arrive",
+        compiler_params=pltpu.CompilerParams(collective_id=1, has_side_effects=True, vmem_limit_bytes=56 << 20),
+        cost_estimate=pl.CostEstimate(flops=60_000_000_000, bytes_accessed=20_000_000, transcendentals=0),
+    )(x, g, place, order, vin)
+
+
+def ring_spot(row, rows):
+    return jnp.where(row % 2 == 0, row // 2, rows - 1 - row // 2)
+
+
+def ring_row(spot, rows):
+    spot = (spot + rows) % rows
+    return jnp.where(spot < rows // 2, 2 * spot, 2 * (rows - 1 - spot) + 1)
+
+
+class Ring:
+    def __init__(self, rows, own, sbuf, rbuf, sems):
+        self.rows, self.hops = rows, rows // 2
+        self.own = own
+        self.sbuf, self.rbuf = sbuf, rbuf
+        self.send, self.recv = sems
+        self.r, self.c = lax.axis_index("row"), lax.axis_index("col")
+        self.spot = ring_spot(self.r, rows)
+
+    def copy(self, way, t):
+        to = ring_row(self.spot + (1 if way == 0 else self.rows - 1), self.rows)
+        return remote(
+            self.sbuf.at[way, t], self.rbuf.at[way, t], self.send.at[way, t], self.recv.at[way, t], (to, self.c)
+        )
+
+    def block(self, way, t):
+        if way == 0:
+            return ring_row(self.spot + self.hops - t, self.rows)
+        return ring_row(self.spot + self.rows - (self.hops - 1) + t, self.rows)
+
+    def start(self):
+        for way in range(2 if self.hops > 1 else 1):
+            self.sbuf[way, 0] = self.own(self.block(way, 0)).astype(bf16)
+            self.copy(way, 0).start()
+
+    def hop(self, t):
+        for way in range(2):
+            if t < self.hops - way:
+                self.copy(way, t - 1).wait_recv()
+                total = self.own(self.block(way, t)) + self.rbuf[way, t - 1].astype(f32)
+                self.sbuf[way, t] = total.astype(bf16)
+                self.copy(way, t).start()
+
+    def result(self):
+        self.copy(0, self.hops - 1).wait_recv()
+        total = self.own(self.r) + self.rbuf[0, self.hops - 1].astype(f32)
+        if self.hops > 1:
+            self.copy(1, self.hops - 2).wait_recv()
+            total = total + self.rbuf[1, self.hops - 2].astype(f32)
+        return total
+
+    def finish(self):
+        for way in range(2):
+            for t in range(self.hops - way):
+                self.copy(way, t).wait_send()
+
+
+def depart_body(
+    rows, out_in, g1_ref, dqkv_ref, w_ref, tok_ref, rank_ref, dwo_ref, dwin_ref, dwout_ref, dvec_ref, dbin_ref,
+    out_ref, grad_ref, gw_ref, gff_ref, gvec_ref, gwide_ref,
+    *scratch,
+):
+    bufs, sems = scratch[:4], scratch[4:14]
+    key, col_g, sums, dw = scratch[14:18]
+    d2ds, d2dr, keep, xs, xr, gsend, grecv, r1s, r1r, r2s, r2r, vmine, vall, vrow = scratch[18:32]
+    ds_s, ds_r, x_s, x_r, fin_s, fin_r, q1_s, q1_r, q2_s, q2_r, vc_s, vc_r, vr_s, vr_r = scratch[32:]
+    r, c, sib, nbr, diag = col_peers()
+    h = c // 2
+    own_rows = out_in.shape[0]
+    tokens = 4 * own_rows
+    chunks = own_rows // CH
+    block = D // rows
+    greet((sib, nbr, diag), rows, r, c)
+
+    def rows_of(k):
+        return pl.ds(pl.multiple_of(k * CH, CH), CH)
+
+    outs, grads = Deal(0, rows, bufs, sems), Deal(1, rows, bufs, sems)
+    outs.split(out_in)
+    ring_ff = Ring(
+        rows, lambda b: jnp.concatenate([dwin_ref[b], dwout_ref[b]], axis=1), r1s, r1r, (q1_s, q1_r)
+    )
+    ring_at = Ring(
+        rows, lambda b: jnp.concatenate([dw[b], dwo_ref[b]], axis=1), r2s, r2r, (q2_s, q2_r)
+    )
+    ring_ff.start()
+
+    vmine[...] = jnp.zeros_like(vmine)
+    vmine[0:8, :] = dvec_ref[...]
+
+    def vec_col(i, peer):
+        return remote(vmine, vall.at[c], vc_s.at[i], vc_r.at[i], (r, peer))
+
+    for i, peer in enumerate((sib, nbr, diag)):
+        vec_col(i, peer).start()
+
+    def d2d(k):
+        return remote(d2ds.at[k], d2dr.at[k], ds_s.at[k], ds_r.at[k], (r, sib))
+
+    def xcopy(k):
+        return remote(xs.at[k], xr.at[k], x_s.at[k], x_r.at[k], (r, nbr))
+
+    def part(q, k):
+        return mm(dqkv_ref[pl.ds(pl.multiple_of(q * own_rows + k * CH, CH), CH), :], w_ref[...], NT)
+
+    @pl.loop(0, chunks)
+    def _(k):
+        d2ds[k, 0] = part(sib, k).astype(bf16)
+        d2ds[k, 1] = part(diag, k).astype(bf16)
+        d2d(k).start()
+        for i, q in ((0, c), (1, nbr)):
+            keep[k, i] = part(q, k)
+
+    @pl.loop(0, chunks)
+    def _(k):
+        d2d(k).wait_recv()
+        for i in range(2):
+            keep[k, i] = keep[k, i] + d2dr[k, i].astype(f32)
+            xs[k, 1 - i] = keep[k, i, :, half_lanes(1 - h)].astype(bf16)
+        xcopy(k).start()
+
+    key[...] = rank_ref[0:1, :]
+    to_col(key, col_g)
+    rank_w = rank_ref[1:2, :]
+    outs.joined()
+    outs.pick_and_send(rank_w)
+
+    whole = mm(tok_ref[...].reshape(tokens, D), dqkv_ref[...], TN)
+    for b in range(rows):
+        dw[b] = whole[b * block : (b + 1) * block]
+    sums[...] = jnp.zeros_like(sums)
+
+    @pl.loop(0, tokens // QB)
+    def _(k):
+        part_rows = dqkv_ref[pl.ds(pl.multiple_of(k * QB, QB), QB), :].astype(f32)
+        sums[0:1, :] += jnp.sum(part_rows, axis=0, keepdims=True)
+
+    ring_ff.hop(1)
+
+    @pl.loop(0, chunks)
+    def _(k):
+        xcopy(k).wait_recv()
+        for i, q in ((0, c), (1, nbr)):
+            total = keep[k, i, :, half_lanes(h)] + xr[k, i].astype(f32) + g1_ref[q, rows_of(k), half_lanes(h)].astype(f32)
+            grads.xin[1, q, rows_of(k), :] = total.astype(bf16)
+
+    shares = [
+        remote(grads.xin.at[1, q], grads.xin.at[1, q], s.at[1], rr.at[1], (r, sib))
+        for q, s, rr in ((c, grads.sib_s, grads.sib_r), (nbr, grads.fwd_s, grads.fwd_r))
+    ]
+    for copy in shares:
+        copy.start()
+    for copy in shares:
+        copy.wait_recv()
+    grads.pick_and_send(rank_w)
+    ring_at.start()
+
+    for i, peer in enumerate((sib, nbr, diag)):
+        vec_col(i, peer).wait_recv()
+    total = vmine[...] + vall[sib] + vall[nbr] + vall[diag]
+    vrow[r, 0:8, :] = total[0:8, :]
+    vrow[r, 8:9, :] = dbin_ref[...]
+    vrow[r, 9:10, :] = jnp.concatenate([sums[0:1, :], jnp.zeros((1, FEAT), f32)], axis=1)
+
+    def vec_row(i):
+        v = vrow.at[r]
+        return remote(v, v, vr_s.at[i], vr_r.at[i], ((r + i) % rows, c))
+
+    @pl.loop(1, rows)
+    def _(i):
+        vec_row(i).start()
+
+    for t in range(2, rows // 2):
+        ring_ff.hop(t)
+    gff_ref[...] = ring_ff.result()
+    for t in range(1, rows // 2):
+        ring_at.hop(t)
+    gw_ref[...] = ring_at.result()
+
+    outs.shared()
+
+    def final(deal, i):
+        rank = col_g[pl.ds(pl.multiple_of(nbr * own_rows, CH), own_rows), :]
+        gsend[i] = deal.placed(rank).astype(bf16)
+        return remote(gsend.at[i], grecv.at[i], fin_s.at[i], fin_r.at[i], (r, nbr))
+
+    def own_half(deal, ref):
+        rank = col_g[pl.ds(pl.multiple_of(c * own_rows, CH), own_rows), :]
+        ref[:, half_lanes(h)] = deal.placed(rank)
+
+    out_copy = final(outs, 0)
+    out_copy.start()
+    own_half(outs, out_ref)
+    grads.shared()
+    grad_copy = final(grads, 1)
+    grad_copy.start()
+    own_half(grads, grad_ref)
+
+    @pl.loop(1, rows)
+    def _(i):
+        vec_row(i).wait_recv()
+
+    total = vrow[0]
+    for i in range(1, rows):
+        total = total + vrow[i]
+    width, wide = D // (4 * rows), 4 * D // (4 * rows)
+    spots = lax.broadcasted_iota(jnp.int32, (D, 128), 0)
+    outs_at = lax.broadcasted_iota(jnp.int32, (D, 128), 1)
+
+    def chosen(values, first, size):
+        hot = jnp.where((spots - first == outs_at) & (outs_at < size), 1.0, 0.0)
+        return lax.dot_general(values, hot, NN, precision=lax.Precision.HIGHEST, preferred_element_type=f32)
+
+    gvec_ref[0:8, :] = chosen(total[0:8, :], (c * rows + r) * width, width)
+    gwide_ref[0:1, :] = chosen(total[8:16, :], r * wide, wide)[0:1, :]
+    gwide_ref[1:2, :] = chosen(total[8:16, :], r * width, width)[1:2, :]
+    gwide_ref[2:3, :] = chosen(total[8:16, :], 2 * FEAT + r * width, width)[1:2, :]
+
+    out_copy.wait_recv()
+    out_ref[:, half_lanes(1 - h)] = grecv[0].astype(f32)
+    grad_copy.wait_recv()
+    grad_ref[:, half_lanes(1 - h)] = grecv[1].astype(f32)
+
+    out_copy.wait_send()
+    grad_copy.wait_send()
+    outs.finish()
+    for copy in shares:
+        copy.wait_send()
+
+    @pl.loop(1, rows)
+    def _(i):
+        grads.row_copy(i).wait_send()
+
+    @pl.loop(0, rows)
+    def _(i):
+        grads.share(i).wait_send()
+
+    @pl.loop(0, chunks)
+    def _(k):
+        d2d(k).wait_send()
+        xcopy(k).wait_send()
+
+    ring_ff.finish()
+    ring_at.finish()
+    for i, peer in enumerate((sib, nbr, diag)):
+        vec_col(i, peer).wait_send()
+
+    @pl.loop(1, rows)
+    def _(i):
+        vec_row(i).wait_send()
+
+
+def depart(rows, out, g1, dqkv, w_qkv, tok, rank, dwo, dwin, dwout, dvec, dbin):
+    own_rows = out.shape[0]
+    tokens = 4 * own_rows
+    chunks = own_rows // CH
+    block, hops = D // rows, rows // 2
+    S, V, DS = jax.ShapeDtypeStruct, pltpu.VMEM, pltpu.SemaphoreType.DMA
+    return pl.pallas_call(
+        functools.partial(depart_body, rows),
+        out_shape=(
+            S((own_rows, D), f32), S((own_rows, D), f32), S((block, D), f32), S((block, 2 * D), f32),
+            S((8, 128), f32), S((8, 128), f32),
+        ),
+        in_specs=[VM] * 11,
+        out_specs=(VM,) * 6,
+        scratch_shapes=deal_scratch(rows, own_rows)
+        + deal_sems(rows)
+        + [V((1, tokens), f32), V((tokens, 1), f32), V((8, 3 * FEAT), f32), V((rows, block, 3 * FEAT), f32)]
+        + [
+            V((chunks, 2, CH, D), bf16), V((chunks, 2, CH, D), bf16), V((chunks, 2, CH, D), f32),
+            V((chunks, 2, CH, HALF), bf16), V((chunks, 2, CH, HALF), bf16),
+            V((2, own_rows, HALF), bf16), V((2, own_rows, HALF), bf16),
+            V((2, hops, block, 2 * D), bf16), V((2, hops, block, 2 * D), bf16),
+            V((2, hops, block, D), bf16), V((2, hops, block, D), bf16),
+            V((16, D), f32), V((4, 16, D), f32), V((rows, 16, D), f32),
+        ]
+        + [DS((chunks,))] * 4
+        + [DS((2,))] * 2
+        + [DS((2, hops))] * 4
+        + [DS((3,))] * 2
+        + [DS((rows,))] * 2,
+        name="depart",
+        compiler_params=pltpu.CompilerParams(collective_id=3, has_side_effects=True, vmem_limit_bytes=60 << 20),
+        cost_estimate=pl.CostEstimate(flops=60_000_000_000, bytes_accessed=20_000_000, transcendentals=0),
+    )(out, g1, dqkv, w_qkv, tok, rank, dwo, dwin, dwout, dvec, dbin)
 
 
 def per_device(
@@ -423,31 +1029,18 @@
 ):
     rows = lax.axis_size("row")
     col = lax.axis_index("col")
-    given = lax.all_to_all(inputs.astype(bf16), "col", split_axis=1, concat_axis=0, tiled=True)
-    given_g = lax.all_to_all(cotangent.astype(bf16), "col", split_axis=1, concat_axis=0, tiled=True)
-    tok_rows = given.shape[0]
-    send_order = jnp.argsort(token_place // tok_rows, stable=True)
-    arrive_order = jnp.argsort(token_order, stable=True)
-    got = lax.all_to_all(given[send_order], "row", split_axis=0, concat_axis=0, tiled=True)
-    got_g = lax.all_to_all(given_g[send_order], "row", split_axis=0, concat_axis=0, tiled=True)
-    dealt = jnp.zeros_like(got).at[arrive_order].set(got)
-    dealt_g = jnp.zeros_like(got_g).at[arrive_order].set(got_g)
-    own_rows = tok_rows // 4
+    own_rows = inputs.shape[0]
+    tok_rows = 4 * own_rows
 
     pack = jnp.concatenate(
         [query_weight, key_weight, value_weight, output_weight.T, inner_weight, outer_weight.T], axis=1
     )
     pack = lax.all_gather(pack, "row", axis=0, tiled=True)
     w_qkv, wo, win, wout = pack[:, :576], pack[:, 576:768], pack[:, 768:1536], pack[:, 1536:]
-    vecs = jnp.concatenate(
+    vin = jnp.concatenate(
         [query_bias, value_bias, output_bias, first_gain, first_shift, outer_bias, second_gain, second_shift, inner_bias]
-    )[None]
-    vecs = lax.all_gather(vecs, "row", axis=0, tiled=True)
-    small = query_bias.shape[0]
-    mine = vecs[:, : 8 * small].reshape(rows, 8, small).transpose(1, 0, 2).reshape(8, FEAT)
-    b_in = vecs[:, 8 * small :].reshape(1, D).astype(f32)
-    full = lax.all_gather(mine[2:], "col", axis=1, tiled=True).astype(f32)
-    vec = jnp.concatenate([full, jnp.zeros((2, D), f32)], axis=0)
+    ).astype(f32)
+    vin = jnp.broadcast_to(jnp.pad(vin, (0, HALF - vin.shape[0]))[None], (8, HALF))
 
     seq_ends = jnp.cumsum(seq_lengths[0])
     seq_starts = seq_ends - seq_lengths[0]
@@ -460,49 +1053,24 @@
     hi = (end[QB - 1 :: QB] + KB - 1) // KB
     start, end = start[None], end[None]
 
-    tokens = lax.all_gather(dealt, "col", axis=1, tiled=True)
-    cot = lax.all_to_all(dealt_g, "col", split_axis=0, concat_axis=1, tiled=True)
-    qkv = jnp.dot(tokens, w_qkv, preferred_element_type=f32)
-    q = (qkv[:, :192] + mine[0].astype(f32)).astype(bf16)
-    k = qkv[:, 192:384].astype(bf16)
-    v = (qkv[:, 384:] + mine[1].astype(f32)).astype(bf16)
-    mixed, lse = attend_fwd(lo, hi, start, end, q, k, v)
-    own_tok = lax.dynamic_slice_in_dim(tokens, col * own_rows, own_rows, axis=0)
+    tok, cot, rank, vec, bqv, b_in = arrive(rows, inputs, cotangent, token_place[None], token_order[None], vin)
+    q, k, v, mixed, lse = attend_fwd(lo, hi, start, end, tok.reshape(tok_rows, D), w_qkv, bqv)
+    own_tok = lax.dynamic_index_in_dim(tok, col, axis=0, keepdims=False)
     out, g1, gmix, dwo, dwin, dwout, dvec, dbin = middle(
         mixed.reshape(4, own_rows, FEAT), own_tok, cot, wo, win, wout, vec, b_in
     )
-    dq, dk, dv = attend_bwd(lo, hi, start, end, q, k, v, gmix.reshape(tok_rows, FEAT), lse)
-    dqkv = jnp.concatenate([dq, dk, dv], axis=1)
-    dw_qkv = lax.dot_general(tokens, dqkv, TN, preferred_element_type=f32)
-    db_q = jnp.sum(dq.astype(f32), axis=0)
-    db_v = jnp.sum(dv.astype(f32), axis=0)
-    back = lax.dot_general(dqkv, w_qkv, NT, preferred_element_type=f32).astype(bf16)
-    grad_tok = lax.psum_scatter(back, "col", scatter_dimension=1, tiled=True).astype(f32)
-    g1_cols = lax.dynamic_slice_in_dim(g1.reshape(tok_rows, D), col * FEAT, FEAT, axis=1)
-    grad_tok = (grad_tok + g1_cols.astype(f32)).astype(bf16)
-
-    dpack = jnp.concatenate([dw_qkv.astype(bf16), dwo.astype(bf16), dwin.astype(bf16), dwout.astype(bf16)], axis=1)
-    dpack = sent_and_summed(dpack, 0)
-    dmine = lax.psum_scatter(dvec[1:7], "col", scatter_dimension=1, tiled=True)
-    dmine = jnp.concatenate([db_q[None], db_v[None], dmine], axis=0)
-    dmine = dmine.reshape(8, rows, small).transpose(1, 0, 2).reshape(rows, 8 * small)
-    dall = jnp.concatenate([dmine, dbin.reshape(rows, -1)], axis=1)
-    dsum = jnp.sum(lax.all_to_all(dall, "row", 0, 0, tiled=True), axis=0)
-    dv8 = dsum[: 8 * small].reshape(8, small)
-
-    share = lax.all_to_all(out, "col", split_axis=1, concat_axis=0, tiled=True)
-
-    def send_back(value):
-        got_back = lax.all_to_all(value[arrive_order], "row", split_axis=0, concat_axis=0, tiled=True)
-        placed = jnp.zeros_like(got_back).at[send_order].set(got_back)
-        return lax.all_to_all(placed, "col", split_axis=0, concat_axis=1, tiled=True).astype(f32)
-
-    output, input_grad = send_back(share), send_back(grad_tok)
+    dqkv = attend_bwd(lo, hi, start, end, q, k, v, gmix.reshape(tok_rows, FEAT), lse)
+    output, input_grad, gw, gff, gvec, gwide = depart(
+        rows, out, g1, dqkv, w_qkv, tok, rank,
+        dwo.reshape(rows, -1, FEAT), dwin.reshape(rows, -1, D), dwout.reshape(rows, -1, D), dvec, dbin,
+    )
+    small, wide = query_bias.shape[0], inner_bias.shape[0]
     return (
         output, input_grad,
-        dpack[:, :192], dpack[:, 192:384], dpack[:, 384:576], dpack[:, 576:768].T,
-        dpack[:, 768:1536], dpack[:, 1536:].T,
-        dv8[0], dv8[1], dv8[2], dsum[8 * small :], dv8[3], dv8[4], dv8[5], dv8[6], dv8[7],
+        gw[:, :192], gw[:, 192:384], gw[:, 384:576], gw[:, 576:].T,
+        gff[:, :D], gff[:, D:].T,
+        gwide[1, :small], gwide[2, :small], gvec[1, :small], gwide[0, :wide],
+        gvec[2, :small], gvec[3, :small], gvec[4, :small], gvec[5, :small], gvec[6, :small],
     )
 
 

time: 632 us -> 440 us (0.70); the launches traced: 623 us -> 440 us
  Pallas kernels: 168 us -> 393 us
  waiting for transfers between devices: 129 us -> 0.51 us
  local copies, waits for them, and re-layouts: 148 us -> 29.8 us
  blocking collectives: 74.1 us -> 0 us
  starting transfers between devices: 48 us -> 0.04 us
  other arithmetic: 25.2 us -> 2.22 us
  matrix products: 15 us -> 0 us
    pallas_call x2 -> x4, Pallas kernels: 51.8 us -> 275 us  [the longest x1 143 us: depart(): pl.pallas_call(functools.partial(depart_body, rows), out_shape=(S((own_ro...]
    all_to_all x10 -> x0, waiting for transfers between devices: 129 us -> none  [the longest x1 57.5 us: sent_and_summed(): lax.all_to_all(pieces, 'row', 0, 0, tiled=True).astype(f32)]
    all_to_all x10 -> x0, starting transfers between devices: 47.7 us -> none  [the longest x2 14.3 us: send_back(): lax.all_to_all(value[arrive_order], 'row', split_axis=0, concat_axis=0, t...]
    scatter x5 -> x0, local copies, waits for them, and re-layouts: 41.3 us -> none  [the longest x2 20.6 us: send_back(): placed = jnp.zeros_like(got_back).at[send_order].set(got_back)]
    all_to_all x2 -> x0, blocking collectives: 37.1 us -> none  [the longest x1 21.9 us: per_device(): lax.all_to_all(cotangent.astype(bf16), 'col', split_axis=1, concat_axis=0...]
    gather x4 -> x0, local copies, waits for them, and re-layouts: 33.1 us -> none  [the longest x2 18.1 us: send_back(): value[arrive_order]]
    unnamed x1 -> x0, blocking collectives: 25.9 us -> none
    all_to_all x16 -> x0, local copies, waits for them, and re-layouts: 21.3 us -> none  [the longest x4 8.02 us: send_back(): lax.all_to_all(value[arrive_order], 'row', split_axis=0, concat_axis=0, t...]
  transfers between devices with their start and end apart: 14 -> 1, of which waited for: 6 -> 1; matrix products, arithmetic and copies ran while one was open for 26% -> 3% of each run, Pallas kernels for 5% -> 19%
where the time goes in v2:
time: 440 us
  Pallas kernels  393 us (89%)
  local copies, waits for them, and re-layouts  29.8 us (7%)
  between operations  14.4 us (3%)
    pallas_call x1, Pallas kernels, depart(): pl.pallas_call(functools.partial(depart_body, rows), out_shape=(S((own_ro...  143 us
    pallas_call x1, Pallas kernels, middle(): pl.pallas_call(middle_body, out_shape=(S((own_rows, D), bf16), S((4, own_...  118 us
    pallas_call x1, Pallas kernels, arrive(): pl.pallas_call(functools.partial(arrive_body, rows), out_shape=(S((4, own...  82.8 us
    pallas_call x1, Pallas kernels, attend_bwd(): pl.pallas_call(attend_bwd_body, out_shape=jax.ShapeDtypeStruct((rows, 3 *...  26.9 us
    pallas_call x1, Pallas kernels, attend_fwd(): pl.pallas_call(attend_fwd_body, out_shape=(part, part, part, part, jax.Sh...  22.5 us
  transfers between devices with their start and end apart: 1, of which 1 were waited for; matrix products, arithmetic and copies ran while one was open for 3% of the time, Pallas kernels for 19%

profile of v2, /device:TPU:0, one launch (start us, length us, event | category | flops | bytes accessed | tf_op | source)
XLA Modules:
  0.0 440.2 jit_solution(8285742412469256497)
XLA Ops:
  7.2 0.9 copy.39
  8.1 1.9 concatenate.7
  10.1 0.8 reduce-window.4
  10.9 0.7 fusion
  11.6 0.1 convert_reduce_fusion
  11.7 0.1 select_reduce_fusion
  11.8 0.1 slice.64
  11.9 0.1 slice.63
  12.0 6.1 %concatenate.6 = bf16[288]{0:T(512)(128)(2,1)S(1)} concatenate(bf16[24]{0:T(256)(128)(2,1)} %param.31, bf16[24]{0:T(256)(128)(2,1)} %param.32, bf16[24]{0:T(256)(128)(2,1)} %param.33, bf16[24]{0:T(256)(128)(2,1)} %param.36, bf16[24]{0:T(256)(128)(2,1)} %param.37, bf16[24]{0:T(256)(128)(2,1)} %param.35, bf16[24]{0:T(256)(128)(2,1)} %param.38, bf16[24]{0:T(256)(128)(2,1)} %param.39, ...), dimensions={0} | concatenate | bytes 1152 | tf_op jit(solution)/shard_map/concatenate | solution.py:1040
  18.1 0.6 broadcast_in_dim.28.vin_ref
  18.7 82.8 %arrive.1 = (bf16[4,512,768]{2,1,0:T(8,128)(2,1)}, bf16[512,768]{1,0:T(8,128)(2,1)}, f32[8,2048]{1,0:T(8,128)}, f32[8,768]{1,0:T(8,128)}, f32[8,192]{1,0:T(8,128)}, /*index=5*/f32[1,768]{1,0:T(1,128)}) custom-call(f32[512,768]{1,0:T(8,128)} %x_ref.1, f32[512,768]{1,0:T(8,128)} %g_ref.1, s32[1,2048]{1,0:T(1,128)} %bitcast.55, s32[1,2048]{1,0:T(1,128)} %bitcast.56, ...), custom_call_target="tpu_custom_call" | custom-call | flops 60000002048 | bytes 20000000 | tf_op jit(solution)/shard_map/arrive/pallas_call | solution.py:713
  101.6 2.3 dynamic-slice_bitcast_fusion.tok_ref
  103.8 0.5 and_select_fusion
  104.4 0.5 all-gather.2.cloned.1.call-done
  104.9 1.3 slice.84.w_ref
  106.3 0.7 copy-done.22
  107.0 22.5 %attend_fwd.1 = (bf16[2048,192]{1,0:T(8,128)(2,1)S(1)}, bf16[2048,192]{1,0:T(8,128)(2,1)S(1)}, bf16[2048,192]{1,0:T(8,128)(2,1)S(1)}, bf16[2048,192]{1,0:T(8,128)(2,1)S(1)}, f32[8,2048]{1,0:T(8,128)S(1)}) custom-call(s32[8]{0:T(128)S(1)} %copy-done.10, s32[8]{0:T(128)S(1)} %copy-done.8, s32[1,2048]{1,0:T(1,128)S(1)} %bitcast.47, s32[1,2048]{1,0:T(1,128)S(1)} %bitcast.45, ...), custom_call_target="tpu_custom_call" | custom-call | flops 8000000000 | bytes 8000000 | tf_op jit(solution)/shard_map/attend_fwd/pallas_call | solution.py:106
  129.6 1.1 slice.85.wo_ref
  130.7 1.7 fusion.1
  132.5 118.1 %middle.1 = (bf16[512,768]{1,0:T(8,128)(2,1)}, bf16[4,512,768]{2,1,0:T(8,128)(2,1)}, bf16[4,512,192]{2,1,0:T(8,128)(2,1)}, f32[768,192]{1,0:T(8,128)}, f32[768,7...) custom-call(bf16[4,512,192]{2,1,0:T(8,128)(2,1)} %bitcast.50, ...), custom_call_target="tpu_custom_call" | custom-call | flops 80000000000 | bytes 20000000 | tf_op jit(solution)/shard_map/middle/pallas_call | solution.py:387
  250.7 1.2 copy-done.12
  251.9 26.9 %attend_bwd.1.dqkv_ref = bf16[2048,576]{1,0:T(8,128)(2,1)} custom-call(s32[8]{0:T(128)S(1)} %copy-done.11, s32[8]{0:T(128)S(1)} %copy-done.9, s32[1,2048]{1,0:T(1,128)S(1)} %bitcast.48, s32[1,2048]{1,0:T(1,128)S(1)} %bitcast.46, bf16[2048,192]{1,0:T(8,128)(2,1)S(1)} %copy-done.15, bf16[2048,192]{1,0:T(8,128)(2,1)S(1)} %copy-done.17, ...), custom_call_target="tpu_custom_call" | custom-call | flops 20000000000 | bytes 6000000 | tf_op jit(solution)/shard_map/attend_bwd/pallas_call | solution.py:183
  278.8 143.0 %depart.1 = (f32[512,768]{1,0:T(8,128)}, f32[512,768]{1,0:T(8,128)}, f32[96,768]{1,0:T(8,128)}, f32[96,1536]{1,0:T(8,128)}, f32[8,128]{1,0:T(8,128)}, /*index=5*/f32[8,128]{1,0:T(8,128)}) custom-call(bf16[512,768]{1,0:T(8,128)(2,1)} %get-tuple-element.48.out_in, bf16[4,512,768]{2,1,0:T(8,128)(2,1)} %get-tuple-element.49.g1_ref, ...), custom_call_target="tpu_custom_call" | custom-call | flops 60000002048 | bytes 20000000 | tf_op jit(solution)/shard_map/depart/pallas_call | solution.py:994
  421.8 1.3 slice_bitcast_fusion.7
  423.1 1.3 slice_bitcast_fusion.9
  424.3 1.4 slice_bitcast_fusion.2
  425.8 1.8 slice_bitcast_fusion.1
  427.6 0.7 copy.40
  428.4 1.9 slice_bitcast_fusion
  430.3 1.1 copy.43
  431.4 0.8 copy-done.24
  432.2 1.1 copy.44
  (52 shorter events, 0.2 us)
Async XLA Ops:
  7.2 97.7 %all-gather.2.cloned.1.call-start = ((), (), s32[]{:S(2)}) async-start(), calls=%async_computation | async-start | bytes 3981312 | tf_op jit(solution)/shard_map/all_gather | solution.py:1038
  11.8 89.7 %copy-start.2 = (s32[2048]{0:T(1024)}, s32[2048]{0:T(1024)S(1)}, u32[]{:S(2)}) copy-start(s32[2048]{0:T(1024)S(1)} %get-tuple-element.101) | copy-start | bytes 24580
  11.8 89.7 %copy-start.5 = (s32[2048]{0:T(1024)}, s32[2048]{0:T(1024)S(1)}, u32[]{:S(2)}) copy-start(s32[2048]{0:T(1024)S(1)} %get-tuple-element.102) | copy-start | bytes 24580
  101.6 4.6 %copy-start.1 = (bf16[4,512,768]{2,1,0:T(8,128)(2,1)S(1)}, bf16[4,512,768]{2,1,0:T(8,128)(2,1)}, u32[]{:S(2)}) copy-start(bf16[4,512,768]{2,1,0:T(8,128)(2,1)} %get-tuple-element.42.tok_ref) | copy-start | bytes 9437188
  104.8 1.4 copy-start.3
  104.9 1.4 copy-start.6
  104.9 1.4 copy-start.8
  104.9 1.4 copy-start.10
  106.2 23.3 %copy-start = (bf16[768,576]{1,0:T(8,128)(2,1)}, bf16[768,576]{1,0:T(8,128)(2,1)S(1)}, u32[]{:S(2)}) copy-start(bf16[768,576]{1,0:T(8,128)(2,1)S(1)} %slice.84.w_ref) | copy-start | bytes 2654212
  106.3 0.7 copy-start.22
  107.0 22.5 %copy-start.23 = (bf16[768,2304]{1,0:T(8,128)(2,1)S(1)}, bf16[768,2304]{1,0:T(8,128)(2,1)}, u32[]{:S(2)}) copy-start(bf16[768,2304]{1,0:T(8,128)(2,1)} %all-gather.2.cloned.1.call-done) | copy-start | bytes 10616836
  129.5 2.9 copy-start.13
  129.5 2.9 copy-start.14
  129.5 2.9 copy-start.16
  129.6 2.9 copy-start.18
  129.6 2.9 copy-start.20
  132.4 118.2 %copy-start.4 = (s32[2048]{0:T(1024)S(1)}, s32[2048]{0:T(1024)}, u32[]{:S(2)}) copy-start(s32[2048]{0:T(1024)} %copy-done.2) | copy-start | bytes 24580
  132.5 118.2 %copy-start.7 = (s32[2048]{0:T(1024)S(1)}, s32[2048]{0:T(1024)}, u32[]{:S(2)}) copy-start(s32[2048]{0:T(1024)} %copy-done.5) | copy-start | bytes 24580
  132.5 118.2 %copy-start.9 = (s32[8]{0:T(128)S(1)}, s32[8]{0:T(128)}, u32[]{:S(2)}) copy-start(s32[8]{0:T(128)} %get-tuple-element.119.hi_ref) | copy-start | bytes 100
  132.5 118.2 %copy-start.11 = (s32[8]{0:T(128)S(1)}, s32[8]{0:T(128)}, u32[]{:S(2)}) copy-start(s32[8]{0:T(128)} %get-tuple-element.120.lo_ref) | copy-start | bytes 100
  132.5 118.2 %copy-start.15 = (bf16[2048,192]{1,0:T(8,128)(2,1)S(1)}, bf16[2048,192]{1,0:T(8,128)(2,1)}, u32[]{:S(2)}) copy-start(bf16[2048,192]{1,0:T(8,128)(2,1)} %copy-done.14) | copy-start | bytes 2359300
  132.5 118.2 %copy-start.17 = (bf16[2048,192]{1,0:T(8,128)(2,1)S(1)}, bf16[2048,192]{1,0:T(8,128)(2,1)}, u32[]{:S(2)}) copy-start(bf16[2048,192]{1,0:T(8,128)(2,1)} %copy-done.16) | copy-start | bytes 2359300
  132.5 118.2 %copy-start.19 = (bf16[2048,192]{1,0:T(8,128)(2,1)S(1)}, bf16[2048,192]{1,0:T(8,128)(2,1)}, u32[]{:S(2)}) copy-start(bf16[2048,192]{1,0:T(8,128)(2,1)} %copy-done.18) | copy-start | bytes 2359300
  132.5 118.2 %copy-start.21 = (f32[8,2048]{1,0:T(8,128)S(1)}, f32[8,2048]{1,0:T(8,128)}, u32[]{:S(2)}) copy-start(f32[8,2048]{1,0:T(8,128)} %copy-done.20) | copy-start | bytes 196612
  250.7 1.2 copy-start.12
  421.8 8.5 %copy-start.25 = (f32[512,768]{1,0:T(8,128)S(1)}, f32[512,768]{1,0:T(8,128)}, u32[]{:S(2)}) copy-start(f32[512,768]{1,0:T(8,128)} %get-tuple-element.138) | copy-start | bytes 4718596
  430.3 2.0 copy-start.24
Sparse Core Ops, SparseCore 0:
  10.8 94.0 all-gather.1

commit v3 on v2

--- a/solution.py
+++ b/solution.py
@@ -229,197 +229,6 @@
 CH = 128
 
 
-def middle_body(
-    mixed_ref, tok_ref, cot_ref, wo_ref, win_ref, wout_ref, vec_ref, bin_ref,
-    out_ref, g1_ref, gmix_ref, dwo_ref, dwin_ref, dwout_ref, dvec_ref, dbin_ref,
-    nfull, hidden, slope, g2full, own, d2ds, d2dr, xs, xr, normed, hat1, inv1, grad2,
-    ds_s, ds_r, x_s, x_r, asib_s, asib_r, anbr_s, anbr_r, afwd_s, afwd_r,
-):
-    r, c, sib, nbr, diag = col_peers()
-    chunks = tok_ref.shape[0] // CH
-
-    barrier = pltpu.get_barrier_semaphore()
-    for peer in (sib, nbr):
-        pl.semaphore_signal(barrier, inc=1, device_id=(r, peer), device_id_type=MESH)
-    pl.semaphore_wait(barrier, 2)
-
-    bo, g1, s1, b2, g2, s2 = [vec_ref[pl.ds(i, 1), :] for i in range(6)]
-
-    def d2d(st, k):
-        return remote(d2ds.at[st, k], d2dr.at[st, k], ds_s.at[st, k], ds_r.at[st, k], (r, sib))
-
-    def xcopy(st, k):
-        return remote(xs.at[st, k], xr.at[st, k], x_s.at[st, k], x_r.at[st, k], (r, nbr))
-
-    def rs_start(st, k, part):
-        d2ds[st, k, 0] = part(sib).astype(bf16)
-        d2ds[st, k, 1] = part(diag).astype(bf16)
-        d2d(st, k).start()
-        mine = part(c)
-        other = part(nbr)
-        d2d(st, k).wait_recv()
-        xs[st, k] = (other + d2dr[st, k, 1].astype(f32)).astype(bf16)
-        xcopy(st, k).start()
-        own[st, k] = mine + d2dr[st, k, 0].astype(f32)
-
-    def rs_end(st, k):
-        xcopy(st, k).wait_recv()
-        return own[st, k] + xr[st, k].astype(f32)
-
-    gathered = (nfull, g2full, g1_ref)
-
-    def piece(st, q, k):
-        return gathered[st].at[q, pl.ds(pl.multiple_of(k * CH, CH), CH), :]
-
-    def ag_copy(st, k, q, sems, target):
-        return remote(piece(st, q, k), piece(st, q, k), sems[0].at[st, k], sems[1].at[st, k], (r, target))
-
-    to_sib = functools.partial(ag_copy, sems=(asib_s, asib_r), target=sib)
-    to_nbr = functools.partial(ag_copy, sems=(anbr_s, anbr_r), target=nbr)
-    fwd = functools.partial(ag_copy, sems=(afwd_s, afwd_r), target=sib)
-
-    def ag_start(st, k, value):
-        gathered[st][c, pl.ds(pl.multiple_of(k * CH, CH), CH), :] = value
-        to_nbr(st, k, c).start()
-        to_sib(st, k, c).start()
-
-    def ag_end(st, k):
-        to_nbr(st, k, c).wait_recv()
-        fwd(st, k, nbr).start()
-        to_sib(st, k, c).wait_recv()
-        fwd(st, k, nbr).wait_recv()
-
-    def rows_of(k):
-        return pl.ds(pl.multiple_of(k * CH, CH), CH)
-
-    def all_rows(ref, k):
-        return ref[:, rows_of(k), :].reshape(4 * CH, ref.shape[2])
-
-    @pl.loop(0, chunks)
-    def _(k):
-        rs_start(0, k, lambda q: mm(mixed_ref[q, rows_of(k), :], wo_ref[...], NT))
-
-    @pl.loop(0, chunks)
-    def _(k):
-        resid = rs_end(0, k) + tok_ref[rows_of(k), :].astype(f32) + bo
-        hat, inv = norm_rows(resid)
-        hat1[k] = hat
-        inv1[k] = inv
-        val = hat * g1 + s1
-        normed[k] = val
-        ag_start(0, k, val.astype(bf16))
-
-    @pl.loop(0, chunks)
-    def _(k):
-        ag_end(0, k)
-        pre = mm(all_rows(nfull, k), win_ref[...], NN) + bin_ref[...]
-        cum = 0.5 * (1.0 + lax.erf(pre * root_half))
-        dens = jnp.exp(-0.5 * pre * pre) * inv_root_two_pi
-        hidden[:, rows_of(k), :] = (pre * cum).astype(bf16).reshape(4, CH, D)
-        slope[:, rows_of(k), :] = (cum + pre * dens).reshape(4, CH, D)
-        rs_start(1, k, lambda q: mm(hidden[q, rows_of(k), :], wout_ref[...], NT))
-
-    dvec_ref[...] = jnp.zeros_like(dvec_ref)
-
-    @pl.loop(0, chunks)
-    def _(k):
-        resid = rs_end(1, k) + normed[k] + b2
-        hat, inv = norm_rows(resid)
-        out_ref[rows_of(k), :] = (hat * g2 + s2).astype(out_ref.dtype)
-        cot = cot_ref[rows_of(k), :].astype(f32)
-        grad = norm_back(cot, g2, hat, inv)
-        grad2[k] = grad
-        ag_start(1, k, grad.astype(bf16))
-        dvec_ref[pl.ds(2, 1), :] += jnp.sum(grad, axis=0, keepdims=True)
-        dvec_ref[pl.ds(5, 1), :] += jnp.sum(cot * hat, axis=0, keepdims=True)
-        dvec_ref[pl.ds(6, 1), :] += jnp.sum(cot, axis=0, keepdims=True)
-
-    dwin_ref[...] = jnp.zeros_like(dwin_ref)
-    dwout_ref[...] = jnp.zeros_like(dwout_ref)
-    dwo_ref[...] = jnp.zeros_like(dwo_ref)
-    dbin_ref[...] = jnp.zeros_like(dbin_ref)
-
-    @pl.loop(0, chunks)
-    def _(k):
-        ag_end(1, k)
-        g2c = all_rows(g2full, k)
-        grad_pre = mm(g2c, wout_ref[...], NN) * all_rows(slope, k)
-        dbin_ref[...] += jnp.sum(grad_pre, axis=0, keepdims=True)
-        low = grad_pre.astype(bf16)
-        hid = all_rows(hidden, k)
-        hidden[:, rows_of(k), :] = low.reshape(4, CH, D)
-        rs_start(2, k, lambda q: mm(hidden[q, rows_of(k), :], win_ref[...], NT))
-        dwout_ref[...] += mm(g2c, hid, TN)
-        dwin_ref[...] += mm(all_rows(nfull, k), low, TN)
-
-    @pl.loop(0, chunks)
-    def _(k):
-        grad_normed = rs_end(2, k) + grad2[k]
-        hat = hat1[k]
-        grad = norm_back(grad_normed, g1, hat, inv1[k])
-        ag_start(2, k, grad.astype(bf16))
-        dvec_ref[pl.ds(1, 1), :] += jnp.sum(grad, axis=0, keepdims=True)
-        dvec_ref[pl.ds(3, 1), :] += jnp.sum(grad_normed * hat, axis=0, keepdims=True)
-        dvec_ref[pl.ds(4, 1), :] += jnp.sum(grad_normed, axis=0, keepdims=True)
-
-    @pl.loop(0, chunks)
-    def _(k):
-        ag_end(2, k)
-        g1c = all_rows(g1_ref, k)
-        gmix_ref[:, rows_of(k), :] = mm(g1c, wo_ref[...], NN).astype(bf16).reshape(4, CH, FEAT)
-        dwo_ref[...] += mm(g1c, all_rows(mixed_ref, k), TN)
-
-    @pl.loop(0, chunks)
-    def _(k):
-        for st in range(3):
-            d2d(st, k).wait_send()
-            xcopy(st, k).wait_send()
-            to_sib(st, k, c).wait_send()
-            to_nbr(st, k, c).wait_send()
-            fwd(st, k, nbr).wait_send()
-
-
-def middle(mixed, tok, cot, wo, win, wout, vec, b_in):
-    own_rows = tok.shape[0]
-    chunks = own_rows // CH
-    sem = pltpu.SemaphoreType.DMA((3, chunks))
-    S = jax.ShapeDtypeStruct
-    return pl.pallas_call(
-        middle_body,
-        out_shape=(
-            S((own_rows, D), bf16),
-            S((4, own_rows, D), bf16),
-            S((4, own_rows, FEAT), bf16),
-            S((D, FEAT), f32),
-            S((D, D), f32),
-            S((D, D), f32),
-            S((8, D), f32),
-            S((1, D), f32),
-        ),
-        in_specs=[VM] * 8,
-        out_specs=(VM,) * 8,
-        scratch_shapes=[
-            pltpu.VMEM((4, own_rows, D), bf16),
-            pltpu.VMEM((4, own_rows, D), bf16),
-            pltpu.VMEM((4, own_rows, D), f32),
-            pltpu.VMEM((4, own_rows, D), bf16),
-            pltpu.VMEM((3, chunks, CH, D), f32),
-            pltpu.VMEM((3, chunks, 2, CH, D), bf16),
-            pltpu.VMEM((3, chunks, 2, CH, D), bf16),
-            pltpu.VMEM((3, chunks, CH, D), bf16),
-            pltpu.VMEM((3, chunks, CH, D), bf16),
-            pltpu.VMEM((chunks, CH, D), f32),
-            pltpu.VMEM((chunks, CH, D), f32),
-            pltpu.VMEM((chunks, CH, 1), f32),
-            pltpu.VMEM((chunks, CH, D), f32),
-        ]
-        + [sem] * 10,
-        name="middle",
-        compiler_params=pltpu.CompilerParams(collective_id=2, has_side_effects=True, vmem_limit_bytes=60 << 20),
-        cost_estimate=pl.CostEstimate(flops=80_000_000_000, bytes_accessed=20_000_000, transcendentals=4_000_000),
-    )(mixed, tok, cot, wo, win, wout, vec, b_in)
-
-
 HALF = 384
 
 
@@ -469,6 +278,11 @@
 def picker_cols(rank, count):
     have = lax.broadcasted_iota(jnp.int32, (rank.shape[0], count), 1).astype(f32)
     return jnp.where(rank == have, 1.0, 0.0).astype(bf16)
+
+
+def placed(rank_col, got):
+    tokens = got.shape[0] * got.shape[1] * got.shape[2]
+    return mm(picker_cols(rank_col, tokens), got.reshape(tokens, HALF), NN)
 
 
 class Deal:
@@ -541,14 +355,14 @@
             self.share(i).wait_recv()
 
     def placed(self, rank_col):
-        return mm(picker_cols(rank_col, self.tokens), self.rbuf[self.a].reshape(self.tokens, HALF), NN)
-
-    def finish(self, joins=True):
-        if joins:
-            self.to_sib().wait_send()
-            self.to_nbr().wait_send()
+        return placed(rank_col, self.rbuf[self.a])
+
+    def joined_sent(self):
+        self.to_sib().wait_send()
+        self.to_nbr().wait_send()
         self.fwd().wait_send()
 
+    def rows_sent(self):
         @pl.loop(1, self.rows)
         def _(i):
             self.row_copy(i).wait_send()
@@ -558,28 +372,28 @@
             self.share(i).wait_send()
 
 
-def deal_scratch(rows, own_rows):
+def deal_scratch(rows, own_rows, count):
     slots = 4 * own_rows // rows
     return [
-        pltpu.VMEM((2, 4, own_rows, HALF), bf16),
-        pltpu.VMEM((2, own_rows, HALF), bf16),
-        pltpu.VMEM((2, rows, slots // 2, HALF), bf16),
-        pltpu.VMEM((2, rows, 2, slots // 2, HALF), bf16),
+        pltpu.VMEM((count, 4, own_rows, HALF), bf16),
+        pltpu.VMEM((count, own_rows, HALF), bf16),
+        pltpu.VMEM((count, rows, slots // 2, HALF), bf16),
+        pltpu.VMEM((count, rows, 2, slots // 2, HALF), bf16),
     ]
 
 
-def deal_sems(rows):
-    return [pltpu.SemaphoreType.DMA((2,))] * 6 + [pltpu.SemaphoreType.DMA((2, rows))] * 4
+def deal_sems(rows, count):
+    return [pltpu.SemaphoreType.DMA((count,))] * 6 + [pltpu.SemaphoreType.DMA((count, rows))] * 4
 
 
 def arrive_body(
     rows, x_ref, g_ref, place_ref, order_ref, vin_ref,
-    tok_ref, cot_ref, rank_ref, vec_ref, bqv_ref, bin_ref,
+    tok_ref, own_ref, cot_ref, cot_send, rank_ref, vec_ref, bqv_ref, bin_ref,
     *scratch,
 ):
     bufs, sems = scratch[:4], scratch[4:14]
-    key_g, key_w, col_g, col_w, cot_send, vbuf = scratch[14:20]
-    an_s, an_r, as_s, as_r, af_s, af_r, ct_s, ct_r, vr_s, vr_r, vc_s, vc_r = scratch[20:]
+    key_g, key_w, col_g, col_w, vbuf = scratch[14:19]
+    an_s, an_r, as_s, as_r, af_s, af_r, vr_s, vr_r, vc_s, vc_r = scratch[19:]
     r, c, sib, nbr, diag = col_peers()
     h = c // 2
     own_rows = x_ref.shape[0]
@@ -670,19 +484,20 @@
             tok_copy(qi, q, k, h, an_s, an_r, nbr).start()
             tok_copy(qi, q, k, h, as_s, as_r, sib).start()
 
-    second.shared()
-    rank = col_w[pl.ds(pl.multiple_of(nbr * own_rows, CH), own_rows), :]
-    cot_send[...] = second.placed(rank).astype(bf16)
-    cot_copy = remote(cot_send, cot_ref.at[:, half_lanes(h)], ct_s.at[0], ct_r.at[0], (r, nbr))
-    cot_copy.start()
-    rank = col_w[pl.ds(pl.multiple_of(c * own_rows, CH), own_rows), :]
-    cot_ref[:, half_lanes(h)] = second.placed(rank).astype(bf16)
-
-    @pl.loop(0, chunks)
-    def _(k):
+    def pass_on(k):
         for qi, q in ours:
             tok_copy(1 - qi, q, k, 1 - h, an_s, an_r, nbr).wait_recv()
             tok_copy(qi, q, k, 1 - h, af_s, af_r, sib).start()
+
+    pl.loop(0, chunks // 2)(pass_on)
+    second.shared()
+    pl.loop(chunks // 2, chunks)(pass_on)
+    for q, ref in ((nbr, cot_send), (c, cot_ref)):
+
+        @pl.loop(0, chunks)
+        def _(k):
+            rank = col_w[pl.ds(pl.multiple_of(q * own_rows + k * CH, CH), CH), :]
+            ref[pl.ds(pl.multiple_of(k * CH, CH), CH), :] = second.placed(rank).astype(bf16)
 
     @pl.loop(0, chunks)
     def _(k):
@@ -693,9 +508,11 @@
             tok_copy(qi, q, k, h, as_s, as_r, sib).wait_send()
             tok_copy(qi, q, k, 1 - h, af_s, af_r, sib).wait_send()
 
-    cot_copy.wait()
-    first.finish()
-    second.finish()
+    own_ref[...] = tok_ref[c]
+
+    for deal in (first, second):
+        deal.joined_sent()
+        deal.rows_sent()
 
     @pl.loop(1, rows)
     def _(i):
@@ -713,19 +530,19 @@
     return pl.pallas_call(
         functools.partial(arrive_body, rows),
         out_shape=(
-            S((4, own_rows, D), bf16), S((own_rows, D), bf16), S((8, tokens), f32),
+            S((4, own_rows, D), bf16), S((own_rows, D), bf16),
+            S((own_rows, HALF), bf16), S((own_rows, HALF), bf16), S((8, tokens), f32),
             S((8, D), f32), S((8, FEAT), f32), S((1, D), f32),
         ),
         in_specs=[VM] * 5,
-        out_specs=(VM,) * 6,
-        scratch_shapes=deal_scratch(rows, own_rows)
-        + deal_sems(rows)
+        out_specs=(VM,) * 8,
+        scratch_shapes=deal_scratch(rows, own_rows, 2)
+        + deal_sems(rows, 2)
         + [
             V((1, tokens), f32), V((1, tokens), f32), V((tokens, 1), f32), V((tokens, 1), f32),
-            V((own_rows, HALF), bf16), V((4, rows, 8, HALF), f32),
+            V((4, rows, 8, HALF), f32),
         ]
         + [DS((2, chunks))] * 6
-        + [DS((1,))] * 2
         + [DS((rows,))] * 2
         + [DS((3,))] * 2,
         name="arrive",
@@ -790,18 +607,254 @@
                 self.copy(way, t).wait_send()
 
 
+def middle_body(
+    rows, mixed_ref, tok_ref, cot_own, cot_got, wo_ref, win_ref, wout_ref, vec_ref, bin_ref, rank_ref,
+    back_ref, g1_ref, gmix_ref, dwo_ref, gin_ref, gout_ref, dvec_ref, dbin_ref,
+    *scratch,
+):
+    nfull, hidden, slope, g2full, own, d2ds, d2dr, xs, xr, hat1, inv1, grad2, dwin, dwout = scratch[:14]
+    out_buf, xin, xout, sbuf, ring_out, ring_in = scratch[14:20]
+    ds_s, ds_r, x_s, x_r, asib_s, asib_r, anbr_s, anbr_r, afwd_s, afwd_r, q_s, q_r = scratch[20:32]
+    r, c, sib, nbr, diag = col_peers()
+    h = c // 2
+    chunks = out_buf.shape[0] // CH
+    block = D // rows
+    greet((sib, nbr), rows, r, c)
+    outs = Deal(0, rows, (xin, xout, sbuf, back_ref), scratch[32:])
+    ring = Ring(rows, lambda b: jnp.concatenate([dwin[b], dwout[b]], axis=1), ring_out, ring_in, (q_s, q_r))
+
+    bo, g1, s1, b2, g2, s2 = [vec_ref[pl.ds(i, 1), :] for i in range(6)]
+
+    def d2d(st, k):
+        return remote(d2ds.at[k], d2dr.at[k], ds_s.at[st, k], ds_r.at[st, k], (r, sib))
+
+    def xcopy(st, k):
+        return remote(xs.at[k], xr.at[k], x_s.at[st, k], x_r.at[st, k], (r, nbr))
+
+    def rs_start(st, k, part):
+        if st > 0:
+            d2d(st - 1, k).wait_send()
+            xcopy(st - 1, k).wait_send()
+        d2ds[k, 0] = part(sib).astype(bf16)
+        d2ds[k, 1] = part(diag).astype(bf16)
+        d2d(st, k).start()
+        mine = part(c)
+        other = part(nbr)
+        d2d(st, k).wait_recv()
+        xs[k] = (other + d2dr[k, 1].astype(f32)).astype(bf16)
+        xcopy(st, k).start()
+        own[k] = mine + d2dr[k, 0].astype(f32)
+
+    def rs_end(st, k):
+        xcopy(st, k).wait_recv()
+        return own[k] + xr[k].astype(f32)
+
+    gathered = (nfull, g2full, g1_ref)
+
+    def piece(st, q, k):
+        return gathered[st].at[q, pl.ds(pl.multiple_of(k * CH, CH), CH), :]
+
+    def ag_copy(st, k, q, sems, target):
+        return remote(piece(st, q, k), piece(st, q, k), sems[0].at[st, k], sems[1].at[st, k], (r, target))
+
+    to_sib = functools.partial(ag_copy, sems=(asib_s, asib_r), target=sib)
+    to_nbr = functools.partial(ag_copy, sems=(anbr_s, anbr_r), target=nbr)
+    fwd = functools.partial(ag_copy, sems=(afwd_s, afwd_r), target=sib)
+
+    def ag_start(st, k, value):
+        gathered[st][c, pl.ds(pl.multiple_of(k * CH, CH), CH), :] = value
+        to_nbr(st, k, c).start()
+        to_sib(st, k, c).start()
+
+    def ag_end(st, k):
+        to_nbr(st, k, c).wait_recv()
+        fwd(st, k, nbr).start()
+        to_sib(st, k, c).wait_recv()
+        fwd(st, k, nbr).wait_recv()
+
+    def rows_of(k):
+        return pl.ds(pl.multiple_of(k * CH, CH), CH)
+
+    def all_rows(ref, k):
+        return ref[:, rows_of(k), :].reshape(4 * CH, ref.shape[2])
+
+    @pl.loop(0, chunks)
+    def _(k):
+        rs_start(0, k, lambda q: mm(mixed_ref[q, rows_of(k), :], wo_ref[...], NT))
+
+    @pl.loop(0, chunks)
+    def _(k):
+        resid = rs_end(0, k) + tok_ref[rows_of(k), :].astype(f32) + bo
+        hat, inv = norm_rows(resid)
+        hat1[k] = hat
+        inv1[k] = inv
+        val = hat * g1 + s1
+        ag_start(0, k, val.astype(bf16))
+
+    @pl.loop(0, chunks)
+    def _(k):
+        ag_end(0, k)
+        pre = mm(all_rows(nfull, k), win_ref[...], NN) + bin_ref[...]
+        cum = 0.5 * (1.0 + lax.erf(pre * root_half))
+        dens = jnp.exp(-0.5 * pre * pre) * inv_root_two_pi
+        hidden[:, rows_of(k), :] = (pre * cum).astype(bf16).reshape(4, CH, D)
+        slope[:, rows_of(k), :] = (cum + pre * dens).reshape(4, CH, D)
+        rs_start(1, k, lambda q: mm(hidden[q, rows_of(k), :], wout_ref[...], NT))
+
+    dvec_ref[...] = jnp.zeros_like(dvec_ref)
+
+    @pl.loop(0, chunks)
+    def _(k):
+        resid = rs_end(1, k) + (hat1[k] * g1 + s1) + b2
+        hat, inv = norm_rows(resid)
+        out_buf[rows_of(k), :] = (hat * g2 + s2).astype(bf16)
+        halves = (cot_own[rows_of(k), :], cot_got[rows_of(k), :])
+        low, high = jnp.where(h == 0, halves[0], halves[1]), jnp.where(h == 0, halves[1], halves[0])
+        cot = jnp.concatenate([low, high], axis=1).astype(f32)
+        grad = norm_back(cot, g2, hat, inv)
+        grad2[k] = grad
+        ag_start(1, k, grad.astype(bf16))
+        dvec_ref[pl.ds(2, 1), :] += jnp.sum(grad, axis=0, keepdims=True)
+        dvec_ref[pl.ds(5, 1), :] += jnp.sum(cot * hat, axis=0, keepdims=True)
+        dvec_ref[pl.ds(6, 1), :] += jnp.sum(cot, axis=0, keepdims=True)
+
+    outs.split(out_buf)
+    dwin[...] = jnp.zeros_like(dwin)
+    dwout[...] = jnp.zeros_like(dwout)
+    dwo_ref[...] = jnp.zeros_like(dwo_ref)
+    dbin_ref[...] = jnp.zeros_like(dbin_ref)
+
+    def add_blocks(ref, value):
+        if block % 8 == 0:
+            ref[...] += value.reshape(rows, block, D)
+        else:
+            for b in range(rows):
+                ref[b] += value[b * block : (b + 1) * block]
+
+    def back_hidden(k):
+        ag_end(1, k)
+        g2c = all_rows(g2full, k)
+        grad_pre = mm(g2c, wout_ref[...], NN) * all_rows(slope, k)
+        dbin_ref[...] += jnp.sum(grad_pre, axis=0, keepdims=True)
+        low = grad_pre.astype(bf16)
+        hid = all_rows(hidden, k)
+        hidden[:, rows_of(k), :] = low.reshape(4, CH, D)
+        rs_start(2, k, lambda q: mm(hidden[q, rows_of(k), :], win_ref[...], NT))
+        add_blocks(dwout, mm(g2c, hid, TN))
+        add_blocks(dwin, mm(all_rows(nfull, k), low, TN))
+
+    pl.loop(0, chunks // 2)(back_hidden)
+    outs.joined()
+    outs.pick_and_send(rank_ref[1:2, :])
+    pl.loop(chunks // 2, chunks)(back_hidden)
+    ring.start()
+
+    def hops(part):
+        for t in range(1 + part * (ring.hops - 1) // 3, 1 + (part + 1) * (ring.hops - 1) // 3):
+            ring.hop(t)
+
+    def back_first(k):
+        grad_normed = rs_end(2, k) + grad2[k]
+        hat = hat1[k]
+        grad = norm_back(grad_normed, g1, hat, inv1[k])
+        ag_start(2, k, grad.astype(bf16))
+        dvec_ref[pl.ds(1, 1), :] += jnp.sum(grad, axis=0, keepdims=True)
+        dvec_ref[pl.ds(3, 1), :] += jnp.sum(grad_normed * hat, axis=0, keepdims=True)
+        dvec_ref[pl.ds(4, 1), :] += jnp.sum(grad_normed, axis=0, keepdims=True)
+
+    pl.loop(0, chunks // 2)(back_first)
+    hops(0)
+    pl.loop(chunks // 2, chunks)(back_first)
+    hops(1)
+
+    def back_mixed(k):
+        ag_end(2, k)
+        g1c = all_rows(g1_ref, k)
+        gmix_ref[:, rows_of(k), :] = mm(g1c, wo_ref[...], NN).astype(bf16).reshape(4, CH, FEAT)
+        dwo_ref[...] += mm(g1c, all_rows(mixed_ref, k), TN)
+
+    pl.loop(0, chunks // 2)(back_mixed)
+    hops(2)
+    pl.loop(chunks // 2, chunks)(back_mixed)
+    outs.shared()
+    total = ring.result()
+    gin_ref[...] = total[:, :D]
+    gout_ref[...] = total[:, D:].T
+
+    @pl.loop(0, chunks)
+    def _(k):
+        d2d(2, k).wait_send()
+        xcopy(2, k).wait_send()
+        for st in range(3):
+            to_sib(st, k, c).wait_send()
+            to_nbr(st, k, c).wait_send()
+            fwd(st, k, nbr).wait_send()
+
+    outs.joined_sent()
+    outs.rows_sent()
+    ring.finish()
+
+
+def middle(rows, mixed, tok, cot_own, cot_got, wo, win, wout, vec, b_in, rank):
+    own_rows = tok.shape[0]
+    chunks = own_rows // CH
+    block, hops, slots = D // rows, rows // 2, 4 * own_rows // rows
+    sem = pltpu.SemaphoreType.DMA((3, chunks))
+    S, V = jax.ShapeDtypeStruct, pltpu.VMEM
+    return pl.pallas_call(
+        functools.partial(middle_body, rows),
+        out_shape=(
+            S((1, rows, 2, slots // 2, HALF), bf16),
+            S((4, own_rows, D), bf16),
+            S((4, own_rows, FEAT), bf16),
+            S((D, FEAT), f32),
+            S((block, D), f32),
+            S((D, block), f32),
+            S((8, D), f32),
+            S((1, D), f32),
+        ),
+        in_specs=[VM] * 10,
+        out_specs=(VM,) * 8,
+        scratch_shapes=[
+            pltpu.VMEM((4, own_rows, D), bf16),
+            pltpu.VMEM((4, own_rows, D), bf16),
+            pltpu.VMEM((4, own_rows, D), f32),
+            pltpu.VMEM((4, own_rows, D), bf16),
+            pltpu.VMEM((chunks, CH, D), f32),
+            pltpu.VMEM((chunks, 2, CH, D), bf16),
+            pltpu.VMEM((chunks, 2, CH, D), bf16),
+            pltpu.VMEM((chunks, CH, D), bf16),
+            pltpu.VMEM((chunks, CH, D), bf16),
+            pltpu.VMEM((chunks, CH, D), f32),
+            pltpu.VMEM((chunks, CH, 1), f32),
+            pltpu.VMEM((chunks, CH, D), f32),
+            V((rows, block, D), f32),
+            V((rows, block, D), f32),
+            V((own_rows, D), bf16),
+        ]
+        + deal_scratch(rows, own_rows, 1)[:3]
+        + [V((2, hops, block, 2 * D), bf16)] * 2
+        + [sem] * 10
+        + [pltpu.SemaphoreType.DMA((2, hops))] * 2
+        + deal_sems(rows, 1),
+        name="middle",
+        compiler_params=pltpu.CompilerParams(collective_id=2, has_side_effects=True, vmem_limit_bytes=62 << 20),
+        cost_estimate=pl.CostEstimate(flops=80_000_000_000, bytes_accessed=20_000_000, transcendentals=4_000_000),
+    )(mixed, tok, cot_own, cot_got, wo, win, wout, vec, b_in, rank)
+
+
 def depart_body(
-    rows, out_in, g1_ref, dqkv_ref, w_ref, tok_ref, rank_ref, dwo_ref, dwin_ref, dwout_ref, dvec_ref, dbin_ref,
-    out_ref, grad_ref, gw_ref, gff_ref, gvec_ref, gwide_ref,
+    rows, back_ref, g1_ref, dqkv_ref, w_ref, tok_ref, rank_ref, dwo_ref, dvec_ref, dbin_ref,
+    out_ref, grad_ref, gq_ref, gk_ref, gv_ref, go_ref, gvec_ref, gwide_ref,
     *scratch,
 ):
     bufs, sems = scratch[:4], scratch[4:14]
     key, col_g, sums, dw = scratch[14:18]
-    d2ds, d2dr, keep, xs, xr, gsend, grecv, r1s, r1r, r2s, r2r, vmine, vall, vrow = scratch[18:32]
-    ds_s, ds_r, x_s, x_r, fin_s, fin_r, q1_s, q1_r, q2_s, q2_r, vc_s, vc_r, vr_s, vr_r = scratch[32:]
+    d2ds, d2dr, keep, xs, xr, gsend, grecv, r2s, r2r, vmine, vall, vrow = scratch[18:30]
+    ds_s, ds_r, x_s, x_r, fin_s, fin_r, q2_s, q2_r, sh_s, sh_r, vc_s, vc_r, vr_s, vr_r = scratch[30:]
     r, c, sib, nbr, diag = col_peers()
     h = c // 2
-    own_rows = out_in.shape[0]
+    own_rows = out_ref.shape[0]
     tokens = 4 * own_rows
     chunks = own_rows // CH
     block = D // rows
@@ -810,15 +863,12 @@
     def rows_of(k):
         return pl.ds(pl.multiple_of(k * CH, CH), CH)
 
-    outs, grads = Deal(0, rows, bufs, sems), Deal(1, rows, bufs, sems)
-    outs.split(out_in)
-    ring_ff = Ring(
-        rows, lambda b: jnp.concatenate([dwin_ref[b], dwout_ref[b]], axis=1), r1s, r1r, (q1_s, q1_r)
-    )
-    ring_at = Ring(
-        rows, lambda b: jnp.concatenate([dw[b], dwo_ref[b]], axis=1), r2s, r2r, (q2_s, q2_r)
-    )
-    ring_ff.start()
+    def token_rows(q, k):
+        return pl.ds(pl.multiple_of(q * own_rows + k * CH, CH), CH)
+
+    grads = Deal(0, rows, bufs, sems)
+    ring = Ring(rows, lambda b: jnp.concatenate([dw[b], dwo_ref[b]], axis=1), r2s, r2r, (q2_s, q2_r))
+    ours = ((0, c), (1, nbr))
 
     vmine[...] = jnp.zeros_like(vmine)
     vmine[0:8, :] = dvec_ref[...]
@@ -836,59 +886,32 @@
         return remote(xs.at[k], xr.at[k], x_s.at[k], x_r.at[k], (r, nbr))
 
     def part(q, k):
-        return mm(dqkv_ref[pl.ds(pl.multiple_of(q * own_rows + k * CH, CH), CH), :], w_ref[...], NT)
+        return mm(dqkv_ref[token_rows(q, k), :], w_ref[...], NT)
 
     @pl.loop(0, chunks)
     def _(k):
         d2ds[k, 0] = part(sib, k).astype(bf16)
         d2ds[k, 1] = part(diag, k).astype(bf16)
         d2d(k).start()
-        for i, q in ((0, c), (1, nbr)):
+        for i, q in ours:
             keep[k, i] = part(q, k)
-
-    @pl.loop(0, chunks)
-    def _(k):
         d2d(k).wait_recv()
         for i in range(2):
             keep[k, i] = keep[k, i] + d2dr[k, i].astype(f32)
             xs[k, 1 - i] = keep[k, i, :, half_lanes(1 - h)].astype(bf16)
         xcopy(k).start()
 
-    key[...] = rank_ref[0:1, :]
-    to_col(key, col_g)
-    rank_w = rank_ref[1:2, :]
-    outs.joined()
-    outs.pick_and_send(rank_w)
-
     whole = mm(tok_ref[...].reshape(tokens, D), dqkv_ref[...], TN)
     for b in range(rows):
         dw[b] = whole[b * block : (b + 1) * block]
+    ring.start()
+
     sums[...] = jnp.zeros_like(sums)
 
     @pl.loop(0, tokens // QB)
     def _(k):
         part_rows = dqkv_ref[pl.ds(pl.multiple_of(k * QB, QB), QB), :].astype(f32)
         sums[0:1, :] += jnp.sum(part_rows, axis=0, keepdims=True)
-
-    ring_ff.hop(1)
-
-    @pl.loop(0, chunks)
-    def _(k):
-        xcopy(k).wait_recv()
-        for i, q in ((0, c), (1, nbr)):
-            total = keep[k, i, :, half_lanes(h)] + xr[k, i].astype(f32) + g1_ref[q, rows_of(k), half_lanes(h)].astype(f32)
-            grads.xin[1, q, rows_of(k), :] = total.astype(bf16)
-
-    shares = [
-        remote(grads.xin.at[1, q], grads.xin.at[1, q], s.at[1], rr.at[1], (r, sib))
-        for q, s, rr in ((c, grads.sib_s, grads.sib_r), (nbr, grads.fwd_s, grads.fwd_r))
-    ]
-    for copy in shares:
-        copy.start()
-    for copy in shares:
-        copy.wait_recv()
-    grads.pick_and_send(rank_w)
-    ring_at.start()
 
     for i, peer in enumerate((sib, nbr, diag)):
         vec_col(i, peer).wait_recv()
@@ -905,31 +928,59 @@
     def _(i):
         vec_row(i).start()
 
-    for t in range(2, rows // 2):
-        ring_ff.hop(t)
-    gff_ref[...] = ring_ff.result()
-    for t in range(1, rows // 2):
-        ring_at.hop(t)
-    gw_ref[...] = ring_at.result()
-
-    outs.shared()
-
-    def final(deal, i):
-        rank = col_g[pl.ds(pl.multiple_of(nbr * own_rows, CH), own_rows), :]
-        gsend[i] = deal.placed(rank).astype(bf16)
-        return remote(gsend.at[i], grecv.at[i], fin_s.at[i], fin_r.at[i], (r, nbr))
-
-    def own_half(deal, ref):
-        rank = col_g[pl.ds(pl.multiple_of(c * own_rows, CH), own_rows), :]
-        ref[:, half_lanes(h)] = deal.placed(rank)
-
-    out_copy = final(outs, 0)
-    out_copy.start()
-    own_half(outs, out_ref)
-    grads.shared()
-    grad_copy = final(grads, 1)
-    grad_copy.start()
-    own_half(grads, grad_ref)
+    key[...] = rank_ref[0:1, :]
+    to_col(key, col_g)
+
+    def final(i, k):
+        return remote(gsend.at[i, k], grecv.at[i, k], fin_s.at[i, k], fin_r.at[i, k], (r, nbr))
+
+    def send_final(i, got):
+        @pl.loop(0, chunks)
+        def _(k):
+            gsend[i, k] = placed(col_g[token_rows(nbr, k), :], got[0]).astype(bf16)
+            final(i, k).start()
+
+    def own_final(got, ref):
+        @pl.loop(0, chunks)
+        def _(k):
+            ref[rows_of(k), half_lanes(h)] = placed(col_g[token_rows(c, k), :], got[0])
+
+    def take_final(i, ref):
+        @pl.loop(0, chunks)
+        def _(k):
+            final(i, k).wait_recv()
+            ref[rows_of(k), half_lanes(1 - h)] = grecv[i, k].astype(f32)
+
+    send_final(0, back_ref)
+    if ring.hops > 1:
+        ring.hop(1)
+    own_final(back_ref, out_ref)
+
+    def shared(k, i, q):
+        v = grads.xin.at[0, q, rows_of(k)]
+        return remote(v, v, sh_s.at[i, k], sh_r.at[i, k], (r, sib))
+
+    def grad_rows(k):
+        xcopy(k).wait_recv()
+        for i, q in ours:
+            total = keep[k, i, :, half_lanes(h)] + xr[k, i].astype(f32) + g1_ref[q, rows_of(k), half_lanes(h)].astype(f32)
+            grads.xin[0, q, rows_of(k), :] = total.astype(bf16)
+            shared(k, i, q).start()
+
+    pl.loop(0, chunks)(grad_rows)
+
+    @pl.loop(0, chunks)
+    def _(k):
+        for i, q in ours:
+            shared(k, i, q).wait_recv()
+
+    grads.pick_and_send(rank_ref[1:2, :])
+    for t in range(2, ring.hops):
+        ring.hop(t)
+    total = ring.result()
+    for i, ref in enumerate((gq_ref, gk_ref, gv_ref)):
+        ref[...] = total[:, i * FEAT : (i + 1) * FEAT]
+    go_ref[...] = total[:, 3 * FEAT :].T
 
     @pl.loop(1, rows)
     def _(i):
@@ -950,33 +1001,24 @@
     gwide_ref[0:1, :] = chosen(total[8:16, :], r * wide, wide)[0:1, :]
     gwide_ref[1:2, :] = chosen(total[8:16, :], r * width, width)[1:2, :]
     gwide_ref[2:3, :] = chosen(total[8:16, :], 2 * FEAT + r * width, width)[1:2, :]
-
-    out_copy.wait_recv()
-    out_ref[:, half_lanes(1 - h)] = grecv[0].astype(f32)
-    grad_copy.wait_recv()
-    grad_ref[:, half_lanes(1 - h)] = grecv[1].astype(f32)
-
-    out_copy.wait_send()
-    grad_copy.wait_send()
-    outs.finish()
-    for copy in shares:
-        copy.wait_send()
-
-    @pl.loop(1, rows)
-    def _(i):
-        grads.row_copy(i).wait_send()
-
-    @pl.loop(0, rows)
-    def _(i):
-        grads.share(i).wait_send()
+    take_final(0, out_ref)
+
+    grads.shared()
+    send_final(1, grads.rbuf)
+    own_final(grads.rbuf, grad_ref)
+    take_final(1, grad_ref)
+
+    grads.rows_sent()
 
     @pl.loop(0, chunks)
     def _(k):
+        for i, q in ours:
+            shared(k, i, q).wait_send()
+            final(i, k).wait_send()
         d2d(k).wait_send()
         xcopy(k).wait_send()
 
-    ring_ff.finish()
-    ring_at.finish()
+    ring.finish()
     for i, peer in enumerate((sib, nbr, diag)):
         vec_col(i, peer).wait_send()
 
@@ -985,40 +1027,41 @@
         vec_row(i).wait_send()
 
 
-def depart(rows, out, g1, dqkv, w_qkv, tok, rank, dwo, dwin, dwout, dvec, dbin):
-    own_rows = out.shape[0]
+def depart(rows, back, g1, dqkv, w_qkv, tok, rank, dwo, dvec, dbin):
+    own_rows = tok.shape[1]
     tokens = 4 * own_rows
     chunks = own_rows // CH
     block, hops = D // rows, rows // 2
     S, V, DS = jax.ShapeDtypeStruct, pltpu.VMEM, pltpu.SemaphoreType.DMA
+    third = S((block, FEAT), f32)
     return pl.pallas_call(
         functools.partial(depart_body, rows),
         out_shape=(
-            S((own_rows, D), f32), S((own_rows, D), f32), S((block, D), f32), S((block, 2 * D), f32),
+            S((own_rows, D), f32), S((own_rows, D), f32), third, third, third, S((FEAT, block), f32),
             S((8, 128), f32), S((8, 128), f32),
         ),
-        in_specs=[VM] * 11,
-        out_specs=(VM,) * 6,
-        scratch_shapes=deal_scratch(rows, own_rows)
-        + deal_sems(rows)
+        in_specs=[VM] * 9,
+        out_specs=(VM,) * 8,
+        scratch_shapes=deal_scratch(rows, own_rows, 1)
+        + deal_sems(rows, 1)
         + [V((1, tokens), f32), V((tokens, 1), f32), V((8, 3 * FEAT), f32), V((rows, block, 3 * FEAT), f32)]
         + [
             V((chunks, 2, CH, D), bf16), V((chunks, 2, CH, D), bf16), V((chunks, 2, CH, D), f32),
             V((chunks, 2, CH, HALF), bf16), V((chunks, 2, CH, HALF), bf16),
-            V((2, own_rows, HALF), bf16), V((2, own_rows, HALF), bf16),
-            V((2, hops, block, 2 * D), bf16), V((2, hops, block, 2 * D), bf16),
+            V((2, chunks, CH, HALF), bf16), V((2, chunks, CH, HALF), bf16),
             V((2, hops, block, D), bf16), V((2, hops, block, D), bf16),
             V((16, D), f32), V((4, 16, D), f32), V((rows, 16, D), f32),
         ]
         + [DS((chunks,))] * 4
-        + [DS((2,))] * 2
-        + [DS((2, hops))] * 4
+        + [DS((2, chunks))] * 2
+        + [DS((2, hops))] * 2
+        + [DS((2, chunks))] * 2
         + [DS((3,))] * 2
         + [DS((rows,))] * 2,
         name="depart",
         compiler_params=pltpu.CompilerParams(collective_id=3, has_side_effects=True, vmem_limit_bytes=60 << 20),
         cost_estimate=pl.CostEstimate(flops=60_000_000_000, bytes_accessed=20_000_000, transcendentals=0),
-    )(out, g1, dqkv, w_qkv, tok, rank, dwo, dwin, dwout, dvec, dbin)
+    )(back, g1, dqkv, w_qkv, tok, rank, dwo, dvec, dbin)
 
 
 def per_device(
@@ -1028,7 +1071,6 @@
     first_gain, first_shift, second_gain, second_shift,
 ):
     rows = lax.axis_size("row")
-    col = lax.axis_index("col")
     own_rows = inputs.shape[0]
     tok_rows = 4 * own_rows
 
@@ -1053,22 +1095,21 @@
     hi = (end[QB - 1 :: QB] + KB - 1) // KB
     start, end = start[None], end[None]
 
-    tok, cot, rank, vec, bqv, b_in = arrive(rows, inputs, cotangent, token_place[None], token_order[None], vin)
+    tok, own_tok, cot_own, cot_send, rank, vec, bqv, b_in = arrive(
+        rows, inputs, cotangent, token_place[None], token_order[None], vin
+    )
+    cot_got = lax.ppermute(cot_send, "col", [(i, (i + 2) % 4) for i in range(4)])
     q, k, v, mixed, lse = attend_fwd(lo, hi, start, end, tok.reshape(tok_rows, D), w_qkv, bqv)
-    own_tok = lax.dynamic_index_in_dim(tok, col, axis=0, keepdims=False)
-    out, g1, gmix, dwo, dwin, dwout, dvec, dbin = middle(
-        mixed.reshape(4, own_rows, FEAT), own_tok, cot, wo, win, wout, vec, b_in
+    back, g1, gmix, dwo, g_in, g_out, dvec, dbin = middle(
+        rows, mixed.reshape(4, own_rows, FEAT), own_tok, cot_own, cot_got, wo, win, wout, vec, b_in, rank
     )
     dqkv = attend_bwd(lo, hi, start, end, q, k, v, gmix.reshape(tok_rows, FEAT), lse)
-    output, input_grad, gw, gff, gvec, gwide = depart(
-        rows, out, g1, dqkv, w_qkv, tok, rank,
-        dwo.reshape(rows, -1, FEAT), dwin.reshape(rows, -1, D), dwout.reshape(rows, -1, D), dvec, dbin,
+    output, input_grad, gq, gk, gv, go, gvec, gwide = depart(
+        rows, back, g1, dqkv, w_qkv, tok, rank, dwo.reshape(rows, -1, FEAT), dvec, dbin
     )
     small, wide = query_bias.shape[0], inner_bias.shape[0]
     return (
-        output, input_grad,
-        gw[:, :192], gw[:, 192:384], gw[:, 384:576], gw[:, 576:].T,
-        gff[:, :D], gff[:, D:].T,
+        output, input_grad, gq, gk, gv, go, g_in, g_out,
         gwide[1, :small], gwide[2, :small], gvec[1, :small], gwide[0, :wide],
         gvec[2, :small], gvec[3, :small], gvec[4, :small], gvec[5, :small], gvec[6, :small],
     )

time: 440 us -> 415 us (0.943); the launches traced: 440 us -> 409 us
  Pallas kernels: 393 us -> 350 us
  waiting for transfers between devices: 0.51 us -> 9.24 us
    pallas_call x1, Pallas kernels: 143 us -> 73.2 us  [depart(): pl.pallas_call(functools.partial(depart_body, rows), out_shape=(S((own_ro...]
    pallas_call x1, Pallas kernels: 118 us -> 148 us  [middle(): pl.pallas_call(functools.partial(middle_body, rows), out_shape=(S((1, row...]
    unnamed x56 -> x51, local copies, waits for them, and re-layouts: 6.79 us -> 16.9 us
    all_gather x1, waiting for transfers between devices: 0.49 us -> 9.22 us  [per_device(): pack = lax.all_gather(pack, 'row', axis=0, tiled=True)]
    pallas_call x1, Pallas kernels: 82.8 us -> 76.7 us  [arrive(): pl.pallas_call(functools.partial(arrive_body, rows), out_shape=(S((4, own...]
  transfers between devices with their start and end apart: 1 -> 2, of which waited for: 1 -> 1; matrix products, arithmetic and copies ran while one was open for 3% -> 3% of each run, Pallas kernels for 19% -> 25%
where the time goes in v3:
time: 415 us; the launch traced here: 409 us
  Pallas kernels  350 us (84%)
  local copies, waits for them, and re-layouts  33.7 us (8%)
  between operations  14.3 us (3%)
  waiting for transfers between devices  9.24 us (2%)
    pallas_call x1, Pallas kernels, middle(): pl.pallas_call(functools.partial(middle_body, rows), out_shape=(S((1, row...  148 us
    pallas_call x1, Pallas kernels, arrive(): pl.pallas_call(functools.partial(arrive_body, rows), out_shape=(S((4, own...  76.7 us
    pallas_call x1, Pallas kernels, depart(): pl.pallas_call(functools.partial(depart_body, rows), out_shape=(S((own_ro...  73.2 us
    pallas_call x1, Pallas kernels, attend_bwd(): pl.pallas_call(attend_bwd_body, out_shape=jax.ShapeDtypeStruct((rows, 3 *...  28.9 us
    pallas_call x1, Pallas kernels, attend_fwd(): pl.pallas_call(attend_fwd_body, out_shape=(part, part, part, part, jax.Sh...  24 us
    unnamed x51, local copies, waits for them, and re-layouts  16.9 us
    all_gather x1, waiting for transfers between devices, per_device(): pack = lax.all_gather(pack, 'row', axis=0, tiled=True)  9.22 us
  transfers between devices with their start and end apart: 2, of which 1 were waited for; matrix products, arithmetic and copies ran while one was open for 3% of the time, Pallas kernels for 25%

profile of v3, /device:TPU:0, one launch (start us, length us, event | category | flops | bytes accessed | tf_op | source)
XLA Modules:
  0.0 409.4 jit_solution(7664030643679125860)
XLA Ops:
  7.2 0.9 copy.39
  8.1 1.9 concatenate.7
  10.1 6.1 %concatenate.6 = bf16[288]{0:T(512)(128)(2,1)S(1)} concatenate(bf16[24]{0:T(256)(128)(2,1)} %param.31, bf16[24]{0:T(256)(128)(2,1)} %param.32, bf16[24]{0:T(256)(128)(2,1)} %param.33, bf16[24]{0:T(256)(128)(2,1)} %param.36, bf16[24]{0:T(256)(128)(2,1)} %param.37, bf16[24]{0:T(256)(128)(2,1)} %param.35, bf16[24]{0:T(256)(128)(2,1)} %param.38, bf16[24]{0:T(256)(128)(2,1)} %param.39, ...), dimensions={0} | concatenate | bytes 1152 | tf_op jit(solution)/shard_map/concatenate | solution.py:1082
  16.2 0.6 broadcast_in_dim.28.vin_ref
  16.8 76.7 %arrive.1 = (bf16[4,512,768]{2,1,0:T(8,128)(2,1)}, bf16[512,768]{1,0:T(8,128)(2,1)}, bf16[512,384]{1,0:T(8,128)(2,1)}, bf16[512,384]{1,0:T(8,128)(2,1)}, f32[8,2...) custom-call(f32[512,768]{1,0:T(8,128)} %x_ref.1, f32[512,768]{1,0:T(8,128)} %g_ref.1, ...), custom_call_target="tpu_custom_call" | custom-call | flops 60000002048 | bytes 20000000 | tf_op jit(solution)/shard_map/arrive/pallas_call | solution.py:530
  93.5 1.3 collective-permute-start
  94.8 0.2 reduce-window.4
  95.4 9.2 %all-gather.2.cloned.1.call-done = bf16[768,2304]{1,0:T(8,128)(2,1)} async-done(((bf16[96,2304]{1,0:T(8,128)(2,1)}), bf16[768,2304]{1,0:T(8,128)(2,1)}) %all-gather.2.cloned.1.call-update) | async-done | bytes 3538960 | tf_op jit(solution)/shard_map/all_gather | solution.py:1080
  104.7 1.3 slice.60.w_ref
  106.0 2.2 copy-done.1
  108.2 24.0 %attend_fwd.1 = (bf16[2048,192]{1,0:T(8,128)(2,1)S(1)}, bf16[2048,192]{1,0:T(8,128)(2,1)S(1)}, bf16[2048,192]{1,0:T(8,128)(2,1)S(1)}, bf16[2048,192]{1,0:T(8,128)(2,1)S(1)}, f32[8,2048]{1,0:T(8,128)S(1)}) custom-call(s32[8]{0:T(128)S(1)} %get-tuple-element.122.lo_ref, s32[8]{0:T(128)S(1)} %get-tuple-element.121.hi_ref, s32[1,2048]{1,0:T(1,128)S(1)} %bitcast.38, ...), custom_call_target="tpu_custom_call" | custom-call | flops 8000000000 | bytes 8000000 | tf_op jit(solution)/shard_map/attend_fwd/pallas_call | solution.py:106
  132.3 1.1 slice.61.wo_ref
  133.4 1.7 fusion.1
  135.2 0.8 copy-done.19
  135.9 147.6 %middle.1 = (bf16[1,8,2,128,384]{4,3,2,1,0:T(8,128)(2,1)}, bf16[4,512,768]{2,1,0:T(8,128)(2,1)}, bf16[4,512,192]{2,1,0:T(8,128)(2,1)}, f32[768,192]{1,0:T(8,128)...) custom-call(bf16[4,512,192]{2,1,0:T(8,128)(2,1)} %bitcast.41, ...), custom_call_target="tpu_custom_call" | custom-call | flops 80000000000 | bytes 20000000 | tf_op jit(solution)/shard_map/middle/pallas_call | solution.py:804
  283.5 1.2 copy-done.3
  284.8 1.2 copy-done.5
  286.0 1.2 copy-done.7
  287.2 1.2 copy-done.9
  288.4 28.9 %attend_bwd.1.dqkv_ref = bf16[2048,576]{1,0:T(8,128)(2,1)} custom-call(s32[8]{0:T(128)S(1)} %get-tuple-element.122.lo_ref, s32[8]{0:T(128)S(1)} %get-tuple-element.121.hi_ref, s32[1,2048]{1,0:T(1,128)S(1)} %bitcast.39, s32[1,2048]{1,0:T(1,128)S(1)} %bitcast.37, bf16[2048,192]{1,0:T(8,128)(2,1)S(1)} %copy-done.5, bf16[2048,192]{1,0:T(8,128)(2,1)S(1)} %copy-done.7, ...), custom_call_target="tpu_custom_call" | custom-call | flops 20000000000 | bytes 6000000 | tf_op jit(solution)/shard_map/attend_bwd/pallas_call | solution.py:183
  317.4 73.2 %depart.1 = (f32[512,768]{1,0:T(8,128)}, f32[512,768]{1,0:T(8,128)}, f32[96,192]{1,0:T(8,128)}, f32[96,192]{1,0:T(8,128)}, f32[96,192]{1,0:T(8,128)}, /*index=5*...) custom-call(bf16[1,8,2,128,384]{4,3,2,1,0:T(8,128)(2,1)} %get-tuple-element.55.back_ref, ...), custom_call_target="tpu_custom_call" | custom-call | flops 60000002048 | bytes 20000000 | tf_op jit(solution)/shard_map/depart/pallas_call | solution.py:1037
  390.6 1.2 slice_bitcast_fusion.5
  391.7 1.3 slice_bitcast_fusion.7
  393.0 1.4 slice_bitcast_fusion
  394.5 0.9 copy.40
  395.3 2.8 copy.48
  398.1 1.1 copy.49
  399.3 0.6 copy.50
  399.9 0.6 copy.51
  400.6 0.6 copy.52
  401.2 0.6 copy.53
  401.9 0.7 copy.54
  (46 shorter events, 0.5 us)
Async XLA Ops:
  7.2 97.5 %all-gather.2.cloned.1.call-start = ((), (), s32[]{:S(2)}) async-start(), calls=%async_computation | async-start | bytes 3981312 | tf_op jit(solution)/shard_map/all_gather | solution.py:1080
  16.8 78.0 %copy-start.20 = (s32[1,8]{1,0:T(1,128)S(1)}, s32[1,8]{1,0:T(1,128)}, u32[]{:S(2)}) copy-start(s32[1,8]{1,0:T(1,128)} %param.24) | copy-start | bytes 100
  93.5 12.5 %copy-start.10 = (f32[8,192]{1,0:T(8,128)S(1)}, f32[8,192]{1,0:T(8,128)}, u32[]{:S(2)}) copy-start(f32[8,192]{1,0:T(8,128)} %get-tuple-element.47.b_ref) | copy-start | bytes 18436
  93.5 41.7 %collective-permute-start = (bf16[512,384]{1,0:T(8,128)(2,1)}, bf16[512,384]{1,0:T(8,128)(2,1)S(1)}, u32[]{:S(2)}, u32[]{:S(2)}) collective-permute-start(bf16[512,384]{1,0:T(8,128)(2,1)} %get-tuple-element.51), channel_id=1, source_target_pairs={{0,2},{1,3},{2,0},{3,1},{4,6},{5,7},{6,4},{7,5},{8,10},{9,11},{10,... | collective-permute-start | bytes 1179656 | tf_op jit(solution)/shard_map/ppermute | solution.py:1101
  106.0 26.3 %copy-start = (bf16[768,576]{1,0:T(8,128)(2,1)}, bf16[768,576]{1,0:T(8,128)(2,1)S(1)}, u32[]{:S(2)}) copy-start(bf16[768,576]{1,0:T(8,128)(2,1)S(1)} %slice.60.w_ref) | copy-start | bytes 2654212
  106.0 2.2 copy-start.1
  108.2 24.0 %copy-start.11 = (bf16[768,2304]{1,0:T(8,128)(2,1)S(1)}, bf16[768,2304]{1,0:T(8,128)(2,1)}, u32[]{:S(2)}) copy-start(bf16[768,2304]{1,0:T(8,128)(2,1)} %all-gather.2.cloned.1.call-done) | copy-start | bytes 10616836
  132.3 2.9 copy-start.2
  132.3 2.9 copy-start.4
  132.3 2.9 copy-start.6
  132.3 2.8 copy-start.8
  135.2 0.8 copy-start.19
  283.5 1.2 copy-start.3
  284.8 1.2 copy-start.5
  286.0 1.2 copy-start.7
  287.2 1.2 copy-start.9
  317.4 77.1 %copy-start.13 = (f32[768,96]{1,0:T(8,128)S(1)}, f32[768,96]{1,0:T(8,128)}, u32[]{:S(2)}) copy-start(f32[768,96]{1,0:T(8,128)} %get-tuple-element.99) | copy-start | bytes 884740
  395.3 2.8 copy-start.12
  398.1 1.2 copy-start.18
  398.1 1.8 copy-start.17
  398.1 2.5 copy-start.16
  398.1 3.1 copy-start.15
  398.1 3.7 copy-start.14
Sparse Core Ops, SparseCore 0:
  10.8 93.8 all-gather.1

commit v4 on v3

--- a/solution.py
+++ b/solution.py
@@ -12,7 +12,7 @@
 FEAT = 192
 HEADS = 3
 QB = 256
-KB = 256
+WINS = (384, 512, 640, 768, 1024, 1408)
 
 norm_eps = 1e-12
 root_half = 0.7071067811865476
@@ -25,6 +25,7 @@
 bf16 = jnp.bfloat16
 VM = pl.BlockSpec(memory_space=pltpu.VMEM)
 SM = pl.BlockSpec(memory_space=pltpu.SMEM)
+ANY = pl.BlockSpec(memory_space=pl.ANY)
 
 
 def mm(a, b, dims):
@@ -35,167 +36,176 @@
     return lax.broadcasted_iota(jnp.int32, (rows, FEAT), 1) // HD
 
 
-def attend_fwd_body(
-    lo_ref, hi_ref, start_ref, end_ref, tok_ref, w_ref, b_ref, q_ref, k_ref, v_ref, mix_ref, lse_ref, s_buf,
-):
+def sequence_of(lens_ref, pos):
+    start, end, run = jnp.zeros_like(pos), jnp.zeros_like(pos), 0
+    for i in range(lens_ref.shape[1]):
+        length = lens_ref[0, i]
+        end = end + jnp.where(pos >= run, length, 0)
+        run = run + length
+        start = start + jnp.where(pos >= run, length, 0)
+    return start, end
+
+
+def for_window(lens_ref, qb, rows, body):
+    first = sequence_of(lens_ref, qb * QB)[0] // 128 * 128
+    span = sequence_of(lens_ref, qb * QB + QB - 1)[1] - first
+    for less, win in zip((0,) + WINS, WINS):
+
+        @pl.when((span > less) & (span <= win))
+        def _():
+            body(pl.multiple_of(jnp.minimum(first, rows - win), 128), win)
+
+
+def attend_fwd_body(lens_ref, tok_ref, pack_ref, b_ref, q_ref, k_ref, v_ref, mix_ref, lse_ref, w_ref, sem):
+    fetch = pltpu.make_async_copy(pack_ref, w_ref, sem.at[0])
+    fetch.start()
     scale = HD ** (-0.5)
-    blocks = q_ref.shape[0] // QB
+    total_rows = q_ref.shape[0]
     heads = lane_head(QB)
+    lanes = lax.broadcasted_iota(jnp.int32, (QB, 128), 1)
     b_q, b_v = b_ref[0:1, :], b_ref[1:2, :]
-
-    @pl.loop(0, blocks)
-    def _(qb):
-        rows = pl.ds(qb * QB, QB)
-        out = mm(tok_ref[rows, :], w_ref[...], NN)
+    step = 2 * QB
+    fetch.wait()
+
+    @pl.loop(0, total_rows // step)
+    def _(i):
+        rows = pl.ds(pl.multiple_of(i * step, step), step)
+        out = mm(tok_ref[rows, :], w_ref[:, : 3 * FEAT], NN)
         q_ref[rows, :] = (out[:, :FEAT] + b_q).astype(bf16)
         k_ref[rows, :] = out[:, FEAT : 2 * FEAT].astype(bf16)
         v_ref[rows, :] = (out[:, 2 * FEAT :] + b_v).astype(bf16)
 
-    @pl.loop(0, blocks)
+    def by_head(parts):
+        return jnp.where(heads == 0, parts[0], jnp.where(heads == 1, parts[1], parts[2]))
+
+    @pl.loop(0, total_rows // QB)
     def _(qb):
-        rows = pl.ds(qb * QB, QB)
-        qv = q_ref[rows, :]
-        qs = [jnp.where(heads == h, qv, jnp.zeros_like(qv)) for h in range(HEADS)]
-        q_start = start_ref[:, rows]
-        q_end = end_ref[:, rows]
-        lo, hi = lo_ref[qb], hi_ref[qb]
-
-        def scores(kb, tops):
-            keys = pl.ds(pl.multiple_of(kb * KB, KB), KB)
-            kv = k_ref[keys, :]
-            pos = lax.broadcasted_iota(jnp.int32, (KB, QB), 0) + kb * KB
-            allowed = (pos >= q_start) & (pos < q_end)
-            out = []
+        rows = pl.ds(pl.multiple_of(qb * QB, QB), QB)
+        start, end = sequence_of(lens_ref, lax.broadcasted_iota(jnp.int32, (QB, 1), 0) + qb * QB)
+
+        def window(at, win):
+            qv = q_ref[rows, :] * scale
+            kv, vv = k_ref[pl.ds(at, win), :], v_ref[pl.ds(at, win), :]
+            pos = lax.broadcasted_iota(jnp.int32, (QB, win), 1) + at
+            allowed = (pos >= start) & (pos < end)
+            scores = [
+                jnp.where(allowed, mm(jnp.where(heads == h, qv, jnp.zeros_like(qv)), kv, NT), -1e30)
+                for h in range(HEADS)
+            ]
+            tops = [jnp.max(s, axis=1, keepdims=True) for s in scores]
+            weights = [jnp.exp(scores[h] - tops[h]) for h in range(HEADS)]
+            totals = [jnp.sum(e, axis=1, keepdims=True) for e in weights]
+            mixed = by_head([mm(weights[h].astype(bf16), vv, NN) for h in range(HEADS)])
+            mix_ref[rows, :] = (mixed / by_head(totals)).astype(bf16)
+            lse = jnp.zeros((QB, 128), f32)
             for h in range(HEADS):
-                s = jnp.where(allowed, mm(kv, qs[h], NT) * scale, -1e30)
-                s_buf[h, keys, :] = s
-                out.append(jnp.maximum(tops[h], jnp.max(s, axis=0, keepdims=True)))
-            return tuple(out)
-
-        tops = lax.fori_loop(lo, hi, scores, tuple(jnp.full((1, QB), -1e30, f32) for _ in range(HEADS)))
-
-        def weigh(kb, sums):
-            keys = pl.ds(pl.multiple_of(kb * KB, KB), KB)
-            out = []
-            for h in range(HEADS):
-                e = jnp.exp(s_buf[h, keys, :] - tops[h])
-                s_buf[h, keys, :] = e
-                out.append(sums[h] + jnp.sum(e, axis=0, keepdims=True))
-            return tuple(out)
-
-        sums = lax.fori_loop(lo, hi, weigh, tuple(jnp.zeros((1, QB), f32) for _ in range(HEADS)))
-        inv = [1.0 / s for s in sums]
-
-        def mix(kb, acc):
-            keys = pl.ds(pl.multiple_of(kb * KB, KB), KB)
-            vv = v_ref[keys, :]
-            for h in range(HEADS):
-                p = (s_buf[h, keys, :] * inv[h]).astype(bf16)
-                acc = acc + jnp.where(heads == h, mm(p, vv, TN), 0.0)
-            return acc
-
-        acc = lax.fori_loop(lo, hi, mix, jnp.zeros((QB, FEAT), f32))
-        mix_ref[rows, :] = acc.astype(bf16)
-        for h in range(HEADS):
-            lse_ref[pl.ds(h, 1), rows] = tops[h] + jnp.log(sums[h])
-
-
-def attend_fwd(lo, hi, start, end, tokens, w_qkv, bias):
+                lse = jnp.where(lanes == h, tops[h] + jnp.log(totals[h]), lse)
+            lse_ref[:, rows] = lse.T[:8]
+
+        for_window(lens_ref, qb, total_rows, window)
+
+
+def attend_fwd(lens, tokens, pack, bias):
     rows = tokens.shape[0]
     part = jax.ShapeDtypeStruct((rows, FEAT), bf16)
     return pl.pallas_call(
         attend_fwd_body,
         out_shape=(part, part, part, part, jax.ShapeDtypeStruct((8, rows), f32)),
-        in_specs=[SM, SM] + [VM] * 5,
+        in_specs=[SM, VM, ANY, VM],
         out_specs=(VM,) * 5,
-        scratch_shapes=[pltpu.VMEM((HEADS, rows, QB), f32)],
+        scratch_shapes=[pltpu.VMEM((D, D), bf16), pltpu.SemaphoreType.DMA((1,))],
         name="attend_fwd",
-        compiler_params=pltpu.CompilerParams(vmem_limit_bytes=40 << 20),
+        compiler_params=pltpu.CompilerParams(vmem_limit_bytes=62 << 20),
         cost_estimate=pl.CostEstimate(flops=8_000_000_000, bytes_accessed=8_000_000, transcendentals=4_000_000),
-    )(lo, hi, start, end, tokens, w_qkv, bias)
+    )(lens, tokens, pack, bias)
 
 
 def attend_bwd_body(
-    lo_ref, hi_ref, start_ref, end_ref, q_ref, k_ref, v_ref, do_ref, lse_ref,
-    dqkv_ref, p_buf, dp_buf, dq_acc, dk_acc, dv_acc,
+    lens_ref, q_in, k_in, v_in, mix_in, lse_in, do_ref, dqkv_ref,
+    k_ref, q_ref, v_ref, mix_ref, lse_ref, k_turned, dq_acc, dk_acc, dv_acc, fetch_sem,
 ):
+    fetches = [
+        pltpu.make_async_copy(src, dst, fetch_sem.at[i])
+        for i, (src, dst) in enumerate(
+            ((k_in, k_ref), (q_in, q_ref), (v_in, v_ref), (mix_in, mix_ref), (lse_in, lse_ref))
+        )
+    ]
+    for fetch in fetches:
+        fetch.start()
     scale = HD ** (-0.5)
-    blocks = q_ref.shape[0] // QB
+    total_rows = q_ref.shape[0]
+    blocks = total_rows // QB
     heads = lane_head(QB)
-    key_heads = lane_head(KB)
     dk_acc[...] = jnp.zeros_like(dk_acc)
     dv_acc[...] = jnp.zeros_like(dv_acc)
+    fetches[0].wait()
 
     @pl.loop(0, blocks)
     def _(qb):
-        rows = pl.ds(qb * QB, QB)
-        qv = q_ref[rows, :]
-        dv_in = do_ref[rows, :]
-        qs = [jnp.where(heads == h, qv, jnp.zeros_like(qv)) for h in range(HEADS)]
-        dos = [jnp.where(heads == h, dv_in, jnp.zeros_like(dv_in)) for h in range(HEADS)]
-        q_start = start_ref[:, rows]
-        q_end = end_ref[:, rows]
-        lse = [lse_ref[pl.ds(h, 1), rows] for h in range(HEADS)]
-        lo, hi = lo_ref[qb], hi_ref[qb]
-
-        def first(kb, sums):
-            keys = pl.ds(pl.multiple_of(kb * KB, KB), KB)
-            kv, vv = k_ref[keys, :], v_ref[keys, :]
-            pos = lax.broadcasted_iota(jnp.int32, (KB, QB), 0) + kb * KB
-            allowed = (pos >= q_start) & (pos < q_end)
-            out = []
-            grad_v = dv_acc[keys, :]
-            for h in range(HEADS):
-                p = jnp.where(allowed, jnp.exp(mm(kv, qs[h], NT) * scale - lse[h]), 0.0)
-                dp = mm(vv, dos[h], NT)
-                p_buf[h, keys, :] = p
-                dp_buf[h, keys, :] = dp
-                out.append(sums[h] + jnp.sum(p * dp, axis=0, keepdims=True))
-                grad_v = grad_v + mm(p.astype(bf16), dos[h], NN)
-            dv_acc[keys, :] = grad_v
-            return tuple(out)
-
-        sums = lax.fori_loop(lo, hi, first, tuple(jnp.zeros((1, QB), f32) for _ in range(HEADS)))
-
-        def second(kb, acc):
-            keys = pl.ds(pl.multiple_of(kb * KB, KB), KB)
-            kv = k_ref[keys, :]
-            grad_k = dk_acc[keys, :]
-            for h in range(HEADS):
-                ds = (p_buf[h, keys, :] * (dp_buf[h, keys, :] - sums[h])).astype(bf16)
-                grad_k = grad_k + mm(ds, qs[h], NN)
-                acc = acc + jnp.where(heads == h, mm(ds, kv, TN), 0.0)
-            dk_acc[keys, :] = grad_k
-            return acc
-
-        acc = lax.fori_loop(lo, hi, second, jnp.zeros((QB, FEAT), f32))
-        dq_acc[rows, :] = acc
+        rows = pl.ds(pl.multiple_of(qb * QB, QB), QB)
+        k_turned[:, rows] = k_ref[rows, :].T
+
+    for fetch in fetches[1:]:
+        fetch.wait()
 
     @pl.loop(0, blocks)
     def _(qb):
-        rows = pl.ds(qb * QB, QB)
-        parts = [dq_acc[rows, :] * scale, dk_acc[rows, :] * scale, dv_acc[rows, :]]
+        rows = pl.ds(pl.multiple_of(qb * QB, QB), QB)
+        start, end = sequence_of(lens_ref, lax.broadcasted_iota(jnp.int32, (1, QB), 1) + qb * QB)
+
+        def window(at, win):
+            qv = q_ref[rows, :] * scale
+            do = do_ref[rows, :]
+            along = (do.astype(f32) * mix_ref[rows, :].astype(f32)).T
+            keys = pl.ds(at, win)
+            kv, vv = k_ref[keys, :], v_ref[keys, :]
+            pos = lax.broadcasted_iota(jnp.int32, (win, QB), 0) + at
+            allowed = (pos >= start) & (pos < end)
+            each = range(HEADS)
+            qs = [jnp.where(heads == h, qv, jnp.zeros_like(qv)) for h in each]
+            dos = [jnp.where(heads == h, do, jnp.zeros_like(do)) for h in each]
+            inner = [jnp.sum(along[h * HD : (h + 1) * HD], axis=0, keepdims=True) for h in each]
+            scores = [mm(kv, qs[h], NT) for h in each]
+            probs = [jnp.where(allowed, jnp.exp(scores[h] - lse_ref[h : h + 1, rows]), 0.0) for h in each]
+            dps = [mm(vv, dos[h], NT) for h in each]
+            lows = [p.astype(bf16) for p in probs]
+            dss = [(probs[h] * (dps[h] - inner[h])).astype(bf16) for h in each]
+            grad_v = sum([mm(lows[h], dos[h], NN) for h in each])
+            grad_k = sum([mm(dss[h], qs[h], NN) for h in each])
+            grad_q = [mm(k_turned[h * HD : (h + 1) * HD, keys], dss[h], NN) for h in each]
+            dk_acc[keys, :] += grad_k
+            dv_acc[keys, :] += grad_v
+            dq_acc[rows, :] = jnp.concatenate(grad_q, axis=0).T
+
+        for_window(lens_ref, qb, total_rows, window)
+
+    @pl.loop(0, blocks)
+    def _(qb):
+        rows = pl.ds(pl.multiple_of(qb * QB, QB), QB)
+        parts = [dq_acc[rows, :] * scale, dk_acc[rows, :], dv_acc[rows, :]]
         dqkv_ref[rows, :] = jnp.concatenate([p.astype(bf16) for p in parts], axis=1)
 
 
-def attend_bwd(lo, hi, start, end, q, k, v, do, lse):
+def attend_bwd(lens, q, k, v, mixed, do, lse):
     rows = q.shape[0]
     return pl.pallas_call(
         attend_bwd_body,
         out_shape=jax.ShapeDtypeStruct((rows, 3 * FEAT), bf16),
-        in_specs=[SM, SM] + [VM] * 7,
+        in_specs=[SM] + [ANY] * 5 + [VM],
         out_specs=VM,
-        scratch_shapes=[
-            pltpu.VMEM((HEADS, rows, QB), f32),
-            pltpu.VMEM((HEADS, rows, QB), f32),
+        scratch_shapes=[pltpu.VMEM((rows, FEAT), bf16)] * 4
+        + [
+            pltpu.VMEM((8, rows), f32),
+            pltpu.VMEM((FEAT, rows), bf16),
             pltpu.VMEM((rows, FEAT), f32),
             pltpu.VMEM((rows, FEAT), f32),
             pltpu.VMEM((rows, FEAT), f32),
+            pltpu.SemaphoreType.DMA((5,)),
         ],
         name="attend_bwd",
-        compiler_params=pltpu.CompilerParams(vmem_limit_bytes=48 << 20),
+        compiler_params=pltpu.CompilerParams(vmem_limit_bytes=62 << 20),
         cost_estimate=pl.CostEstimate(flops=20_000_000_000, bytes_accessed=6_000_000, transcendentals=4_000_000),
-    )(lo, hi, start, end, q, k, v, do, lse)
+    )(lens, q, k, v, mixed, lse, do)
 
 
 def remote(src, dst, send_sem, recv_sem, device):
@@ -278,6 +288,49 @@
 def picker_cols(rank, count):
     have = lax.broadcasted_iota(jnp.int32, (rank.shape[0], count), 1).astype(f32)
     return jnp.where(rank == have, 1.0, 0.0).astype(bf16)
+
+
+def ring_spot(row, rows):
+    return jnp.where(row % 2 == 0, row // 2, rows - 1 - row // 2)
+
+
+def ring_row(spot, rows):
+    spot = (spot + rows) % rows
+    return jnp.where(spot < rows // 2, 2 * spot, 2 * (rows - 1 - spot) + 1)
+
+
+class RingGather:
+    def __init__(self, rows, place, sems):
+        self.rows, self.hops, self.place = rows, rows // 2, place
+        self.send, self.recv = sems
+        self.r, self.c = lax.axis_index("row"), lax.axis_index("col")
+        self.spot = ring_spot(self.r, rows)
+
+    def copy(self, way, t):
+        step, to = (self.rows - t, 1) if way == 0 else (t, self.rows - 1)
+        v = self.place(ring_row(self.spot + step, self.rows))
+        return remote(v, v, self.send.at[way, t], self.recv.at[way, t], (ring_row(self.spot + to, self.rows), self.c))
+
+    def start(self):
+        for way in range(2):
+            if self.hops > way:
+                self.copy(way, 0).start()
+
+    def hop(self, t):
+        for way in range(2):
+            if t < self.hops - way:
+                self.copy(way, t - 1).wait_recv()
+                self.copy(way, t).start()
+
+    def done(self):
+        for way in range(2):
+            if self.hops > way:
+                self.copy(way, self.hops - way - 1).wait_recv()
+
+    def finish(self):
+        for way in range(2):
+            for t in range(self.hops - way):
+                self.copy(way, t).wait_send()
 
 
 def placed(rank_col, got):
@@ -307,6 +360,10 @@
         v = self.xin.at[self.a, self.nbr]
         return remote(v, v, self.fwd_s.at[self.a], self.fwd_r.at[self.a], (self.r, self.sib))
 
+    def start_split(self):
+        self.to_nbr().start()
+        self.to_sib().start()
+
     def split(self, ref):
         self.xout[self.a] = ref[:, half_lanes(1 - self.h)].astype(bf16)
         self.to_nbr().start()
@@ -387,13 +444,13 @@
 
 
 def arrive_body(
-    rows, x_ref, g_ref, place_ref, order_ref, vin_ref,
-    tok_ref, own_ref, cot_ref, cot_send, rank_ref, vec_ref, bqv_ref, bin_ref,
+    rows, x_ref, g_ref, place_ref, order_ref, vin_ref, part_ref,
+    pack_ref, tok_ref, own_ref, cot_ref, cot_send, rank_ref, vec_ref, bqv_ref, bin_ref,
     *scratch,
 ):
     bufs, sems = scratch[:4], scratch[4:14]
     key_g, key_w, col_g, col_w, vbuf = scratch[14:19]
-    an_s, an_r, as_s, as_r, af_s, af_r, vr_s, vr_r, vc_s, vc_r = scratch[19:]
+    an_s, an_r, as_s, as_r, af_s, af_r, vr_s, vr_r, vc_s, vc_r, w_s, w_r = scratch[19:]
     r, c, sib, nbr, diag = col_peers()
     h = c // 2
     own_rows = x_ref.shape[0]
@@ -403,6 +460,9 @@
 
     first, second = Deal(0, rows, bufs, sems), Deal(1, rows, bufs, sems)
     first.split(x_ref)
+    ring = RingGather(rows, lambda b: pack_ref.at[b], (w_s, w_r))
+    pack_ref[r] = part_ref[...]
+    ring.start()
     second.split(g_ref)
 
     def vec_row(i):
@@ -425,10 +485,14 @@
     to_col(key_g, col_g)
     to_col(key_w, col_w)
     rank_ref[0:1, :] = rank_row(key_g, col_g)
+    if ring.hops > 1:
+        ring.hop(1)
     rank_ref[1:2, :] = rank_row(key_w, col_w)
     rank_g = rank_ref[0:1, :]
     key_w[...] = rank_ref[1:2, :]
     to_col(key_w, col_w)
+    for t in range(2, ring.hops):
+        ring.hop(t)
 
     first.joined()
     first.pick_and_send(rank_g)
@@ -509,6 +573,8 @@
             tok_copy(qi, q, k, 1 - h, af_s, af_r, sib).wait_send()
 
     own_ref[...] = tok_ref[c]
+    ring.done()
+    ring.finish()
 
     for deal in (first, second):
         deal.joined_sent()
@@ -522,7 +588,7 @@
         vec_col(i, peer).wait_send()
 
 
-def arrive(rows, x, g, place, order, vin):
+def arrive(rows, x, g, place, order, vin, part):
     own_rows = x.shape[0]
     tokens = 4 * own_rows
     chunks = own_rows // CH
@@ -530,12 +596,12 @@
     return pl.pallas_call(
         functools.partial(arrive_body, rows),
         out_shape=(
-            S((4, own_rows, D), bf16), S((own_rows, D), bf16),
+            S((rows, D // rows, D), bf16), S((4, own_rows, D), bf16), S((own_rows, D), bf16),
             S((own_rows, HALF), bf16), S((own_rows, HALF), bf16), S((8, tokens), f32),
             S((8, D), f32), S((8, FEAT), f32), S((1, D), f32),
         ),
-        in_specs=[VM] * 5,
-        out_specs=(VM,) * 8,
+        in_specs=[VM] * 6,
+        out_specs=(VM,) * 9,
         scratch_shapes=deal_scratch(rows, own_rows, 2)
         + deal_sems(rows, 2)
         + [
@@ -544,20 +610,12 @@
         ]
         + [DS((2, chunks))] * 6
         + [DS((rows,))] * 2
-        + [DS((3,))] * 2,
+        + [DS((3,))] * 2
+        + [DS((2, rows // 2))] * 2,
         name="arrive",
-        compiler_params=pltpu.CompilerParams(collective_id=1, has_side_effects=True, vmem_limit_bytes=56 << 20),
+        compiler_params=pltpu.CompilerParams(collective_id=1, has_side_effects=True, vmem_limit_bytes=62 << 20),
         cost_estimate=pl.CostEstimate(flops=60_000_000_000, bytes_accessed=20_000_000, transcendentals=0),
-    )(x, g, place, order, vin)
-
-
-def ring_spot(row, rows):
-    return jnp.where(row % 2 == 0, row // 2, rows - 1 - row // 2)
-
-
-def ring_row(spot, rows):
-    spot = (spot + rows) % rows
-    return jnp.where(spot < rows // 2, 2 * spot, 2 * (rows - 1 - spot) + 1)
+    )(x, g, place, order, vin, part)
 
 
 class Ring:
@@ -608,22 +666,35 @@
 
 
 def middle_body(
-    rows, mixed_ref, tok_ref, cot_own, cot_got, wo_ref, win_ref, wout_ref, vec_ref, bin_ref, rank_ref,
+    rows, mixed_ref, tok_ref, cot_own, cot_got, pack_ref, ff_ref, vec_ref, bin_ref, rank_ref,
     back_ref, g1_ref, gmix_ref, dwo_ref, gin_ref, gout_ref, dvec_ref, dbin_ref,
     *scratch,
 ):
     nfull, hidden, slope, g2full, own, d2ds, d2dr, xs, xr, hat1, inv1, grad2, dwin, dwout = scratch[:14]
-    out_buf, xin, xout, sbuf, ring_out, ring_in = scratch[14:20]
-    ds_s, ds_r, x_s, x_r, asib_s, asib_r, anbr_s, anbr_r, afwd_s, afwd_r, q_s, q_r = scratch[20:32]
+    wo_ref, attn_w, ff_all, wide, w_sem, wr_s, wr_r, xin, xout, sbuf, ring_out, ring_in = scratch[14:26]
+    ds_s, ds_r, x_s, x_r, asib_s, asib_r, anbr_s, anbr_r, afwd_s, afwd_r, q_s, q_r = scratch[26:38]
     r, c, sib, nbr, diag = col_peers()
     h = c // 2
-    chunks = out_buf.shape[0] // CH
+    chunks = tok_ref.shape[0] // CH
     block = D // rows
+    fetch = pltpu.make_async_copy(pack_ref, attn_w, w_sem.at[0])
+    fetch.start()
     greet((sib, nbr), rows, r, c)
-    outs = Deal(0, rows, (xin, xout, sbuf, back_ref), scratch[32:])
+    ff_ring = RingGather(rows, lambda b: ff_all.at[b], (wr_s, wr_r))
+    ff_all[r] = ff_ref[...]
+    ff_ring.start()
+    fetch.wait()
+    wo_ref[...] = attn_w[:, 3 * FEAT :]
+    outs = Deal(0, rows, (xin, xout, sbuf, back_ref), scratch[38:])
     ring = Ring(rows, lambda b: jnp.concatenate([dwin[b], dwout[b]], axis=1), ring_out, ring_in, (q_s, q_r))
 
     bo, g1, s1, b2, g2, s2 = [vec_ref[pl.ds(i, 1), :] for i in range(6)]
+
+    def win():
+        return ff_all[:, :, :D].reshape(D, D) if block % 16 == 0 else attn_w[...]
+
+    def wout():
+        return ff_all[:, :, D:].reshape(D, D) if block % 16 == 0 else wide[...]
 
     def d2d(st, k):
         return remote(d2ds.at[k], d2dr.at[k], ds_s.at[st, k], ds_r.at[st, k], (r, sib))
@@ -678,12 +749,14 @@
     def all_rows(ref, k):
         return ref[:, rows_of(k), :].reshape(4 * CH, ref.shape[2])
 
-    @pl.loop(0, chunks)
-    def _(k):
+    def ff_hops(part):
+        for t in range(1 + part * (ff_ring.hops - 1) // 3, 1 + (part + 1) * (ff_ring.hops - 1) // 3):
+            ff_ring.hop(t)
+
+    def mix_heads(k):
         rs_start(0, k, lambda q: mm(mixed_ref[q, rows_of(k), :], wo_ref[...], NT))
 
-    @pl.loop(0, chunks)
-    def _(k):
+    def first_norm(k):
         resid = rs_end(0, k) + tok_ref[rows_of(k), :].astype(f32) + bo
         hat, inv = norm_rows(resid)
         hat1[k] = hat
@@ -691,15 +764,28 @@
         val = hat * g1 + s1
         ag_start(0, k, val.astype(bf16))
 
+    pl.loop(0, chunks // 2)(mix_heads)
+    ff_hops(0)
+    pl.loop(chunks // 2, chunks)(mix_heads)
+    ff_hops(1)
+    pl.loop(0, chunks // 2)(first_norm)
+    ff_hops(2)
+    pl.loop(chunks // 2, chunks)(first_norm)
+    ff_ring.done()
+    if block % 16 != 0:
+        for b in range(rows):
+            attn_w[b * block : (b + 1) * block, :] = ff_all[b, :, :D]
+            wide[b * block : (b + 1) * block, :] = ff_all[b, :, D:]
+
     @pl.loop(0, chunks)
     def _(k):
         ag_end(0, k)
-        pre = mm(all_rows(nfull, k), win_ref[...], NN) + bin_ref[...]
+        pre = mm(all_rows(nfull, k), win(), NN) + bin_ref[...]
         cum = 0.5 * (1.0 + lax.erf(pre * root_half))
         dens = jnp.exp(-0.5 * pre * pre) * inv_root_two_pi
         hidden[:, rows_of(k), :] = (pre * cum).astype(bf16).reshape(4, CH, D)
         slope[:, rows_of(k), :] = (cum + pre * dens).reshape(4, CH, D)
-        rs_start(1, k, lambda q: mm(hidden[q, rows_of(k), :], wout_ref[...], NT))
+        rs_start(1, k, lambda q: mm(hidden[q, rows_of(k), :], wout(), NT))
 
     dvec_ref[...] = jnp.zeros_like(dvec_ref)
 
@@ -707,7 +793,9 @@
     def _(k):
         resid = rs_end(1, k) + (hat1[k] * g1 + s1) + b2
         hat, inv = norm_rows(resid)
-        out_buf[rows_of(k), :] = (hat * g2 + s2).astype(bf16)
+        low, high = [half.astype(bf16) for half in jnp.split(hat * g2 + s2, 2, axis=1)]
+        xin[0, c, rows_of(k), :] = jnp.where(h == 0, low, high)
+        xout[0, rows_of(k), :] = jnp.where(h == 0, high, low)
         halves = (cot_own[rows_of(k), :], cot_got[rows_of(k), :])
         low, high = jnp.where(h == 0, halves[0], halves[1]), jnp.where(h == 0, halves[1], halves[0])
         cot = jnp.concatenate([low, high], axis=1).astype(f32)
@@ -718,7 +806,7 @@
         dvec_ref[pl.ds(5, 1), :] += jnp.sum(cot * hat, axis=0, keepdims=True)
         dvec_ref[pl.ds(6, 1), :] += jnp.sum(cot, axis=0, keepdims=True)
 
-    outs.split(out_buf)
+    outs.start_split()
     dwin[...] = jnp.zeros_like(dwin)
     dwout[...] = jnp.zeros_like(dwout)
     dwo_ref[...] = jnp.zeros_like(dwo_ref)
@@ -734,12 +822,12 @@
     def back_hidden(k):
         ag_end(1, k)
         g2c = all_rows(g2full, k)
-        grad_pre = mm(g2c, wout_ref[...], NN) * all_rows(slope, k)
+        grad_pre = mm(g2c, wout(), NN) * all_rows(slope, k)
         dbin_ref[...] += jnp.sum(grad_pre, axis=0, keepdims=True)
         low = grad_pre.astype(bf16)
         hid = all_rows(hidden, k)
         hidden[:, rows_of(k), :] = low.reshape(4, CH, D)
-        rs_start(2, k, lambda q: mm(hidden[q, rows_of(k), :], win_ref[...], NT))
+        rs_start(2, k, lambda q: mm(hidden[q, rows_of(k), :], win(), NT))
         add_blocks(dwout, mm(g2c, hid, TN))
         add_blocks(dwin, mm(all_rows(nfull, k), low, TN))
 
@@ -793,9 +881,10 @@
     outs.joined_sent()
     outs.rows_sent()
     ring.finish()
-
-
-def middle(rows, mixed, tok, cot_own, cot_got, wo, win, wout, vec, b_in, rank):
+    ff_ring.finish()
+
+
+def middle(rows, mixed, tok, cot_own, cot_got, pack, ff_part, vec, b_in, rank):
     own_rows = tok.shape[0]
     chunks = own_rows // CH
     block, hops, slots = D // rows, rows // 2, 4 * own_rows // rows
@@ -813,7 +902,7 @@
             S((8, D), f32),
             S((1, D), f32),
         ),
-        in_specs=[VM] * 10,
+        in_specs=[VM] * 4 + [ANY] + [VM] * 4,
         out_specs=(VM,) * 8,
         scratch_shapes=[
             pltpu.VMEM((4, own_rows, D), bf16),
@@ -830,7 +919,13 @@
             pltpu.VMEM((chunks, CH, D), f32),
             V((rows, block, D), f32),
             V((rows, block, D), f32),
-            V((own_rows, D), bf16),
+            V((D, FEAT), bf16),
+            V((D, D), bf16),
+            V((rows, block, 2 * D), bf16),
+            V((8, 128) if block % 16 == 0 else (D, D), bf16),
+            pltpu.SemaphoreType.DMA((1,)),
+            pltpu.SemaphoreType.DMA((2, hops)),
+            pltpu.SemaphoreType.DMA((2, hops)),
         ]
         + deal_scratch(rows, own_rows, 1)[:3]
         + [V((2, hops, block, 2 * D), bf16)] * 2
@@ -840,25 +935,28 @@
         name="middle",
         compiler_params=pltpu.CompilerParams(collective_id=2, has_side_effects=True, vmem_limit_bytes=62 << 20),
         cost_estimate=pl.CostEstimate(flops=80_000_000_000, bytes_accessed=20_000_000, transcendentals=4_000_000),
-    )(mixed, tok, cot_own, cot_got, wo, win, wout, vec, b_in, rank)
+    )(mixed, tok, cot_own, cot_got, pack, ff_part, vec, b_in, rank)
 
 
 def depart_body(
-    rows, back_ref, g1_ref, dqkv_ref, w_ref, tok_ref, rank_ref, dwo_ref, dvec_ref, dbin_ref,
+    rows, back_ref, g1_ref, dqkv_ref, pack_ref, tok_ref, rank_ref, dwo_ref, dvec_ref, dbin_ref,
     out_ref, grad_ref, gq_ref, gk_ref, gv_ref, go_ref, gvec_ref, gwide_ref,
     *scratch,
 ):
     bufs, sems = scratch[:4], scratch[4:14]
     key, col_g, sums, dw = scratch[14:18]
-    d2ds, d2dr, keep, xs, xr, gsend, grecv, r2s, r2r, vmine, vall, vrow = scratch[18:30]
-    ds_s, ds_r, x_s, x_r, fin_s, fin_r, q2_s, q2_r, sh_s, sh_r, vc_s, vc_r, vr_s, vr_r = scratch[30:]
+    d2ds, d2dr, keep, xs, xr, gsend, grecv, r2s, r2r, vmine, vall, vrow, w_ref, w_sem = scratch[18:32]
+    ds_s, ds_r, x_s, x_r, fin_s, fin_r, q2_s, q2_r, sh_s, sh_r, vc_s, vc_r, vr_s, vr_r = scratch[32:]
     r, c, sib, nbr, diag = col_peers()
     h = c // 2
     own_rows = out_ref.shape[0]
     tokens = 4 * own_rows
     chunks = own_rows // CH
     block = D // rows
+    fetch = pltpu.make_async_copy(pack_ref, w_ref, w_sem.at[0])
+    fetch.start()
     greet((sib, nbr, diag), rows, r, c)
+    fetch.wait()
 
     def rows_of(k):
         return pl.ds(pl.multiple_of(k * CH, CH), CH)
@@ -886,7 +984,7 @@
         return remote(xs.at[k], xr.at[k], x_s.at[k], x_r.at[k], (r, nbr))
 
     def part(q, k):
-        return mm(dqkv_ref[token_rows(q, k), :], w_ref[...], NT)
+        return mm(dqkv_ref[token_rows(q, k), :], w_ref[:, : 3 * FEAT], NT)
 
     @pl.loop(0, chunks)
     def _(k):
@@ -943,13 +1041,13 @@
     def own_final(got, ref):
         @pl.loop(0, chunks)
         def _(k):
-            ref[rows_of(k), half_lanes(h)] = placed(col_g[token_rows(c, k), :], got[0])
+            ref[rows_of(k), half_lanes(h)] = placed(col_g[token_rows(c, k), :], got[0]).astype(bf16)
 
     def take_final(i, ref):
         @pl.loop(0, chunks)
         def _(k):
             final(i, k).wait_recv()
-            ref[rows_of(k), half_lanes(1 - h)] = grecv[i, k].astype(f32)
+            ref[rows_of(k), half_lanes(1 - h)] = grecv[i, k]
 
     send_final(0, back_ref)
     if ring.hops > 1:
@@ -1027,7 +1125,7 @@
         vec_row(i).wait_send()
 
 
-def depart(rows, back, g1, dqkv, w_qkv, tok, rank, dwo, dvec, dbin):
+def depart(rows, back, g1, dqkv, pack, tok, rank, dwo, dvec, dbin):
     own_rows = tok.shape[1]
     tokens = 4 * own_rows
     chunks = own_rows // CH
@@ -1037,10 +1135,10 @@
     return pl.pallas_call(
         functools.partial(depart_body, rows),
         out_shape=(
-            S((own_rows, D), f32), S((own_rows, D), f32), third, third, third, S((FEAT, block), f32),
+            S((own_rows, D), bf16), S((own_rows, D), bf16), third, third, third, S((FEAT, block), f32),
             S((8, 128), f32), S((8, 128), f32),
         ),
-        in_specs=[VM] * 9,
+        in_specs=[VM] * 3 + [ANY] + [VM] * 5,
         out_specs=(VM,) * 8,
         scratch_shapes=deal_scratch(rows, own_rows, 1)
         + deal_sems(rows, 1)
@@ -1050,7 +1148,7 @@
             V((chunks, 2, CH, HALF), bf16), V((chunks, 2, CH, HALF), bf16),
             V((2, chunks, CH, HALF), bf16), V((2, chunks, CH, HALF), bf16),
             V((2, hops, block, D), bf16), V((2, hops, block, D), bf16),
-            V((16, D), f32), V((4, 16, D), f32), V((rows, 16, D), f32),
+            V((16, D), f32), V((4, 16, D), f32), V((rows, 16, D), f32), V((D, D), bf16), DS((1,)),
         ]
         + [DS((chunks,))] * 4
         + [DS((2, chunks))] * 2
@@ -1059,9 +1157,60 @@
         + [DS((3,))] * 2
         + [DS((rows,))] * 2,
         name="depart",
-        compiler_params=pltpu.CompilerParams(collective_id=3, has_side_effects=True, vmem_limit_bytes=60 << 20),
+        compiler_params=pltpu.CompilerParams(collective_id=3, has_side_effects=True, vmem_limit_bytes=62 << 20),
         cost_estimate=pl.CostEstimate(flops=60_000_000_000, bytes_accessed=20_000_000, transcendentals=0),
-    )(back, g1, dqkv, w_qkv, tok, rank, dwo, dvec, dbin)
+    )(back, g1, dqkv, pack, tok, rank, dwo, dvec, dbin)
+
+
+def gather_up_body(*refs):
+    weights, vectors, (attn_ref, ff_ref, vin_ref) = refs[:6], refs[6:-3], refs[-3:]
+    q, k, v, o, inner, outer = weights
+    attn_ref[...] = jnp.concatenate([q[...], k[...], v[...], o[...].T], axis=1)
+    ff_ref[:, :D] = inner[...]
+    ff_ref[:, D:] = outer[...].T
+    parts = [ref[...].astype(f32) for ref in vectors]
+    left = HALF - sum(part.shape[1] for part in parts)
+    row = jnp.concatenate(parts + [jnp.zeros((1, left), f32)], axis=1)
+    vin_ref[...] = jnp.broadcast_to(row, vin_ref.shape)
+
+
+def gather_up(weights, vectors):
+    S, block = jax.ShapeDtypeStruct, weights[0].shape[0]
+    return pl.pallas_call(
+        gather_up_body,
+        out_shape=(S((block, D), bf16), S((block, 2 * D), bf16), S((8, HALF), f32)),
+        in_specs=[VM] * (len(weights) + len(vectors)),
+        out_specs=(VM, VM, VM),
+        name="gather_up",
+        compiler_params=pltpu.CompilerParams(vmem_limit_bytes=62 << 20),
+    )(*weights, *(v[None] for v in vectors))
+
+
+def hand_out_body(small, wide, *refs):
+    arrays, (gvec_ref, gwide_ref) = refs[:8], refs[8:10]
+    outs = refs[10:]
+    for src, dst in zip(arrays, outs[:8]):
+        dst[...] = src[...].astype(f32)
+    q, v, o, inner, outer, gain1, shift1, gain2, shift2 = outs[8:]
+    q[...] = gwide_ref[1:2, :small]
+    v[...] = gwide_ref[2:3, :small]
+    inner[...] = gwide_ref[0:1, :wide]
+    for i, ref in enumerate((o, outer, gain1, shift1, gain2, shift2)):
+        ref[...] = gvec_ref[i + 1 : i + 2, :small]
+
+
+def hand_out(small, wide, arrays, gvec, gwide):
+    S = jax.ShapeDtypeStruct
+    one, four = S((1, small), f32), S((1, wide), f32)
+    outs = pl.pallas_call(
+        functools.partial(hand_out_body, small, wide),
+        out_shape=tuple(S(a.shape, f32) for a in arrays) + (one, one, one, four) + (one,) * 5,
+        in_specs=[VM] * 10,
+        out_specs=(VM,) * 17,
+        name="hand_out",
+        compiler_params=pltpu.CompilerParams(vmem_limit_bytes=62 << 20),
+    )(*arrays, gvec, gwide)
+    return outs[:8] + tuple(v.reshape(-1) for v in outs[8:])
 
 
 def per_device(
@@ -1074,44 +1223,28 @@
     own_rows = inputs.shape[0]
     tok_rows = 4 * own_rows
 
-    pack = jnp.concatenate(
-        [query_weight, key_weight, value_weight, output_weight.T, inner_weight, outer_weight.T], axis=1
+    attn_part, ff_part, vin = gather_up(
+        (query_weight, key_weight, value_weight, output_weight, inner_weight, outer_weight),
+        (
+            query_bias, value_bias, output_bias, first_gain, first_shift, outer_bias, second_gain, second_shift,
+            inner_bias,
+        ),
     )
-    pack = lax.all_gather(pack, "row", axis=0, tiled=True)
-    w_qkv, wo, win, wout = pack[:, :576], pack[:, 576:768], pack[:, 768:1536], pack[:, 1536:]
-    vin = jnp.concatenate(
-        [query_bias, value_bias, output_bias, first_gain, first_shift, outer_bias, second_gain, second_shift, inner_bias]
-    ).astype(f32)
-    vin = jnp.broadcast_to(jnp.pad(vin, (0, HALF - vin.shape[0]))[None], (8, HALF))
-
-    seq_ends = jnp.cumsum(seq_lengths[0])
-    seq_starts = seq_ends - seq_lengths[0]
-    positions = jnp.arange(tok_rows, dtype=jnp.int32)
-    seg = jnp.sum((positions[:, None] >= seq_ends[None, :]).astype(jnp.int32), axis=1)
-    hot = (seg[:, None] == jnp.arange(seq_ends.shape[0])[None, :]).astype(jnp.int32)
-    start = jnp.sum(hot * seq_starts[None], axis=1)
-    end = jnp.sum(hot * seq_ends[None], axis=1)
-    lo = start[::QB] // KB
-    hi = (end[QB - 1 :: QB] + KB - 1) // KB
-    start, end = start[None], end[None]
-
-    tok, own_tok, cot_own, cot_send, rank, vec, bqv, b_in = arrive(
-        rows, inputs, cotangent, token_place[None], token_order[None], vin
+    pack, tok, own_tok, cot_own, cot_send, rank, vec, bqv, b_in = arrive(
+        rows, inputs, cotangent, token_place[None], token_order[None], vin, attn_part
     )
+    pack = pack.reshape(D, D)
     cot_got = lax.ppermute(cot_send, "col", [(i, (i + 2) % 4) for i in range(4)])
-    q, k, v, mixed, lse = attend_fwd(lo, hi, start, end, tok.reshape(tok_rows, D), w_qkv, bqv)
+    q, k, v, mixed, lse = attend_fwd(seq_lengths, tok.reshape(tok_rows, D), pack, bqv)
     back, g1, gmix, dwo, g_in, g_out, dvec, dbin = middle(
-        rows, mixed.reshape(4, own_rows, FEAT), own_tok, cot_own, cot_got, wo, win, wout, vec, b_in, rank
+        rows, mixed.reshape(4, own_rows, FEAT), own_tok, cot_own, cot_got, pack, ff_part, vec, b_in, rank
     )
-    dqkv = attend_bwd(lo, hi, start, end, q, k, v, gmix.reshape(tok_rows, FEAT), lse)
+    dqkv = attend_bwd(seq_lengths, q, k, v, mixed, gmix.reshape(tok_rows, FEAT), lse)
     output, input_grad, gq, gk, gv, go, gvec, gwide = depart(
-        rows, back, g1, dqkv, w_qkv, tok, rank, dwo.reshape(rows, -1, FEAT), dvec, dbin
+        rows, back, g1, dqkv, pack, tok, rank, dwo.reshape(rows, -1, FEAT), dvec, dbin
     )
-    small, wide = query_bias.shape[0], inner_bias.shape[0]
-    return (
-        output, input_grad, gq, gk, gv, go, g_in, g_out,
-        gwide[1, :small], gwide[2, :small], gvec[1, :small], gwide[0, :wide],
-        gvec[2, :small], gvec[3, :small], gvec[4, :small], gvec[5, :small], gvec[6, :small],
+    return hand_out(
+        query_bias.shape[0], inner_bias.shape[0], (output, input_grad, gq, gk, gv, go, g_in, g_out), gvec, gwide
     )
 
 

time: 415 us -> 357 us (0.86)
  local copies, waits for them, and re-layouts: 33.7 us -> 4.32 us
  between operations: 14.3 us -> 0.94 us
  waiting for transfers between devices: 9.24 us -> 0.01 us
  Pallas kernels: 350 us -> 343 us
    unnamed x51 -> x4, local copies, waits for them, and re-layouts: 16.9 us -> 4.32 us
    pallas_call x1, Pallas kernels: 28.9 us -> 19.2 us  [attend_bwd(): pl.pallas_call(attend_bwd_body, out_shape=jax.ShapeDtypeStruct((rows, 3 *...]
    all_gather x1 -> x0, waiting for transfers between devices: 9.22 us -> none  [per_device(): pack = lax.all_gather(pack, 'row', axis=0, tiled=True)]
    pallas_call x1, Pallas kernels: 148 us -> 156 us  [middle(): pl.pallas_call(functools.partial(middle_body, rows), out_shape=(S((1, row...]
    concatenate x2 -> x0, local copies, waits for them, and re-layouts: 8.05 us -> none  [the longest x1 6.11 us: per_device(): jnp.concatenate([query_bias, value_bias, output_bias, first_gain, first_s...]
    slice x5 -> x0, local copies, waits for them, and re-layouts: 4.29 us -> none  [the longest x1 1.72 us: per_device(): pack[:, 1536:]]
    pallas_call x1 -> x3, Pallas kernels: 76.7 us -> 72.9 us  [the longest x1 67 us: arrive(): pl.pallas_call(functools.partial(arrive_body, rows), out_shape=(S((rows,...]
  transfers between devices with their start and end apart: 2 -> 1, of which waited for: 1 -> 0; matrix products, arithmetic and copies ran while one was open for 3% -> 0% of each run, Pallas kernels for 25% -> 6%
where the time goes in v4:
time: 357 us; the launch traced here: 350 us
  Pallas kernels  343 us (96%)
  local copies, waits for them, and re-layouts  4.32 us (1%)
    pallas_call x1, Pallas kernels, middle(): pl.pallas_call(functools.partial(middle_body, rows), out_shape=(S((1, row...  156 us
    pallas_call x1, Pallas kernels, depart(): pl.pallas_call(functools.partial(depart_body, rows), out_shape=(S((own_ro...  74.7 us
    pallas_call x1, Pallas kernels, arrive(): pl.pallas_call(functools.partial(arrive_body, rows), out_shape=(S((rows,...  67 us
    pallas_call x1, Pallas kernels, attend_fwd(): pl.pallas_call(attend_fwd_body, out_shape=(part, part, part, part, jax.Sh...  20.2 us
    pallas_call x1, Pallas kernels, attend_bwd(): pl.pallas_call(attend_bwd_body, out_shape=jax.ShapeDtypeStruct((rows, 3 *...  19.2 us
  transfers between devices with their start and end apart: 1, of which 0 were waited for; matrix products, arithmetic and copies ran while one was open for 0% of the time, Pallas kernels for 6%

profile of v4, /device:TPU:0, one launch (start us, length us, event | category | flops | bytes accessed | tf_op | source)
XLA Modules:
  0.0 350.4 jit_solution(12199310282033816491)
XLA Ops:
  0.7 1.7 copy.37.refs_5_
  2.4 2.1 gather_up.1
  4.5 67.0 %arrive.1 = (bf16[8,96,768]{2,1,0:T(8,128)(2,1)}, bf16[4,512,768]{2,1,0:T(8,128)(2,1)}, bf16[512,768]{1,0:T(8,128)(2,1)}, bf16[512,384]{1,0:T(8,128)(2,1)}, bf16...) custom-call(f32[512,768]{1,0:T(8,128)} %x_ref.1, ...), custom_call_target="tpu_custom_call" | custom-call | flops 60000002048 | bytes 20000000 | tf_op jit(solution)/shard_map/arrive/pallas_call | solution.py:596
  71.5 1.8 collective-permute-start
  73.3 20.2 %attend_fwd.1 = (bf16[2048,192]{1,0:T(8,128)(2,1)}, bf16[2048,192]{1,0:T(8,128)(2,1)}, bf16[2048,192]{1,0:T(8,128)(2,1)}, bf16[2048,192]{1,0:T(8,128)(2,1)}, f32[8,2048]{1,0:T(8,128)}) custom-call(s32[1,8]{1,0:T(1,128)} %lens_ref.3, bf16[2048,768]{1,0:T(8,128)(2,1)} %bitcast.45, bf16[768,768]{1,0:T(8,128)(2,1)} %bitcast.46, f32[8,192]{1,0:T(8,128)} %get-tuple-element.71.b_ref), custom_call_target="tpu_custom_call" | custom-call | flops 8000000000 | bytes 8000000 | tf_op jit(solution)/shard_map/attend_fwd/pallas_call | solution.py:111
  93.5 0.0 collective-permute-done.cot_got
  93.5 0.0 copy-start
  93.5 0.7 copy-done
  94.3 156.3 %middle.1 = (bf16[1,8,2,128,384]{4,3,2,1,0:T(8,128)(2,1)}, bf16[4,512,768]{2,1,0:T(8,128)(2,1)}, bf16[4,512,192]{2,1,0:T(8,128)(2,1)}, f32[768,192]{1,0:T(8,128)...) custom-call(bf16[4,512,192]{2,1,0:T(8,128)(2,1)} %bitcast.49, ...), custom_call_target="tpu_custom_call" | custom-call | flops 80000000000 | bytes 20000000 | tf_op jit(solution)/shard_map/middle/pallas_call | solution.py:893
  250.6 19.2 %attend_bwd.1.dqkv_ref = bf16[2048,576]{1,0:T(8,128)(2,1)} custom-call(s32[1,8]{1,0:T(1,128)} %lens_ref.3, bf16[2048,192]{1,0:T(8,128)(2,1)} %get-tuple-element.82.q_in, bf16[2048,192]{1,0:T(8,128)(2,1)} %get-tuple-element.83.k_in, bf16[2048,192]{1,0:T(8,128)(2,1)} %get-tuple-element.84.v_in, bf16[2048,192]{1,0:T(8,128)(2,1)} %get-tuple-element.72.mix_in, ...), custom_call_target="tpu_custom_call" | custom-call | flops 20000000000 | bytes 6000000 | tf_op jit(solution)/shard_map/attend_bwd/pallas_call | solution.py:191
  269.8 74.7 %depart.1 = (bf16[512,768]{1,0:T(8,128)(2,1)}, bf16[512,768]{1,0:T(8,128)(2,1)}, f32[96,192]{1,0:T(8,128)}, f32[96,192]{1,0:T(8,128)}, f32[96,192]{1,0:T(8,128)}...) custom-call(bf16[1,8,2,128,384]{4,3,2,1,0:T(8,128)(2,1)} %get-tuple-element.80.back_ref, ...), custom_call_target="tpu_custom_call" | custom-call | flops 60000002048 | bytes 20000000 | tf_op jit(solution)/shard_map/depart/pallas_call | solution.py:1135
  344.5 3.8 %hand_out.1 = (f32[512,768]{1,0:T(8,128)}, f32[512,768]{1,0:T(8,128)}, f32[96,192]{1,0:T(8,128)}, f32[96,192]{1,0:T(8,128)}, f32[96,192]{1,0:T(8,128)}, /*index=...) custom-call(bf16[512,768]{1,0:T(8,128)(2,1)} %get-tuple-element.90.r, ...), custom_call_target="tpu_custom_call" | custom-call | tf_op jit(solution)/shard_map/hand_out/pallas_call | solution.py:1205
  348.3 1.9 copy.38
Async XLA Ops:
  71.5 22.0 %collective-permute-start = (bf16[512,384]{1,0:T(8,128)(2,1)}, bf16[512,384]{1,0:T(8,128)(2,1)S(1)}, u32[]{:S(2)}, u32[]{:S(2)}) collective-permute-start(bf16[512,384]{1,0:T(8,128)(2,1)} %get-tuple-element.75), channel_id=1, source_target_pairs={{0,2},{1,3},{2,0},{3,1},{4,6},{5,7},{6,4},{7,5},{8,10},{9,11},{10,... | collective-permute-start | bytes 1179656 | tf_op jit(solution)/shard_map/ppermute | solution.py:1237
  93.5 0.7 copy-start

commit v5 on v4

--- a/solution.py
+++ b/solution.py
@@ -56,24 +56,41 @@
             body(pl.multiple_of(jnp.minimum(first, rows - win), 128), win)
 
 
-def attend_fwd_body(lens_ref, tok_ref, pack_ref, b_ref, q_ref, k_ref, v_ref, mix_ref, lse_ref, w_ref, sem):
+def attend_fwd_body(
+    lens_ref, tok_in, pack_ref, b_ref, q_out, k_out, v_out, mix_ref, lse_ref, q_ref, k_ref, v_ref, tok_ref, w_ref, sem,
+):
+    step = 2 * QB
+    steps = tok_ref.shape[0] // step
     fetch = pltpu.make_async_copy(pack_ref, w_ref, sem.at[0])
     fetch.start()
+
+    def tokens(i):
+        at = pl.ds(pl.multiple_of(i * step, step), step)
+        return pltpu.make_async_copy(tok_in.at[at], tok_ref.at[at], sem.at[4 + i])
+
+    pl.loop(0, steps)(lambda i: tokens(i).start())
     scale = HD ** (-0.5)
     total_rows = q_ref.shape[0]
     heads = lane_head(QB)
     lanes = lax.broadcasted_iota(jnp.int32, (QB, 128), 1)
     b_q, b_v = b_ref[0:1, :], b_ref[1:2, :]
-    step = 2 * QB
     fetch.wait()
 
-    @pl.loop(0, total_rows // step)
+    @pl.loop(0, steps)
     def _(i):
+        tokens(i).wait()
         rows = pl.ds(pl.multiple_of(i * step, step), step)
         out = mm(tok_ref[rows, :], w_ref[:, : 3 * FEAT], NN)
         q_ref[rows, :] = (out[:, :FEAT] + b_q).astype(bf16)
         k_ref[rows, :] = out[:, FEAT : 2 * FEAT].astype(bf16)
         v_ref[rows, :] = (out[:, 2 * FEAT :] + b_v).astype(bf16)
+
+    leaving = [
+        pltpu.make_async_copy(src, dst, sem.at[n + 1])
+        for n, (src, dst) in enumerate(((q_ref, q_out), (k_ref, k_out), (v_ref, v_out)))
+    ]
+    for copy in leaving:
+        copy.start()
 
     def by_head(parts):
         return jnp.where(heads == 0, parts[0], jnp.where(heads == 1, parts[1], parts[2]))
@@ -104,6 +121,9 @@
 
         for_window(lens_ref, qb, total_rows, window)
 
+    for copy in leaving:
+        copy.wait()
+
 
 def attend_fwd(lens, tokens, pack, bias):
     rows = tokens.shape[0]
@@ -111,9 +131,14 @@
     return pl.pallas_call(
         attend_fwd_body,
         out_shape=(part, part, part, part, jax.ShapeDtypeStruct((8, rows), f32)),
-        in_specs=[SM, VM, ANY, VM],
-        out_specs=(VM,) * 5,
-        scratch_shapes=[pltpu.VMEM((D, D), bf16), pltpu.SemaphoreType.DMA((1,))],
+        in_specs=[SM, ANY, ANY, VM],
+        out_specs=(ANY, ANY, ANY, VM, VM),
+        scratch_shapes=[pltpu.VMEM((rows, FEAT), bf16)] * 3
+        + [
+            pltpu.VMEM((rows, D), bf16),
+            pltpu.VMEM((D, D), bf16),
+            pltpu.SemaphoreType.DMA((4 + rows // (2 * QB),)),
+        ],
         name="attend_fwd",
         compiler_params=pltpu.CompilerParams(vmem_limit_bytes=62 << 20),
         cost_estimate=pl.CostEstimate(flops=8_000_000_000, bytes_accessed=8_000_000, transcendentals=4_000_000),
@@ -702,19 +727,17 @@
     def xcopy(st, k):
         return remote(xs.at[k], xr.at[k], x_s.at[st, k], x_r.at[st, k], (r, nbr))
 
-    def rs_start(st, k, part):
+    def rs_start(st, k, pair):
         if st > 0:
             d2d(st - 1, k).wait_send()
             xcopy(st - 1, k).wait_send()
-        d2ds[k, 0] = part(sib).astype(bf16)
-        d2ds[k, 1] = part(diag).astype(bf16)
+        d2ds[k] = pair(sib, diag).astype(bf16).reshape(2, CH, D)
         d2d(st, k).start()
-        mine = part(c)
-        other = part(nbr)
+        both = pair(c, nbr)
         d2d(st, k).wait_recv()
-        xs[k] = (other + d2dr[k, 1].astype(f32)).astype(bf16)
+        xs[k] = (both[CH:] + d2dr[k, 1].astype(f32)).astype(bf16)
         xcopy(st, k).start()
-        own[k] = mine + d2dr[k, 0].astype(f32)
+        own[k] = both[:CH] + d2dr[k, 0].astype(f32)
 
     def rs_end(st, k):
         xcopy(st, k).wait_recv()
@@ -746,6 +769,13 @@
     def rows_of(k):
         return pl.ds(pl.multiple_of(k * CH, CH), CH)
 
+    def two_rows(ref, p, q, k):
+        return jnp.concatenate([ref[p, rows_of(k), :], ref[q, rows_of(k), :]], axis=0)
+
+    def put_two(ref, p, q, k, value):
+        ref[p, rows_of(k), :] = value[:CH]
+        ref[q, rows_of(k), :] = value[CH:]
+
     def all_rows(ref, k):
         return ref[:, rows_of(k), :].reshape(4 * CH, ref.shape[2])
 
@@ -754,7 +784,7 @@
             ff_ring.hop(t)
 
     def mix_heads(k):
-        rs_start(0, k, lambda q: mm(mixed_ref[q, rows_of(k), :], wo_ref[...], NT))
+        rs_start(0, k, lambda p, q: mm(two_rows(mixed_ref, p, q, k), wo_ref[...], NT))
 
     def first_norm(k):
         resid = rs_end(0, k) + tok_ref[rows_of(k), :].astype(f32) + bo
@@ -780,12 +810,17 @@
     @pl.loop(0, chunks)
     def _(k):
         ag_end(0, k)
-        pre = mm(all_rows(nfull, k), win(), NN) + bin_ref[...]
-        cum = 0.5 * (1.0 + lax.erf(pre * root_half))
-        dens = jnp.exp(-0.5 * pre * pre) * inv_root_two_pi
-        hidden[:, rows_of(k), :] = (pre * cum).astype(bf16).reshape(4, CH, D)
-        slope[:, rows_of(k), :] = (cum + pre * dens).reshape(4, CH, D)
-        rs_start(1, k, lambda q: mm(hidden[q, rows_of(k), :], wout(), NT))
+
+        def pair(p, q):
+            pre = mm(two_rows(nfull, p, q, k), win(), NN) + bin_ref[...]
+            cum = 0.5 * (1.0 + lax.erf(pre * root_half))
+            dens = jnp.exp(-0.5 * pre * pre) * inv_root_two_pi
+            low = (pre * cum).astype(bf16)
+            put_two(hidden, p, q, k, low)
+            put_two(slope, p, q, k, cum + pre * dens)
+            return mm(low, wout(), NT)
+
+        rs_start(1, k, pair)
 
     dvec_ref[...] = jnp.zeros_like(dvec_ref)
 
@@ -821,15 +856,17 @@
 
     def back_hidden(k):
         ag_end(1, k)
-        g2c = all_rows(g2full, k)
-        grad_pre = mm(g2c, wout(), NN) * all_rows(slope, k)
-        dbin_ref[...] += jnp.sum(grad_pre, axis=0, keepdims=True)
-        low = grad_pre.astype(bf16)
-        hid = all_rows(hidden, k)
-        hidden[:, rows_of(k), :] = low.reshape(4, CH, D)
-        rs_start(2, k, lambda q: mm(hidden[q, rows_of(k), :], win(), NT))
-        add_blocks(dwout, mm(g2c, hid, TN))
-        add_blocks(dwin, mm(all_rows(nfull, k), low, TN))
+
+        def pair(p, q):
+            grad_pre = mm(two_rows(g2full, p, q, k), wout(), NN) * two_rows(slope, p, q, k)
+            dbin_ref[...] += jnp.sum(grad_pre, axis=0, keepdims=True)
+            low = grad_pre.astype(bf16)
+            put_two(slope, p, q, k, low.astype(f32))
+            return mm(low, win(), NT)
+
+        rs_start(2, k, pair)
+        add_blocks(dwout, mm(all_rows(g2full, k), all_rows(hidden, k), TN))
+        add_blocks(dwin, mm(all_rows(nfull, k), all_rows(slope, k).astype(bf16), TN))
 
     pl.loop(0, chunks // 2)(back_hidden)
     outs.joined()
@@ -939,24 +976,25 @@
 
 
 def depart_body(
-    rows, back_ref, g1_ref, dqkv_ref, pack_ref, tok_ref, rank_ref, dwo_ref, dvec_ref, dbin_ref,
+    rows, back_in, g1_in, dqkv_in, pack_in, tok_in, rank_ref, dwo_ref, dvec_ref, dbin_ref,
     out_ref, grad_ref, gq_ref, gk_ref, gv_ref, go_ref, gvec_ref, gwide_ref,
     *scratch,
 ):
     bufs, sems = scratch[:4], scratch[4:14]
     key, col_g, sums, dw = scratch[14:18]
-    d2ds, d2dr, keep, xs, xr, gsend, grecv, r2s, r2r, vmine, vall, vrow, w_ref, w_sem = scratch[18:32]
-    ds_s, ds_r, x_s, x_r, fin_s, fin_r, q2_s, q2_r, sh_s, sh_r, vc_s, vc_r, vr_s, vr_r = scratch[32:]
+    d2ds, d2dr, keep, xs, xr, gsend, grecv, r2s, r2r, vmine, vall, vrow, back_ref, g1_ref, dqkv_ref, w_ref, tok_ref, f_sem = scratch[18:36]
+    ds_s, ds_r, x_s, x_r, fin_s, fin_r, q2_s, q2_r, sh_s, sh_r, vc_s, vc_r, vr_s, vr_r = scratch[36:]
     r, c, sib, nbr, diag = col_peers()
     h = c // 2
     own_rows = out_ref.shape[0]
     tokens = 4 * own_rows
     chunks = own_rows // CH
     block = D // rows
-    fetch = pltpu.make_async_copy(pack_ref, w_ref, w_sem.at[0])
-    fetch.start()
+    pairs = ((dqkv_in, dqkv_ref), (pack_in, w_ref), (tok_in, tok_ref), (g1_in, g1_ref), (back_in, back_ref))
+    fetches = [pltpu.make_async_copy(src, dst, f_sem.at[n]) for n, (src, dst) in enumerate(pairs)]
+    for fetch in fetches:
+        fetch.start()
     greet((sib, nbr, diag), rows, r, c)
-    fetch.wait()
 
     def rows_of(k):
         return pl.ds(pl.multiple_of(k * CH, CH), CH)
@@ -986,23 +1024,61 @@
     def part(q, k):
         return mm(dqkv_ref[token_rows(q, k), :], w_ref[:, : 3 * FEAT], NT)
 
-    @pl.loop(0, chunks)
-    def _(k):
+    fetches[0].wait()
+    fetches[1].wait()
+
+    def send_parts(k):
         d2ds[k, 0] = part(sib, k).astype(bf16)
         d2ds[k, 1] = part(diag, k).astype(bf16)
         d2d(k).start()
         for i, q in ours:
             keep[k, i] = part(q, k)
+
+    def combine(k):
         d2d(k).wait_recv()
         for i in range(2):
             keep[k, i] = keep[k, i] + d2dr[k, i].astype(f32)
             xs[k, 1 - i] = keep[k, i, :, half_lanes(1 - h)].astype(bf16)
         xcopy(k).start()
 
+    pl.loop(0, chunks // 2)(send_parts)
+    pl.loop(0, chunks // 2)(combine)
+    fetches[2].wait()
     whole = mm(tok_ref[...].reshape(tokens, D), dqkv_ref[...], TN)
     for b in range(rows):
         dw[b] = whole[b * block : (b + 1) * block]
     ring.start()
+
+    pl.loop(chunks // 2, chunks)(send_parts)
+    pl.loop(chunks // 2, chunks)(combine)
+    fetches[3].wait()
+    if ring.hops > 1:
+        ring.hop(1)
+
+    def shared(k, i, q):
+        v = grads.xin.at[0, q, rows_of(k)]
+        return remote(v, v, sh_s.at[i, k], sh_r.at[i, k], (r, sib))
+
+    def grad_rows(k):
+        xcopy(k).wait_recv()
+        for i, q in ours:
+            total = keep[k, i, :, half_lanes(h)] + xr[k, i].astype(f32) + g1_ref[q, rows_of(k), half_lanes(h)].astype(f32)
+            grads.xin[0, q, rows_of(k), :] = total.astype(bf16)
+            shared(k, i, q).start()
+
+    pl.loop(0, chunks // 2)(grad_rows)
+    if ring.hops > 2:
+        ring.hop(2)
+    pl.loop(chunks // 2, chunks)(grad_rows)
+
+    @pl.loop(0, chunks)
+    def _(k):
+        for i, q in ours:
+            shared(k, i, q).wait_recv()
+
+    grads.pick_and_send(rank_ref[1:2, :])
+    if ring.hops > 3:
+        ring.hop(3)
 
     sums[...] = jnp.zeros_like(sums)
 
@@ -1049,37 +1125,9 @@
             final(i, k).wait_recv()
             ref[rows_of(k), half_lanes(1 - h)] = grecv[i, k]
 
+    fetches[4].wait()
     send_final(0, back_ref)
-    if ring.hops > 1:
-        ring.hop(1)
     own_final(back_ref, out_ref)
-
-    def shared(k, i, q):
-        v = grads.xin.at[0, q, rows_of(k)]
-        return remote(v, v, sh_s.at[i, k], sh_r.at[i, k], (r, sib))
-
-    def grad_rows(k):
-        xcopy(k).wait_recv()
-        for i, q in ours:
-            total = keep[k, i, :, half_lanes(h)] + xr[k, i].astype(f32) + g1_ref[q, rows_of(k), half_lanes(h)].astype(f32)
-            grads.xin[0, q, rows_of(k), :] = total.astype(bf16)
-            shared(k, i, q).start()
-
-    pl.loop(0, chunks)(grad_rows)
-
-    @pl.loop(0, chunks)
-    def _(k):
-        for i, q in ours:
-            shared(k, i, q).wait_recv()
-
-    grads.pick_and_send(rank_ref[1:2, :])
-    for t in range(2, ring.hops):
-        ring.hop(t)
-    total = ring.result()
-    for i, ref in enumerate((gq_ref, gk_ref, gv_ref)):
-        ref[...] = total[:, i * FEAT : (i + 1) * FEAT]
-    go_ref[...] = total[:, 3 * FEAT :].T
-
     @pl.loop(1, rows)
     def _(i):
         vec_row(i).wait_recv()
@@ -1103,6 +1151,13 @@
 
     grads.shared()
     send_final(1, grads.rbuf)
+    for t in range(4, ring.hops):
+        ring.hop(t)
+    total = ring.result()
+    for i, ref in enumerate((gq_ref, gk_ref, gv_ref)):
+        ref[...] = total[:, i * FEAT : (i + 1) * FEAT]
+    go_ref[...] = total[:, 3 * FEAT :].T
+
     own_final(grads.rbuf, grad_ref)
     take_final(1, grad_ref)
 
@@ -1138,7 +1193,7 @@
             S((own_rows, D), bf16), S((own_rows, D), bf16), third, third, third, S((FEAT, block), f32),
             S((8, 128), f32), S((8, 128), f32),
         ),
-        in_specs=[VM] * 3 + [ANY] + [VM] * 5,
+        in_specs=[ANY] * 5 + [VM] * 4,
         out_specs=(VM,) * 8,
         scratch_shapes=deal_scratch(rows, own_rows, 1)
         + deal_sems(rows, 1)
@@ -1148,7 +1203,8 @@
             V((chunks, 2, CH, HALF), bf16), V((chunks, 2, CH, HALF), bf16),
             V((2, chunks, CH, HALF), bf16), V((2, chunks, CH, HALF), bf16),
             V((2, hops, block, D), bf16), V((2, hops, block, D), bf16),
-            V((16, D), f32), V((4, 16, D), f32), V((rows, 16, D), f32), V((D, D), bf16), DS((1,)),
+            V((16, D), f32), V((4, 16, D), f32), V((rows, 16, D), f32),
+            V(back.shape, bf16), V(g1.shape, bf16), V(dqkv.shape, bf16), V((D, D), bf16), V(tok.shape, bf16), DS((5,)),
         ]
         + [DS((chunks,))] * 4
         + [DS((2, chunks))] * 2

time: 357 us -> 350 us (0.980)
  Pallas kernels: 343 us -> 338 us
    pallas_call x1, Pallas kernels: 156 us -> 153 us  [middle(): pl.pallas_call(functools.partial(middle_body, rows), out_shape=(S((1, row...]
  transfers between devices with their start and end apart: 1 -> 1, of which waited for: 0 -> 0; matrix products, arithmetic and copies ran while one was open for 0% -> 0% of each run, Pallas kernels for 6% -> 5%
where the time goes in v5:
time: 350 us; the launch traced here: 345 us
  Pallas kernels  338 us (97%)
  local copies, waits for them, and re-layouts  4.32 us (1%)
    pallas_call x1, Pallas kernels, middle(): pl.pallas_call(functools.partial(middle_body, rows), out_shape=(S((1, row...  153 us
    pallas_call x1, Pallas kernels, depart(): pl.pallas_call(functools.partial(depart_body, rows), out_shape=(S((own_ro...  75.1 us
    pallas_call x1, Pallas kernels, arrive(): pl.pallas_call(functools.partial(arrive_body, rows), out_shape=(S((rows,...  67 us
    pallas_call x1, Pallas kernels, attend_bwd(): pl.pallas_call(attend_bwd_body, out_shape=jax.ShapeDtypeStruct((rows, 3 *...  19.6 us
    pallas_call x1, Pallas kernels, attend_fwd(): pl.pallas_call(attend_fwd_body, out_shape=(part, part, part, part, jax.Sh...  18.1 us
  transfers between devices with their start and end apart: 1, of which 0 were waited for; matrix products, arithmetic and copies ran while one was open for 0% of the time, Pallas kernels for 5%

profile of v5, /device:TPU:0, one launch (start us, length us, event | category | flops | bytes accessed | tf_op | source)
XLA Modules:
  0.0 345.3 jit_solution(14076957010424217807)
XLA Ops:
  0.7 1.7 copy.37.refs_5_
  2.4 2.1 gather_up.1
  4.5 67.0 %arrive.1 = (bf16[8,96,768]{2,1,0:T(8,128)(2,1)}, bf16[4,512,768]{2,1,0:T(8,128)(2,1)}, bf16[512,768]{1,0:T(8,128)(2,1)}, bf16[512,384]{1,0:T(8,128)(2,1)}, bf16...) custom-call(f32[512,768]{1,0:T(8,128)} %x_ref.1, ...), custom_call_target="tpu_custom_call" | custom-call | flops 60000002048 | bytes 20000000 | tf_op jit(solution)/shard_map/arrive/pallas_call | solution.py:621
  71.5 1.8 collective-permute-start
  73.3 18.1 %attend_fwd.1 = (bf16[2048,192]{1,0:T(8,128)(2,1)}, bf16[2048,192]{1,0:T(8,128)(2,1)}, bf16[2048,192]{1,0:T(8,128)(2,1)}, bf16[2048,192]{1,0:T(8,128)(2,1)}, f32[8,2048]{1,0:T(8,128)}) custom-call(s32[1,8]{1,0:T(1,128)} %lens_ref.3, bf16[2048,768]{1,0:T(8,128)(2,1)} %bitcast.45, bf16[768,768]{1,0:T(8,128)(2,1)} %bitcast.46, f32[8,192]{1,0:T(8,128)} %get-tuple-element.71.b_ref), custom_call_target="tpu_custom_call" | custom-call | flops 8000000000 | bytes 8000000 | tf_op jit(solution)/shard_map/attend_fwd/pallas_call | solution.py:131
  91.4 0.0 collective-permute-done.cot_got
  91.4 0.0 copy-start
  91.4 0.7 copy-done
  92.2 152.6 %middle.1 = (bf16[1,8,2,128,384]{4,3,2,1,0:T(8,128)(2,1)}, bf16[4,512,768]{2,1,0:T(8,128)(2,1)}, bf16[4,512,192]{2,1,0:T(8,128)(2,1)}, f32[768,192]{1,0:T(8,128)...) custom-call(bf16[4,512,192]{2,1,0:T(8,128)(2,1)} %bitcast.49, ...), custom_call_target="tpu_custom_call" | custom-call | flops 80000000000 | bytes 20000000 | tf_op jit(solution)/shard_map/middle/pallas_call | solution.py:930
  244.8 19.6 %attend_bwd.1.dqkv_in = bf16[2048,576]{1,0:T(8,128)(2,1)} custom-call(s32[1,8]{1,0:T(1,128)} %lens_ref.3, bf16[2048,192]{1,0:T(8,128)(2,1)} %get-tuple-element.82.q_in, bf16[2048,192]{1,0:T(8,128)(2,1)} %get-tuple-element.83.k_in, bf16[2048,192]{1,0:T(8,128)(2,1)} %get-tuple-element.84.v_in, bf16[2048,192]{1,0:T(8,128)(2,1)} %get-tuple-element.72.mix_in, ...), custom_call_target="tpu_custom_call" | custom-call | flops 20000000000 | bytes 6000000 | tf_op jit(solution)/shard_map/attend_bwd/pallas_call | solution.py:216
  264.4 75.1 %depart.1 = (bf16[512,768]{1,0:T(8,128)(2,1)}, bf16[512,768]{1,0:T(8,128)(2,1)}, f32[96,192]{1,0:T(8,128)}, f32[96,192]{1,0:T(8,128)}, f32[96,192]{1,0:T(8,128)}...) custom-call(bf16[1,8,2,128,384]{4,3,2,1,0:T(8,128)(2,1)} %get-tuple-element.80.back_in, ...), custom_call_target="tpu_custom_call" | custom-call | flops 60000002048 | bytes 20000000 | tf_op jit(solution)/shard_map/depart/pallas_call | solution.py:1190
  339.4 3.8 %hand_out.1 = (f32[512,768]{1,0:T(8,128)}, f32[512,768]{1,0:T(8,128)}, f32[96,192]{1,0:T(8,128)}, f32[96,192]{1,0:T(8,128)}, f32[96,192]{1,0:T(8,128)}, /*index=...) custom-call(bf16[512,768]{1,0:T(8,128)(2,1)} %get-tuple-element.90.r, ...), custom_call_target="tpu_custom_call" | custom-call | tf_op jit(solution)/shard_map/hand_out/pallas_call | solution.py:1261
  343.3 1.9 copy.38
Async XLA Ops:
  71.5 19.9 %collective-permute-start = (bf16[512,384]{1,0:T(8,128)(2,1)}, bf16[512,384]{1,0:T(8,128)(2,1)S(1)}, u32[]{:S(2)}, u32[]{:S(2)}) collective-permute-start(bf16[512,384]{1,0:T(8,128)(2,1)} %get-tuple-element.75), channel_id=1, source_target_pairs={{0,2},{1,3},{2,0},{3,1},{4,6},{5,7},{6,4},{7,5},{8,10},{9,11},{10,... | collective-permute-start | bytes 1179656 | tf_op jit(solution)/shard_map/ppermute | solution.py:1293
  91.4 0.7 copy-start

commit v6 on v5

--- a/solution.py
+++ b/solution.py
@@ -265,6 +265,8 @@
 
 
 HALF = 384
+PARTS = 3
+WIDE = HALF // PARTS
 
 
 def half_lanes(h):
@@ -360,7 +362,7 @@
 
 def placed(rank_col, got):
     tokens = got.shape[0] * got.shape[1] * got.shape[2]
-    return mm(picker_cols(rank_col, tokens), got.reshape(tokens, HALF), NN)
+    return mm(picker_cols(rank_col, tokens), got.reshape(tokens, got.shape[-1]), NN)
 
 
 class Deal:
@@ -413,7 +415,7 @@
         return remote(v, v, self.sh_s.at[self.a, i], self.sh_r.at[self.a, i], (self.r, self.sib))
 
     def pick_and_send(self, rank):
-        source = self.xin[self.a].reshape(self.tokens, HALF)
+        source = self.xin[self.a].reshape(self.tokens, self.xin.shape[-1])
 
         def picked(to):
             return mm(picker_rows(rank, to * self.slots + self.core * self.own_slots, self.own_slots), source, NN).astype(bf16)
@@ -454,13 +456,13 @@
             self.share(i).wait_send()
 
 
-def deal_scratch(rows, own_rows, count):
+def deal_scratch(rows, own_rows, count, width=HALF):
     slots = 4 * own_rows // rows
     return [
-        pltpu.VMEM((count, 4, own_rows, HALF), bf16),
-        pltpu.VMEM((count, own_rows, HALF), bf16),
-        pltpu.VMEM((count, rows, slots // 2, HALF), bf16),
-        pltpu.VMEM((count, rows, 2, slots // 2, HALF), bf16),
+        pltpu.VMEM((count, 4, own_rows, width), bf16),
+        pltpu.VMEM((count, own_rows, width), bf16),
+        pltpu.VMEM((count, rows, slots // 2, width), bf16),
+        pltpu.VMEM((count, rows, 2, slots // 2, width), bf16),
     ]
 
 
@@ -982,8 +984,8 @@
 ):
     bufs, sems = scratch[:4], scratch[4:14]
     key, col_g, sums, dw = scratch[14:18]
-    d2ds, d2dr, keep, xs, xr, gsend, grecv, r2s, r2r, vmine, vall, vrow, back_ref, g1_ref, dqkv_ref, w_ref, tok_ref, f_sem = scratch[18:36]
-    ds_s, ds_r, x_s, x_r, fin_s, fin_r, q2_s, q2_r, sh_s, sh_r, vc_s, vc_r, vr_s, vr_r = scratch[36:]
+    d2ds, d2dr, keep, xs, xr, gsend, grecv, r2s, r2r, vmine, vall, vrow, back_ref, g1_ref, dqkv_ref, w_ref, tok_ref, f_sem, psend, precv = scratch[18:38]
+    ds_s, ds_r, x_s, x_r, fin_s, fin_r, q2_s, q2_r, sh_s, sh_r, vc_s, vc_r, vr_s, vr_r, pf_s, pf_r = scratch[38:]
     r, c, sib, nbr, diag = col_peers()
     h = c // 2
     own_rows = out_ref.shape[0]
@@ -1002,7 +1004,7 @@
     def token_rows(q, k):
         return pl.ds(pl.multiple_of(q * own_rows + k * CH, CH), CH)
 
-    grads = Deal(0, rows, bufs, sems)
+    grads = [Deal(f, rows, bufs, sems) for f in range(PARTS)]
     ring = Ring(rows, lambda b: jnp.concatenate([dw[b], dwo_ref[b]], axis=1), r2s, r2r, (q2_s, q2_r))
     ours = ((0, c), (1, nbr))
 
@@ -1021,62 +1023,59 @@
     def xcopy(k):
         return remote(xs.at[k], xr.at[k], x_s.at[k], x_r.at[k], (r, nbr))
 
-    def part(q, k):
-        return mm(dqkv_ref[token_rows(q, k), :], w_ref[:, : 3 * FEAT], NT)
+    def lanes_of(half, f):
+        return pl.ds(pl.multiple_of(half * HALF + f * WIDE, WIDE), WIDE)
+
+    def send_parts(f):
+        w = jnp.concatenate([w_ref[lanes_of(h, f), : 3 * FEAT], w_ref[lanes_of(1 - h, f), : 3 * FEAT]], axis=0)
+
+        def part(q):
+            return mm(dqkv_ref[pl.ds(pl.multiple_of(q * own_rows, own_rows), own_rows), :], w, NT)
+
+        d2ds[f, 0] = part(sib).astype(bf16)
+        d2ds[f, 1] = part(diag).astype(bf16)
+        d2d(f).start()
+        for i, q in ours:
+            keep[f, i] = part(q)
+        d2d(f).wait_recv()
+        for i in range(2):
+            keep[f, i] = keep[f, i] + d2dr[f, i].astype(f32)
+            xs[f, 1 - i] = keep[f, i, :, WIDE:].astype(bf16)
+        xcopy(f).start()
+
+    def shared(f, i, q):
+        v = grads[f].xin.at[f, q]
+        return remote(v, v, sh_s.at[i, f], sh_r.at[i, f], (r, sib))
+
+    def grad_rows(f):
+        xcopy(f).wait_recv()
+        for i, q in ours:
+            total = keep[f, i, :, :WIDE] + xr[f, i].astype(f32) + g1_ref[q, :, lanes_of(h, f)].astype(f32)
+            grads[f].xin[f, q] = total.astype(bf16)
+            shared(f, i, q).start()
+        for i, q in ours:
+            shared(f, i, q).wait_recv()
+        grads[f].pick_and_send(rank_ref[1:2, :])
 
     fetches[0].wait()
     fetches[1].wait()
-
-    def send_parts(k):
-        d2ds[k, 0] = part(sib, k).astype(bf16)
-        d2ds[k, 1] = part(diag, k).astype(bf16)
-        d2d(k).start()
-        for i, q in ours:
-            keep[k, i] = part(q, k)
-
-    def combine(k):
-        d2d(k).wait_recv()
-        for i in range(2):
-            keep[k, i] = keep[k, i] + d2dr[k, i].astype(f32)
-            xs[k, 1 - i] = keep[k, i, :, half_lanes(1 - h)].astype(bf16)
-        xcopy(k).start()
-
-    pl.loop(0, chunks // 2)(send_parts)
-    pl.loop(0, chunks // 2)(combine)
+    send_parts(0)
+    send_parts(1)
     fetches[2].wait()
     whole = mm(tok_ref[...].reshape(tokens, D), dqkv_ref[...], TN)
     for b in range(rows):
         dw[b] = whole[b * block : (b + 1) * block]
     ring.start()
-
-    pl.loop(chunks // 2, chunks)(send_parts)
-    pl.loop(chunks // 2, chunks)(combine)
+    for f in range(2, PARTS):
+        send_parts(f)
     fetches[3].wait()
+    grad_rows(0)
+    grad_rows(1)
     if ring.hops > 1:
         ring.hop(1)
-
-    def shared(k, i, q):
-        v = grads.xin.at[0, q, rows_of(k)]
-        return remote(v, v, sh_s.at[i, k], sh_r.at[i, k], (r, sib))
-
-    def grad_rows(k):
-        xcopy(k).wait_recv()
-        for i, q in ours:
-            total = keep[k, i, :, half_lanes(h)] + xr[k, i].astype(f32) + g1_ref[q, rows_of(k), half_lanes(h)].astype(f32)
-            grads.xin[0, q, rows_of(k), :] = total.astype(bf16)
-            shared(k, i, q).start()
-
-    pl.loop(0, chunks // 2)(grad_rows)
+    grad_rows(2)
     if ring.hops > 2:
         ring.hop(2)
-    pl.loop(chunks // 2, chunks)(grad_rows)
-
-    @pl.loop(0, chunks)
-    def _(k):
-        for i, q in ours:
-            shared(k, i, q).wait_recv()
-
-    grads.pick_and_send(rank_ref[1:2, :])
     if ring.hops > 3:
         ring.hop(3)
 
@@ -1149,8 +1148,24 @@
     gwide_ref[2:3, :] = chosen(total[8:16, :], 2 * FEAT + r * width, width)[1:2, :]
     take_final(0, out_ref)
 
-    grads.shared()
-    send_final(1, grads.rbuf)
+    def grad_final(f):
+        return remote(psend.at[f], precv.at[f], pf_s.at[f], pf_r.at[f], (r, nbr))
+
+    for f in range(PARTS):
+        grads[f].shared()
+
+        @pl.loop(0, chunks)
+        def _(k):
+            psend[f, rows_of(k), :] = placed(col_g[token_rows(nbr, k), :], grads[f].rbuf[f]).astype(bf16)
+
+        grad_final(f).start()
+
+    for f in range(PARTS):
+
+        @pl.loop(0, chunks)
+        def _(k):
+            grad_ref[rows_of(k), lanes_of(h, f)] = placed(col_g[token_rows(c, k), :], grads[f].rbuf[f]).astype(bf16)
+
     for t in range(4, ring.hops):
         ring.hop(t)
     total = ring.result()
@@ -1158,18 +1173,18 @@
         ref[...] = total[:, i * FEAT : (i + 1) * FEAT]
     go_ref[...] = total[:, 3 * FEAT :].T
 
-    own_final(grads.rbuf, grad_ref)
-    take_final(1, grad_ref)
-
-    grads.rows_sent()
+    for f in range(PARTS):
+        grad_final(f).wait()
+        grad_ref[:, lanes_of(1 - h, f)] = precv[f]
+        grads[f].rows_sent()
+        d2d(f).wait_send()
+        xcopy(f).wait_send()
+        for i, q in ours:
+            shared(f, i, q).wait_send()
 
     @pl.loop(0, chunks)
     def _(k):
-        for i, q in ours:
-            shared(k, i, q).wait_send()
-            final(i, k).wait_send()
-        d2d(k).wait_send()
-        xcopy(k).wait_send()
+        final(0, k).wait_send()
 
     ring.finish()
     for i, peer in enumerate((sib, nbr, diag)):
@@ -1195,23 +1210,26 @@
         ),
         in_specs=[ANY] * 5 + [VM] * 4,
         out_specs=(VM,) * 8,
-        scratch_shapes=deal_scratch(rows, own_rows, 1)
-        + deal_sems(rows, 1)
+        scratch_shapes=deal_scratch(rows, own_rows, PARTS, WIDE)
+        + deal_sems(rows, PARTS)
         + [V((1, tokens), f32), V((tokens, 1), f32), V((8, 3 * FEAT), f32), V((rows, block, 3 * FEAT), f32)]
         + [
-            V((chunks, 2, CH, D), bf16), V((chunks, 2, CH, D), bf16), V((chunks, 2, CH, D), f32),
-            V((chunks, 2, CH, HALF), bf16), V((chunks, 2, CH, HALF), bf16),
-            V((2, chunks, CH, HALF), bf16), V((2, chunks, CH, HALF), bf16),
+            V((PARTS, 2, own_rows, 2 * WIDE), bf16), V((PARTS, 2, own_rows, 2 * WIDE), bf16),
+            V((PARTS, 2, own_rows, 2 * WIDE), f32),
+            V((PARTS, 2, own_rows, WIDE), bf16), V((PARTS, 2, own_rows, WIDE), bf16),
+            V((1, chunks, CH, HALF), bf16), V((1, chunks, CH, HALF), bf16),
             V((2, hops, block, D), bf16), V((2, hops, block, D), bf16),
             V((16, D), f32), V((4, 16, D), f32), V((rows, 16, D), f32),
             V(back.shape, bf16), V(g1.shape, bf16), V(dqkv.shape, bf16), V((D, D), bf16), V(tok.shape, bf16), DS((5,)),
+            V((PARTS, own_rows, WIDE), bf16), V((PARTS, own_rows, WIDE), bf16),
         ]
-        + [DS((chunks,))] * 4
-        + [DS((2, chunks))] * 2
+        + [DS((PARTS,))] * 4
+        + [DS((1, chunks))] * 2
         + [DS((2, hops))] * 2
-        + [DS((2, chunks))] * 2
+        + [DS((2, PARTS))] * 2
         + [DS((3,))] * 2
-        + [DS((rows,))] * 2,
+        + [DS((rows,))] * 2
+        + [DS((PARTS,))] * 2,
         name="depart",
         compiler_params=pltpu.CompilerParams(collective_id=3, has_side_effects=True, vmem_limit_bytes=62 << 20),
         cost_estimate=pl.CostEstimate(flops=60_000_000_000, bytes_accessed=20_000_000, transcendentals=0),

time: 350 us -> 347 us (level)
  Pallas kernels: 338 us -> 334 us
    pallas_call x1, Pallas kernels: 75.1 us -> 70.2 us  [depart(): pl.pallas_call(functools.partial(depart_body, rows), out_shape=(S((own_ro...]
  transfers between devices with their start and end apart: 1 -> 1, of which waited for: 0 -> 0; matrix products, arithmetic and copies ran while one was open for 0% -> 0% of each run, Pallas kernels for 5% -> 6%
where the time goes in v6:
time: 347 us; the launch traced here: 341 us
  Pallas kernels  334 us (96%)
  local copies, waits for them, and re-layouts  4.32 us (1%)
    pallas_call x1, Pallas kernels, middle(): pl.pallas_call(functools.partial(middle_body, rows), out_shape=(S((1, row...  150 us
    pallas_call x1, Pallas kernels, depart(): pl.pallas_call(functools.partial(depart_body, rows), out_shape=(S((own_ro...  70.2 us
    pallas_call x1, Pallas kernels, arrive(): pl.pallas_call(functools.partial(arrive_body, rows), out_shape=(S((rows,...  67 us
    pallas_call x1, Pallas kernels, attend_bwd(): pl.pallas_call(attend_bwd_body, out_shape=jax.ShapeDtypeStruct((rows, 3 *...  20.9 us
    pallas_call x1, Pallas kernels, attend_fwd(): pl.pallas_call(attend_fwd_body, out_shape=(part, part, part, part, jax.Sh...  19.4 us
  transfers between devices with their start and end apart: 1, of which 0 were waited for; matrix products, arithmetic and copies ran while one was open for 0% of the time, Pallas kernels for 6%

profile of v6, /device:TPU:0, one launch (start us, length us, event | category | flops | bytes accessed | tf_op | source)
XLA Modules:
  0.0 341.0 jit_solution(13231298469413205326)
XLA Ops:
  0.7 1.7 copy.37.refs_5_
  2.4 2.1 gather_up.1
  4.5 67.0 %arrive.1 = (bf16[8,96,768]{2,1,0:T(8,128)(2,1)}, bf16[4,512,768]{2,1,0:T(8,128)(2,1)}, bf16[512,768]{1,0:T(8,128)(2,1)}, bf16[512,384]{1,0:T(8,128)(2,1)}, bf16...) custom-call(f32[512,768]{1,0:T(8,128)} %x_ref.1, ...), custom_call_target="tpu_custom_call" | custom-call | flops 60000002048 | bytes 20000000 | tf_op jit(solution)/shard_map/arrive/pallas_call | solution.py:623
  71.5 1.8 collective-permute-start
  73.3 19.4 %attend_fwd.1 = (bf16[2048,192]{1,0:T(8,128)(2,1)}, bf16[2048,192]{1,0:T(8,128)(2,1)}, bf16[2048,192]{1,0:T(8,128)(2,1)}, bf16[2048,192]{1,0:T(8,128)(2,1)}, f32[8,2048]{1,0:T(8,128)}) custom-call(s32[1,8]{1,0:T(1,128)} %lens_ref.3, bf16[2048,768]{1,0:T(8,128)(2,1)} %bitcast.45, bf16[768,768]{1,0:T(8,128)(2,1)} %bitcast.46, f32[8,192]{1,0:T(8,128)} %get-tuple-element.71.b_ref), custom_call_target="tpu_custom_call" | custom-call | flops 8000000000 | bytes 8000000 | tf_op jit(solution)/shard_map/attend_fwd/pallas_call | solution.py:131
  92.7 0.0 collective-permute-done.cot_got
  92.7 0.0 copy-start
  92.7 0.7 copy-done
  93.4 150.4 %middle.1 = (bf16[1,8,2,128,384]{4,3,2,1,0:T(8,128)(2,1)}, bf16[4,512,768]{2,1,0:T(8,128)(2,1)}, bf16[4,512,192]{2,1,0:T(8,128)(2,1)}, f32[768,192]{1,0:T(8,128)...) custom-call(bf16[4,512,192]{2,1,0:T(8,128)(2,1)} %bitcast.49, ...), custom_call_target="tpu_custom_call" | custom-call | flops 80000000000 | bytes 20000000 | tf_op jit(solution)/shard_map/middle/pallas_call | solution.py:932
  243.8 20.9 %attend_bwd.1.dqkv_in = bf16[2048,576]{1,0:T(8,128)(2,1)} custom-call(s32[1,8]{1,0:T(1,128)} %lens_ref.3, bf16[2048,192]{1,0:T(8,128)(2,1)} %get-tuple-element.82.q_in, bf16[2048,192]{1,0:T(8,128)(2,1)} %get-tuple-element.83.k_in, bf16[2048,192]{1,0:T(8,128)(2,1)} %get-tuple-element.84.v_in, bf16[2048,192]{1,0:T(8,128)(2,1)} %get-tuple-element.72.mix_in, ...), custom_call_target="tpu_custom_call" | custom-call | flops 20000000000 | bytes 6000000 | tf_op jit(solution)/shard_map/attend_bwd/pallas_call | solution.py:216
  264.7 70.2 %depart.1 = (bf16[512,768]{1,0:T(8,128)(2,1)}, bf16[512,768]{1,0:T(8,128)(2,1)}, f32[96,192]{1,0:T(8,128)}, f32[96,192]{1,0:T(8,128)}, f32[96,192]{1,0:T(8,128)}...) custom-call(bf16[1,8,2,128,384]{4,3,2,1,0:T(8,128)(2,1)} %get-tuple-element.80.back_in, ...), custom_call_target="tpu_custom_call" | custom-call | flops 60000002048 | bytes 20000000 | tf_op jit(solution)/shard_map/depart/pallas_call | solution.py:1205
  334.9 3.8 %hand_out.1 = (f32[512,768]{1,0:T(8,128)}, f32[512,768]{1,0:T(8,128)}, f32[96,192]{1,0:T(8,128)}, f32[96,192]{1,0:T(8,128)}, f32[96,192]{1,0:T(8,128)}, /*index=...) custom-call(bf16[512,768]{1,0:T(8,128)(2,1)} %get-tuple-element.90.r, ...), custom_call_target="tpu_custom_call" | custom-call | tf_op jit(solution)/shard_map/hand_out/pallas_call | solution.py:1279
  338.7 1.9 copy.38
Async XLA Ops:
  71.5 21.2 %collective-permute-start = (bf16[512,384]{1,0:T(8,128)(2,1)}, bf16[512,384]{1,0:T(8,128)(2,1)S(1)}, u32[]{:S(2)}, u32[]{:S(2)}) collective-permute-start(bf16[512,384]{1,0:T(8,128)(2,1)} %get-tuple-element.75), channel_id=1, source_target_pairs={{0,2},{1,3},{2,0},{3,1},{4,6},{5,7},{6,4},{7,5},{8,10},{9,11},{10,... | collective-permute-start | bytes 1179656 | tf_op jit(solution)/shard_map/ppermute | solution.py:1311
  92.7 0.7 copy-start
